TPU v7x, 32 devices: a whole 2x2x4 slice. The times are simulated.
32 devices in a mesh: ctx: 4 (over y, x), tp: 8 (over z, core).
Axes of the slice: x: 2, y: 2, z: 4, core: 2. Of those that a mesh axis runs over, the one named last changes fastest.
Arguments:
- grad_out: bfloat16 [512, 5120], P('ctx', 'tp'), may hold values from -6 to 6
- w_out: bfloat16 [1024, 5120], P('tp'), may hold values from -0.078125 to 0.078125
- query_proj: bfloat16 [512, 1024], P('ctx', 'tp'), may hold values from -6 to 6
- key_proj: bfloat16 [512, 1024], P('ctx', 'tp'), may hold values from -6 to 6
- value_proj: bfloat16 [512, 1024], P('ctx', 'tp'), may hold values from -6 to 6
- w_query: bfloat16 [5120, 1024], P(None, 'tp'), may hold values from -0.25 to 0.25
- w_key: bfloat16 [5120, 1024], P(None, 'tp'), may hold values from -0.1875 to 0.1875
- w_value: bfloat16 [5120, 1024], P(None, 'tp'), may hold values from -0.1875 to 0.1875
- tile_keys: int32 [4, 3], replicated, may hold values from 0 to 3, as said below
Outputs:
- input_grad: float32 [5120, 512], P('tp', 'ctx')
Inputs may be any that keep to these rules, and one draw needn't show every extreme that they name: `tile_keys`: each row lists 3 distinct key tiles, among them the query tile itself; every listed tile u has |u - t| <= 2 for its query tile t.
All inputs are finite; a program needn't handle non-finite values.
Results may differ from a plain program's by a relative error of at most 0.0078.
Values may be sent and summed in bfloat16 or wider, within the bound.
No kernel may reach another device: no remote copies, remote signals or barrier semaphores. Data moves between devices by JAX's collectives and lax.ppermute only.
A program may use at most 64 MiB of HBM per device.

v0:
```python
import functools

import jax
import jax.numpy as jnp
from jax import lax
from jax.experimental import pallas as pl
from jax.experimental.pallas import tpu as pltpu
from jax.sharding import PartitionSpec as P


TILE = 128
CONTRACT_LAST = (((1,), (1,)), ((), ()))
CONTRACT_FIRST = (((0,), (0,)), ((), ()))
VMEM = pl.BlockSpec(memory_space=pltpu.VMEM)
SMEM = pl.BlockSpec(memory_space=pltpu.SMEM)


def dot_f32(a, b, dims):
    return lax.dot_general(a, b, dims, preferred_element_type=jnp.float32)


def many_slabs(
    grad_out, w_out, query_proj, key_proj, value_proj, w_query, w_key, w_value, tile_keys
):
    row_count = query_proj.shape[0]
    head_size = query_proj.shape[1]
    score_scale = head_size ** (-0.5)
    tiles_here = row_count // TILE
    slab_index = lax.axis_index("ctx")
    d_attn = dot_f32(
        lax.all_gather(grad_out, "tp", axis=1, tiled=True), w_out, CONTRACT_LAST
    ).astype(jnp.bfloat16)
    keys_all, values_all = (
        lax.all_gather(key_proj, "ctx", axis=0, tiled=True),
        lax.all_gather(value_proj, "ctx", axis=0, tiled=True),
    )
    total_tiles = keys_all.shape[0] // TILE
    own_lists = lax.dynamic_slice_in_dim(tile_keys, slab_index * tiles_here, tiles_here, 0)
    all_tiles = jnp.arange(total_tiles, dtype=jnp.int32)
    tile_ok = jnp.any(own_lists[:, :, None] == all_tiles[None, None, :], axis=1)
    token_mask = jnp.repeat(jnp.repeat(tile_ok, TILE, axis=0), TILE, axis=1)
    scores = dot_f32(query_proj, keys_all, CONTRACT_LAST) * score_scale
    scores = jnp.where(token_mask, scores, -jnp.inf)
    row_max = jnp.max(scores, axis=1, keepdims=True)
    exponent = jnp.exp(scores - row_max)
    row_total = jnp.sum(exponent, axis=1, keepdims=True)
    prob_exact = exponent / row_total
    prob_half = prob_exact.astype(jnp.bfloat16)
    attn_out = jnp.dot(prob_half, values_all, preferred_element_type=jnp.float32)
    row_delta = jnp.sum(d_attn.astype(jnp.float32) * attn_out, axis=1, keepdims=True)
    d_prob = dot_f32(d_attn, values_all, CONTRACT_LAST)
    d_score = (prob_exact * (d_prob - row_delta) * score_scale).astype(jnp.bfloat16)
    d_query = jnp.dot(d_score, keys_all, preferred_element_type=jnp.float32).astype(jnp.bfloat16)
    key_part = dot_f32(d_score, query_proj, CONTRACT_FIRST)
    value_part = dot_f32(prob_half, d_attn, CONTRACT_FIRST)
    key_sums = lax.psum_scatter(
        jnp.concatenate([key_part, value_part], axis=1), "ctx", scatter_dimension=0, tiled=True
    )
    d_key = key_sums[:, :head_size].astype(jnp.bfloat16)
    d_value = key_sums[:, head_size:].astype(jnp.bfloat16)
    feature_sum = dot_f32(w_query, d_query, CONTRACT_LAST)
    feature_sum = feature_sum + dot_f32(w_key, d_key, CONTRACT_LAST)
    feature_sum = feature_sum + dot_f32(w_value, d_value, CONTRACT_LAST)
    return lax.psum_scatter(feature_sum, "tp", scatter_dimension=0, tiled=True)


def pack_kernel(query_ref, key_ref, value_ref, out_ref):
    size = query_ref.shape[1]
    out_ref[:, :size] = query_ref[...]
    out_ref[:, size : 2 * size] = key_ref[...]
    out_ref[:, 2 * size :] = value_ref[...]


def attn_grad_kernel(chips, cols, *refs):
    blocks = refs[:chips]
    own_w, mate_w, own_ref, mate_ref = refs[chips:]
    index = lax.axis_index("tp")
    own = jnp.zeros(own_ref.shape, jnp.float32)
    mate = jnp.zeros(own_ref.shape, jnp.float32)
    for step in range(chips):
        start = pl.multiple_of((index ^ (2 * step)) * cols, 128)
        block = blocks[step][...]
        own = own + dot_f32(block, own_w[:, pl.ds(start, cols)], CONTRACT_LAST)
        mate = mate + dot_f32(block, mate_w[:, pl.ds(start, cols)], CONTRACT_LAST)
    own_ref[...] = own
    mate_ref[...] = mate


def softmax_kernel(slabs, keep, lists_ref, *refs):
    packs = refs[:slabs]
    row_ref, col_ref, attn_ref = refs[slabs:]
    rows = packs[0].shape[0]
    size = packs[0].shape[1] // 3
    tiles = rows // TILE
    slab = lax.axis_index("ctx")
    scale = size ** (-0.5)
    keys = jnp.concatenate([pack[:, size : 2 * size] for pack in packs], axis=0)
    values = jnp.concatenate([pack[:, 2 * size :] for pack in packs], axis=0)
    for turn in range(slabs):
        for tile in range(tiles):
            query_tile = (slab ^ turn) * tiles + tile
            span = pl.ds(turn * rows + tile * TILE, TILE)
            scores = dot_f32(packs[turn][pl.ds(tile * TILE, TILE), :size], keys, CONTRACT_LAST)
            scores = scores * scale
            parts = []
            for other in range(slabs * tiles):
                key_tile = (slab ^ (other // tiles)) * tiles + other % tiles
                listed = lists_ref[query_tile, 0] == key_tile
                for place in range(1, keep):
                    listed = listed | (lists_ref[query_tile, place] == key_tile)
                part = scores[:, other * TILE : (other + 1) * TILE]
                parts.append(jnp.where(listed, part, -jnp.inf))
            scores = jnp.concatenate(parts, axis=1)
            exponent = jnp.exp(scores - jnp.max(scores, axis=1, keepdims=True))
            prob = exponent / jnp.sum(exponent, axis=1, keepdims=True)
            attn_ref[span, :] = jnp.dot(
                prob.astype(jnp.bfloat16), values, preferred_element_type=jnp.float32
            )
            col_ref[span, :] = prob[:, :rows]
            if turn == 0:
                row_ref[pl.ds(tile * TILE, TILE), :] = prob


def query_grad_kernel(slabs, grad_ref, *refs):
    packs = refs[:slabs]
    row_ref, attn_ref, out_ref = refs[slabs:]
    rows = packs[0].shape[0]
    size = packs[0].shape[1] // 3
    scale = size ** (-0.5)
    grad = grad_ref[...]
    keys = jnp.concatenate([pack[:, size : 2 * size] for pack in packs], axis=0)
    values = jnp.concatenate([pack[:, 2 * size :] for pack in packs], axis=0)
    delta = jnp.sum(grad.astype(jnp.float32) * attn_ref[:rows, :], axis=1, keepdims=True)
    d_prob = dot_f32(grad, values, CONTRACT_LAST)
    d_score = (row_ref[...] * (d_prob - delta) * scale).astype(jnp.bfloat16)
    out_ref[...] = jnp.dot(d_score, keys, preferred_element_type=jnp.float32).astype(jnp.bfloat16)


def key_grad_kernel(slabs, *refs):
    grads = refs[:slabs]
    packs = refs[slabs : 2 * slabs]
    query_ref, col_ref, attn_ref, out_ref = refs[2 * slabs :]
    size = packs[0].shape[1] // 3
    scale = size ** (-0.5)
    queries = jnp.concatenate([pack[:, :size] for pack in packs], axis=0)
    grad = jnp.concatenate([part[...] for part in grads], axis=0)
    prob = col_ref[...]
    delta = jnp.sum(grad.astype(jnp.float32) * attn_ref[...], axis=1, keepdims=True)
    d_prob = dot_f32(grad, packs[0][:, 2 * size :], CONTRACT_LAST)
    d_score = (prob * (d_prob - delta) * scale).astype(jnp.bfloat16)
    out_ref[:, :size] = query_ref[...]
    out_ref[:, size : 2 * size] = dot_f32(d_score, queries, CONTRACT_FIRST).astype(jnp.bfloat16)
    out_ref[:, 2 * size :] = dot_f32(prob.astype(jnp.bfloat16), grad, CONTRACT_FIRST).astype(
        jnp.bfloat16
    )


def project_kernel(rows, step, own_ref, mate_ref, *refs):
    weights, out_ref = refs[:6], refs[6]
    start = pl.multiple_of((lax.axis_index("tp") ^ (2 * step)) * rows, 16)
    size = own_ref.shape[1] // 3
    total = None
    for place, weight in enumerate(weights):
        grads = own_ref if place < 3 else mate_ref
        part = grads[:, (place % 3) * size : (place % 3 + 1) * size]
        term = dot_f32(weight[pl.ds(start, rows), :], part, CONTRACT_LAST)
        total = term if total is None else total + term
    out_ref[...] = total.astype(out_ref.dtype)


def sum_kernel(own_ref, *refs):
    total = own_ref[...]
    for part in refs[:-1]:
        total = total + part[...].astype(jnp.float32)
    refs[-1][...] = total


def call(kernel, args, outs, fast_out=True):
    ints = [x.dtype == jnp.int32 for x in args]
    args = [
        x if flag else pltpu.with_memory_space_constraint(x, pltpu.VMEM)
        for x, flag in zip(args, ints)
    ]
    return pl.pallas_call(
        kernel,
        in_specs=[SMEM if flag else VMEM for flag in ints],
        out_specs=[VMEM] * len(outs),
        out_shape=[
            pltpu.VMEM(shape, kind) if fast_out else jax.ShapeDtypeStruct(shape, kind)
            for shape, kind in outs
        ],
        compiler_params=pltpu.CompilerParams(vmem_limit_bytes=16 << 20),
    )(*args)


def few_slabs(
    slabs,
    chips,
    grad_out,
    w_out,
    query_proj,
    key_proj,
    value_proj,
    w_query,
    w_key,
    w_value,
    tile_keys,
):
    rows, cols = grad_out.shape
    size = query_proj.shape[1]
    half, full = jnp.bfloat16, jnp.float32
    hops = sorted(range(1, chips), key=lambda step: (step & (step - 1) != 0, -step))

    def to_chip(x, step):
        return lax.ppermute(x, "tp", [(t, t ^ (2 * step)) for t in range(2 * chips)])

    def to_mate(x):
        return lax.ppermute(x, "tp", [(t, t ^ 1) for t in range(2 * chips)])

    def to_slab(x, turn):
        return lax.ppermute(x, "ctx", [(c, c ^ turn) for c in range(slabs)])

    blocks = [grad_out] + [to_chip(grad_out, step) for step in range(1, chips)]
    (pack,) = call(pack_kernel, [query_proj, key_proj, value_proj], [((rows, 3 * size), half)])
    packs = [pack] + [to_slab(pack, turn) for turn in range(1, slabs)]
    mate_out = to_mate(w_out)
    own_w = [w_query, w_key, w_value]
    mate_w = [to_mate(w) for w in own_w]

    prob_row, prob_col, attn_out = call(
        functools.partial(softmax_kernel, slabs, tile_keys.shape[1]),
        [tile_keys, *packs],
        [((rows, slabs * rows), full), ((slabs * rows, rows), full), ((slabs * rows, size), full)],
    )
    own_part, mate_part = call(
        functools.partial(attn_grad_kernel, chips, cols),
        [*blocks, w_out, mate_out],
        [((rows, size), full), ((rows, size), full)],
    )
    grad = (own_part + to_mate(mate_part)).astype(half)
    grads = [grad] + [to_slab(grad, turn) for turn in range(1, slabs)]
    (d_query,) = call(
        functools.partial(query_grad_kernel, slabs),
        [grad, *packs, prob_row, attn_out],
        [((rows, size), half)],
    )
    (own_grads,) = call(
        functools.partial(key_grad_kernel, slabs),
        [*grads, *packs, d_query, prob_col, attn_out],
        [((rows, 3 * size), half)],
    )
    mate_grads = to_mate(own_grads)
    arrived = []
    for step in hops + [0]:
        (part,) = call(
            functools.partial(project_kernel, cols, step),
            [own_grads, mate_grads, *own_w, *mate_w],
            [((cols, rows), half if step else full)],
        )
        if step:
            arrived.append(to_chip(part, step))
    (out,) = call(sum_kernel, [part, *arrived], [((cols, rows), full)], fast_out=False)
    return out


def solution(mesh):
    slabs, shards = mesh.shape["ctx"], mesh.shape["tp"]
    chips = shards // 2
    few = 1 < slabs <= 8 and slabs & (slabs - 1) == 0
    few = few and shards == 2 * chips and 2 <= chips <= 8 and chips & (chips - 1) == 0
    return jax.shard_map(
        functools.partial(few_slabs, slabs, chips) if few else many_slabs,
        mesh=mesh,
        in_specs=(
            P("ctx", "tp"),
            P("tp", None),
            P("ctx", "tp"),
            P("ctx", "tp"),
            P("ctx", "tp"),
            P(None, "tp"),
            P(None, "tp"),
            P(None, "tp"),
            P(),
        ),
        out_specs=P("tp", "ctx"),
        check_vma=False,
    )
```

profile of v0, /device:TPU:0, one launch (start us, length us, event | category | flops | bytes accessed | tf_op | source)
XLA Modules:
  0.0 66.1 jit_solution(4353024560934754136)
XLA Ops:
  0.0 0.5 collective-permute-start.3
  0.5 0.0 collective-permute-start.12
  0.5 0.5 collective-permute-start.13
  1.0 0.0 collective-permute-start.14
  1.0 4.1 %collective-permute-start.1 = (bf16[128,640]{1,0:T(8,128)(2,1)}, bf16[128,640]{1,0:T(8,128)(2,1)S(1)}, u32[]{:S(2)}, u32[]{:S(2)}) collective-permute-start(bf16[128,640]{1,0:T(8,128)(2,1)} %refs_0_.5), channel_id=1, source_target_pairs={{0,4},{1,5},{2,6},{3,7},{4,0},{5,1},{6,2},{7,3},{8,12},{9,13},{10,... | collective-permute-start | bytes 491528 | tf_op jit(solution)/shard_map/ppermute | solution.py:215
  5.1 8.1 %collective-permute-done.1.refs_2_ = bf16[128,640]{1,0:T(8,128)(2,1)S(1)} collective-permute-done((bf16[128,640]{1,0:T(8,128)(2,1)}, bf16[128,640]{1,0:T(8,128)(2,1)S(1)}, u32[]{:S(2)}, u32[]{:S(2)}) %collective-permute-start.1) | collective-permute-done | bytes 163872 | tf_op jit(solution)/shard_map/ppermute | solution.py:215
  13.2 0.8 %collective-permute-start = (bf16[128,640]{1,0:T(8,128)(2,1)}, bf16[128,640]{1,0:T(8,128)(2,1)S(1)}, u32[]{:S(2)}, u32[]{:S(2)}) collective-permute-start(bf16[128,640]{1,0:T(8,128)(2,1)} %refs_0_.5), channel_id=1, source_target_pairs={{0,2},{1,3},{2,0},{3,1},{4,6},{5,7},{6,4},{7,5},{8,10},{9,11},{10,... | collective-permute-start | bytes 491528 | tf_op jit(solution)/shard_map/ppermute | solution.py:215
  14.0 4.9 %collective-permute-done.refs_1_ = bf16[128,640]{1,0:T(8,128)(2,1)S(1)} collective-permute-done((bf16[128,640]{1,0:T(8,128)(2,1)}, bf16[128,640]{1,0:T(8,128)(2,1)S(1)}, u32[]{:S(2)}, u32[]{:S(2)}) %collective-permute-start) | collective-permute-done | bytes 163872 | tf_op jit(solution)/shard_map/ppermute | solution.py:215
  18.9 4.1 %collective-permute-start.2 = (bf16[128,640]{1,0:T(8,128)(2,1)}, bf16[128,640]{1,0:T(8,128)(2,1)S(1)}, u32[]{:S(2)}, u32[]{:S(2)}) collective-permute-start(bf16[128,640]{1,0:T(8,128)(2,1)} %refs_0_.5), channel_id=1, source_target_pairs={{0,6},{1,7},{2,4},{3,5},{4,2},{5,3},{6,0},{7,1},{8,14},{9,15},{10,... | collective-permute-start | bytes 491528 | tf_op jit(solution)/shard_map/ppermute | solution.py:215
  23.1 0.0 copy-start.5
  23.1 0.8 %copy-done.5 = bf16[128,128]{1,0:T(8,128)(2,1)S(1)} copy-done((bf16[128,128]{1,0:T(8,128)(2,1)S(1)}, bf16[128,128]{1,0:T(8,128)(2,1)}, u32[]{:S(2)}) %copy-start.5) | copy-done | bytes 32792
  23.8 0.0 copy-start.6
  23.8 0.8 %copy-done.6 = bf16[128,128]{1,0:T(8,128)(2,1)S(1)} copy-done((bf16[128,128]{1,0:T(8,128)(2,1)S(1)}, bf16[128,128]{1,0:T(8,128)(2,1)}, u32[]{:S(2)}) %copy-start.6) | copy-done | bytes 32792
  24.6 0.0 copy-start.7
  24.6 0.8 %copy-done.7 = bf16[128,128]{1,0:T(8,128)(2,1)S(1)} copy-done((bf16[128,128]{1,0:T(8,128)(2,1)S(1)}, bf16[128,128]{1,0:T(8,128)(2,1)}, u32[]{:S(2)}) %copy-start.7) | copy-done | bytes 32792
  25.3 0.0 copy-start.8
  25.4 1.5 %collective-permute-done.2.refs_3_ = bf16[128,640]{1,0:T(8,128)(2,1)S(1)} collective-permute-done((bf16[128,640]{1,0:T(8,128)(2,1)}, bf16[128,640]{1,0:T(8,128)(2,1)S(1)}, u32[]{:S(2)}, u32[]{:S(2)}) %collective-permute-start.2) | collective-permute-done | bytes 163872 | tf_op jit(solution)/shard_map/ppermute | solution.py:215
  26.9 2.4 %collective-permute-start.10 = (bf16[128,384]{1,0:T(8,128)(2,1)S(1)}, bf16[128,384]{1,0:T(8,128)(2,1)S(1)}, u32[]{:S(2)}, u32[]{:S(2)}) collective-permute-start(bf16[128,384]{1,0:T(8,128)(2,1)S(1)} %shard_map.92.refs_0_.refs_4_), channel_id=1, source_target_pairs={{0,24},{8,16},{16,8},{24,0},{1,25},{9,17},{17,9},{25,1},{2,26},{10... | collective-permute-start | bytes 294920 | tf_op jit(solution)/shard_map/ppermute | solution.py:221
  29.3 0.0 collective-permute-done.3.refs_5_
  29.3 0.0 copy-start.3
  29.3 1.3 %copy-done.3 = bf16[128,5120]{1,0:T(8,128)(2,1)S(1)} copy-done((bf16[128,5120]{1,0:T(8,128)(2,1)S(1)}, bf16[128,5120]{1,0:T(8,128)(2,1)}, u32[]{:S(2)}) %copy-start.3) | copy-done | bytes 1310744
  30.7 0.0 copy-start.4
  30.7 0.9 %copy-done.4 = bf16[128,640]{1,0:T(8,128)(2,1)S(1)} copy-done((bf16[128,640]{1,0:T(8,128)(2,1)S(1)}, bf16[128,640]{1,0:T(8,128)(2,1)}, u32[]{:S(2)}) %copy-start.4) | copy-done | bytes 163864
  31.6 0.0 copy-start.2
  31.6 0.6 shard_map.91
  32.2 0.1 collective-permute-start.4
  32.3 0.2 collective-permute-done.10.refs_3_.refs_7_
  32.4 1.5 %collective-permute-start.9 = (bf16[128,384]{1,0:T(8,128)(2,1)S(1)}, bf16[128,384]{1,0:T(8,128)(2,1)S(1)}, u32[]{:S(2)}, u32[]{:S(2)}) collective-permute-start(bf16[128,384]{1,0:T(8,128)(2,1)S(1)} %shard_map.92.refs_0_.refs_4_), channel_id=1, source_target_pairs={{0,16},{8,24},{16,0},{24,8},{1,17},{9,25},{17,1},{25,9},{2,18},{10... | collective-permute-start | bytes 294920 | tf_op jit(solution)/shard_map/ppermute | solution.py:221
  33.9 0.0 collective-permute-done.4
  33.9 1.5 %collective-permute-start.8 = (bf16[128,384]{1,0:T(8,128)(2,1)S(1)}, bf16[128,384]{1,0:T(8,128)(2,1)S(1)}, u32[]{:S(2)}, u32[]{:S(2)}) collective-permute-start(bf16[128,384]{1,0:T(8,128)(2,1)S(1)} %shard_map.92.refs_0_.refs_4_), channel_id=1, source_target_pairs={{0,8},{8,0},{16,24},{24,16},{1,9},{9,1},{17,25},{25,17},{2,10},{10... | collective-permute-start | bytes 294920 | tf_op jit(solution)/shard_map/ppermute | solution.py:221
  35.4 0.0 copy-start.1
  35.4 0.0 copy-start
  35.4 2.0 %collective-permute-done.9.refs_2_.refs_6_ = bf16[128,384]{1,0:T(8,128)(2,1)S(1)} collective-permute-done((bf16[128,384]{1,0:T(8,128)(2,1)S(1)}, bf16[128,384]{1,0:T(8,128)(2,1)S(1)}, u32[]{:S(2)}, u32[]{:S(2)}) %collective-permute-start.9) | collective-permute-done | bytes 98336 | tf_op jit(solution)/shard_map/ppermute | solution.py:221
  37.5 2.0 %collective-permute-start.7 = (bf16[128,128]{1,0:T(8,128)(2,1)S(1)}, bf16[128,128]{1,0:T(8,128)(2,1)S(1)}, u32[]{:S(2)}, u32[]{:S(2)}) collective-permute-start(bf16[128,128]{1,0:T(8,128)(2,1)S(1)} %add_convert_fusion.grad_ref.refs_0_), channel_id=1, source_target_pairs={{0,24},{8,16},{16,8},{24,0},{1,25},{9,17},{17,9},{25,1},{2,26},{10... | collective-permute-start | bytes 98312 | tf_op jit(solution)/shard_map/ppermute | solution.py:221
  39.5 0.0 collective-permute-done.8.refs_1_.refs_5_
  39.5 0.5 collective-permute-start.6
  40.0 2.3 %collective-permute-done.7.refs_3_ = bf16[128,128]{1,0:T(8,128)(2,1)S(1)} collective-permute-done((bf16[128,128]{1,0:T(8,128)(2,1)S(1)}, bf16[128,128]{1,0:T(8,128)(2,1)S(1)}, u32[]{:S(2)}, u32[]{:S(2)}) %collective-permute-start.7) | collective-permute-done | bytes 32800 | tf_op jit(solution)/shard_map/ppermute | solution.py:221
  42.3 1.1 %collective-permute-start.5 = (bf16[128,128]{1,0:T(8,128)(2,1)S(1)}, bf16[128,128]{1,0:T(8,128)(2,1)S(1)}, u32[]{:S(2)}, u32[]{:S(2)}) collective-permute-start(bf16[128,128]{1,0:T(8,128)(2,1)S(1)} %add_convert_fusion.grad_ref.refs_0_), channel_id=1, source_target_pairs={{0,8},{8,0},{16,24},{24,16},{1,9},{9,1},{17,25},{25,17},{2,10},{10... | collective-permute-start | bytes 98312 | tf_op jit(solution)/shard_map/ppermute | solution.py:221
  43.3 0.0 copy-done.8
  43.3 2.1 %shard_map.93 = (f32[128,512]{1,0:T(8,128)S(1)}, f32[512,128]{1,0:T(8,128)S(1)}, f32[512,128]{1,0:T(8,128)S(1)}) custom-call(s32[4,3]{1,0:T(4,128)S(1)} %copy-done.8, bf16[128,384]{1,0:T(8,128)(2,1)S(1)} %shard_map.92.refs_0_.refs_4_, bf16[128,384]{1,0:T(8,128)(2,1)S(1)} %collective-permute-done.8.refs_1_.refs_5_, ...), custom_call_target="tpu_custom_call" | custom-call | tf_op jit(solution)/shard_map/pallas_call | solution.py:184
  45.4 0.3 shard_map.94.refs_8_
  45.8 0.0 collective-permute-done.6.refs_2_
  45.8 0.4 collective-permute-done.5.refs_1_
  46.2 0.5 shard_map.95.own_ref
  46.6 0.1 collective-permute-start.11
  46.7 0.0 collective-permute-done.12.refs_3_
  46.7 0.0 collective-permute-done.13.refs_4_
  46.7 0.0 collective-permute-done.14.refs_5_
  46.8 1.3 %collective-permute-done.11.mate_ref = bf16[128,384]{1,0:T(8,128)(2,1)S(1)} collective-permute-done((bf16[128,384]{1,0:T(8,128)(2,1)S(1)}, bf16[128,384]{1,0:T(8,128)(2,1)S(1)}, u32[]{:S(2)}, u32[]{:S(2)}) %collective-permute-start.11) | collective-permute-done | bytes 98336 | tf_op jit(solution)/shard_map/ppermute | solution.py:218
  48.0 0.0 copy-done.2
  48.0 0.0 copy-done.1
  48.0 0.0 copy-done
  48.0 0.4 shard_map.97
  48.4 4.3 %collective-permute-start.15 = (bf16[640,128]{1,0:T(8,128)(2,1)S(1)}, bf16[640,128]{1,0:T(8,128)(2,1)S(1)}, u32[]{:S(2)}, u32[]{:S(2)}) collective-permute-start(bf16[640,128]{1,0:T(8,128)(2,1)S(1)} %shard_map.97), channel_id=1, source_target_pairs={{0,4},{1,5},{2,6},{3,7},{4,0},{5,1},{6,2},{7,3},{8,12},{9,13},{10,... | collective-permute-start | bytes 491528 | tf_op jit(solution)/shard_map/ppermute | solution.py:215
  52.8 0.4 shard_map.98
  53.2 0.1 collective-permute-start.16
  53.3 0.4 shard_map.99
  53.7 1.5 %collective-permute-start.17 = (bf16[640,128]{1,0:T(8,128)(2,1)S(1)}, bf16[640,128]{1,0:T(8,128)(2,1)S(1)}, u32[]{:S(2)}, u32[]{:S(2)}) collective-permute-start(bf16[640,128]{1,0:T(8,128)(2,1)S(1)} %shard_map.99), channel_id=1, source_target_pairs={{0,6},{1,7},{2,4},{3,5},{4,2},{5,3},{6,0},{7,1},{8,14},{9,15},{10,... | collective-permute-start | bytes 491528 | tf_op jit(solution)/shard_map/ppermute | solution.py:215
  55.2 0.4 shard_map.96.own_ref
  55.6 6.2 %collective-permute-done.15.refs_0_ = bf16[640,128]{1,0:T(8,128)(2,1)S(1)} collective-permute-done((bf16[640,128]{1,0:T(8,128)(2,1)S(1)}, bf16[640,128]{1,0:T(8,128)(2,1)S(1)}, u32[]{:S(2)}, u32[]{:S(2)}) %collective-permute-start.15) | collective-permute-done | bytes 163872 | tf_op jit(solution)/shard_map/ppermute | solution.py:215
  61.8 0.7 %collective-permute-done.16.refs_1_ = bf16[640,128]{1,0:T(8,128)(2,1)S(1)} collective-permute-done((bf16[640,128]{1,0:T(8,128)(2,1)S(1)}, bf16[640,128]{1,0:T(8,128)(2,1)S(1)}, u32[]{:S(2)}, u32[]{:S(2)}) %collective-permute-start.16) | collective-permute-done | bytes 163872 | tf_op jit(solution)/shard_map/ppermute | solution.py:215
  62.6 2.8 %collective-permute-done.17.refs_2_ = bf16[640,128]{1,0:T(8,128)(2,1)S(1)} collective-permute-done((bf16[640,128]{1,0:T(8,128)(2,1)S(1)}, bf16[640,128]{1,0:T(8,128)(2,1)S(1)}, u32[]{:S(2)}, u32[]{:S(2)}) %collective-permute-start.17) | collective-permute-done | bytes 163872 | tf_op jit(solution)/shard_map/ppermute | solution.py:215
  65.3 0.8 %shard_map.100 = f32[640,128]{1,0:T(8,128)} custom-call(f32[640,128]{1,0:T(8,128)S(1)} %shard_map.96.own_ref, bf16[640,128]{1,0:T(8,128)(2,1)S(1)} %collective-permute-done.15.refs_0_, bf16[640,128]{1,0:T(8,128)(2,1)S(1)} %collective-permute-done.16.refs_1_, bf16[640,128]{1,0:T(8,128)(2,1)S(1)} %collective-permute-done.17.refs_2_), custom_call_target="tpu_custom_call" | custom-call | tf_op jit(solution)/shard_map/pallas_call | solution.py:184
  (2 shorter events, 0.0 us)
Async XLA Ops:
  0.0 29.3 %collective-permute-start.3 = (bf16[128,5120]{1,0:T(8,128)(2,1)}, bf16[128,5120]{1,0:T(8,128)(2,1)S(1)}, u32[]{:S(2)}, u32[]{:S(2)}) collective-permute-start(bf16[128,5120]{1,0:T(8,128)(2,1)} %refs_4_.1), channel_id=1, source_target_pairs={{0,1},{1,0},{2,3},{3,2},{4,5},{5,4},{6,7},{7,6},{8,9},{9,8},{10,11... | collective-permute-start | bytes 3932168 | tf_op jit(solution)/shard_map/ppermute | solution.py:218
  0.5 46.2 %collective-permute-start.12 = (bf16[5120,128]{1,0:T(8,128)(2,1)}, bf16[5120,128]{1,0:T(8,128)(2,1)S(1)}, u32[]{:S(2)}, u32[]{:S(2)}) collective-permute-start(bf16[5120,128]{1,0:T(8,128)(2,1)} %refs_0_.9), channel_id=1, source_target_pairs={{0,1},{1,0},{2,3},{3,2},{4,5},{5,4},{6,7},{7,6},{8,9},{9,8},{10,11... | collective-permute-start | bytes 3932168 | tf_op jit(solution)/shard_map/ppermute | solution.py:218
  0.5 46.2 %collective-permute-start.13 = (bf16[5120,128]{1,0:T(8,128)(2,1)}, bf16[5120,128]{1,0:T(8,128)(2,1)S(1)}, u32[]{:S(2)}, u32[]{:S(2)}) collective-permute-start(bf16[5120,128]{1,0:T(8,128)(2,1)} %refs_1_.7), channel_id=1, source_target_pairs={{0,1},{1,0},{2,3},{3,2},{4,5},{5,4},{6,7},{7,6},{8,9},{9,8},{10,11... | collective-permute-start | bytes 3932168 | tf_op jit(solution)/shard_map/ppermute | solution.py:218
  1.0 45.7 %collective-permute-start.14 = (bf16[5120,128]{1,0:T(8,128)(2,1)}, bf16[5120,128]{1,0:T(8,128)(2,1)S(1)}, u32[]{:S(2)}, u32[]{:S(2)}) collective-permute-start(bf16[5120,128]{1,0:T(8,128)(2,1)} %refs_2_.7), channel_id=1, source_target_pairs={{0,1},{1,0},{2,3},{3,2},{4,5},{5,4},{6,7},{7,6},{8,9},{9,8},{10,11... | collective-permute-start | bytes 3932168 | tf_op jit(solution)/shard_map/ppermute | solution.py:218
  1.0 12.2 %collective-permute-start.1 = (bf16[128,640]{1,0:T(8,128)(2,1)}, bf16[128,640]{1,0:T(8,128)(2,1)S(1)}, u32[]{:S(2)}, u32[]{:S(2)}) collective-permute-start(bf16[128,640]{1,0:T(8,128)(2,1)} %refs_0_.5), channel_id=1, source_target_pairs={{0,4},{1,5},{2,6},{3,7},{4,0},{5,1},{6,2},{7,3},{8,12},{9,13},{10,... | collective-permute-start | bytes 491528 | tf_op jit(solution)/shard_map/ppermute | solution.py:215
  13.2 5.7 %collective-permute-start = (bf16[128,640]{1,0:T(8,128)(2,1)}, bf16[128,640]{1,0:T(8,128)(2,1)S(1)}, u32[]{:S(2)}, u32[]{:S(2)}) collective-permute-start(bf16[128,640]{1,0:T(8,128)(2,1)} %refs_0_.5), channel_id=1, source_target_pairs={{0,2},{1,3},{2,0},{3,1},{4,6},{5,7},{6,4},{7,5},{8,10},{9,11},{10,... | collective-permute-start | bytes 491528 | tf_op jit(solution)/shard_map/ppermute | solution.py:215
  18.9 8.0 %collective-permute-start.2 = (bf16[128,640]{1,0:T(8,128)(2,1)}, bf16[128,640]{1,0:T(8,128)(2,1)S(1)}, u32[]{:S(2)}, u32[]{:S(2)}) collective-permute-start(bf16[128,640]{1,0:T(8,128)(2,1)} %refs_0_.5), channel_id=1, source_target_pairs={{0,6},{1,7},{2,4},{3,5},{4,2},{5,3},{6,0},{7,1},{8,14},{9,15},{10,... | collective-permute-start | bytes 491528 | tf_op jit(solution)/shard_map/ppermute | solution.py:215
  23.1 0.8 %copy-start.5 = (bf16[128,128]{1,0:T(8,128)(2,1)S(1)}, bf16[128,128]{1,0:T(8,128)(2,1)}, u32[]{:S(2)}) copy-start(bf16[128,128]{1,0:T(8,128)(2,1)} %query_ref.1) | copy-start | bytes 98308
  23.8 0.8 %copy-start.6 = (bf16[128,128]{1,0:T(8,128)(2,1)S(1)}, bf16[128,128]{1,0:T(8,128)(2,1)}, u32[]{:S(2)}) copy-start(bf16[128,128]{1,0:T(8,128)(2,1)} %key_ref.1) | copy-start | bytes 98308
  24.6 0.8 %copy-start.7 = (bf16[128,128]{1,0:T(8,128)(2,1)S(1)}, bf16[128,128]{1,0:T(8,128)(2,1)}, u32[]{:S(2)}) copy-start(bf16[128,128]{1,0:T(8,128)(2,1)} %value_ref.1) | copy-start | bytes 98308
  25.3 18.0 %copy-start.8 = (s32[4,3]{1,0:T(4,128)S(1)}, s32[4,3]{1,0:T(4,128)}, u32[]{:S(2)}) copy-start(s32[4,3]{1,0:T(4,128)} %lists_ref.1) | copy-start | bytes 148
  26.9 5.5 %collective-permute-start.10 = (bf16[128,384]{1,0:T(8,128)(2,1)S(1)}, bf16[128,384]{1,0:T(8,128)(2,1)S(1)}, u32[]{:S(2)}, u32[]{:S(2)}) collective-permute-start(bf16[128,384]{1,0:T(8,128)(2,1)S(1)} %shard_map.92.refs_0_.refs_4_), channel_id=1, source_target_pairs={{0,24},{8,16},{16,8},{24,0},{1,25},{9,17},{17,9},{25,1},{2,26},{10... | collective-permute-start | bytes 294920 | tf_op jit(solution)/shard_map/ppermute | solution.py:221
  29.3 1.3 %copy-start.3 = (bf16[128,5120]{1,0:T(8,128)(2,1)S(1)}, bf16[128,5120]{1,0:T(8,128)(2,1)}, u32[]{:S(2)}) copy-start(bf16[128,5120]{1,0:T(8,128)(2,1)} %refs_4_.1) | copy-start | bytes 3932164
  30.7 0.9 %copy-start.4 = (bf16[128,640]{1,0:T(8,128)(2,1)S(1)}, bf16[128,640]{1,0:T(8,128)(2,1)}, u32[]{:S(2)}) copy-start(bf16[128,640]{1,0:T(8,128)(2,1)} %refs_0_.5) | copy-start | bytes 491524
  31.6 16.4 %copy-start.2 = (bf16[5120,128]{1,0:T(8,128)(2,1)S(1)}, bf16[5120,128]{1,0:T(8,128)(2,1)}, u32[]{:S(2)}) copy-start(bf16[5120,128]{1,0:T(8,128)(2,1)} %refs_2_.7) | copy-start | bytes 3932164
  32.2 1.8 %collective-permute-start.4 = (f32[128,128]{1,0:T(8,128)S(1)}, f32[128,128]{1,0:T(8,128)S(1)}, u32[]{:S(2)}, u32[]{:S(2)}) collective-permute-start(f32[128,128]{1,0:T(8,128)S(1)} %get-tuple-element.11), channel_id=1, source_target_pairs={{0,1},{1,0},{2,3},{3,2},{4,5},{5,4},{6,7},{7,6},{8,9},{9,8},{10,11... | collective-permute-start | bytes 196616 | tf_op jit(solution)/shard_map/ppermute | solution.py:218
  32.4 5.0 %collective-permute-start.9 = (bf16[128,384]{1,0:T(8,128)(2,1)S(1)}, bf16[128,384]{1,0:T(8,128)(2,1)S(1)}, u32[]{:S(2)}, u32[]{:S(2)}) collective-permute-start(bf16[128,384]{1,0:T(8,128)(2,1)S(1)} %shard_map.92.refs_0_.refs_4_), channel_id=1, source_target_pairs={{0,16},{8,24},{16,0},{24,8},{1,17},{9,25},{17,1},{25,9},{2,18},{10... | collective-permute-start | bytes 294920 | tf_op jit(solution)/shard_map/ppermute | solution.py:221
  33.9 5.5 %collective-permute-start.8 = (bf16[128,384]{1,0:T(8,128)(2,1)S(1)}, bf16[128,384]{1,0:T(8,128)(2,1)S(1)}, u32[]{:S(2)}, u32[]{:S(2)}) collective-permute-start(bf16[128,384]{1,0:T(8,128)(2,1)S(1)} %shard_map.92.refs_0_.refs_4_), channel_id=1, source_target_pairs={{0,8},{8,0},{16,24},{24,16},{1,9},{9,1},{17,25},{25,17},{2,10},{10... | collective-permute-start | bytes 294920 | tf_op jit(solution)/shard_map/ppermute | solution.py:221
  35.4 12.6 %copy-start.1 = (bf16[5120,128]{1,0:T(8,128)(2,1)S(1)}, bf16[5120,128]{1,0:T(8,128)(2,1)}, u32[]{:S(2)}) copy-start(bf16[5120,128]{1,0:T(8,128)(2,1)} %refs_1_.7) | copy-start | bytes 3932164
  35.4 12.6 %copy-start = (bf16[5120,128]{1,0:T(8,128)(2,1)S(1)}, bf16[5120,128]{1,0:T(8,128)(2,1)}, u32[]{:S(2)}) copy-start(bf16[5120,128]{1,0:T(8,128)(2,1)} %refs_0_.9) | copy-start | bytes 3932164
  37.5 4.8 %collective-permute-start.7 = (bf16[128,128]{1,0:T(8,128)(2,1)S(1)}, bf16[128,128]{1,0:T(8,128)(2,1)S(1)}, u32[]{:S(2)}, u32[]{:S(2)}) collective-permute-start(bf16[128,128]{1,0:T(8,128)(2,1)S(1)} %add_convert_fusion.grad_ref.refs_0_), channel_id=1, source_target_pairs={{0,24},{8,16},{16,8},{24,0},{1,25},{9,17},{17,9},{25,1},{2,26},{10... | collective-permute-start | bytes 98312 | tf_op jit(solution)/shard_map/ppermute | solution.py:221
  39.5 6.3 %collective-permute-start.6 = (bf16[128,128]{1,0:T(8,128)(2,1)S(1)}, bf16[128,128]{1,0:T(8,128)(2,1)S(1)}, u32[]{:S(2)}, u32[]{:S(2)}) collective-permute-start(bf16[128,128]{1,0:T(8,128)(2,1)S(1)} %add_convert_fusion.grad_ref.refs_0_), channel_id=1, source_target_pairs={{0,16},{8,24},{16,0},{24,8},{1,17},{9,25},{17,1},{25,9},{2,18},{10... | collective-permute-start | bytes 98312 | tf_op jit(solution)/shard_map/ppermute | solution.py:221
  42.3 3.9 %collective-permute-start.5 = (bf16[128,128]{1,0:T(8,128)(2,1)S(1)}, bf16[128,128]{1,0:T(8,128)(2,1)S(1)}, u32[]{:S(2)}, u32[]{:S(2)}) collective-permute-start(bf16[128,128]{1,0:T(8,128)(2,1)S(1)} %add_convert_fusion.grad_ref.refs_0_), channel_id=1, source_target_pairs={{0,8},{8,0},{16,24},{24,16},{1,9},{9,1},{17,25},{25,17},{2,10},{10... | collective-permute-start | bytes 98312 | tf_op jit(solution)/shard_map/ppermute | solution.py:221
  46.6 1.4 %collective-permute-start.11 = (bf16[128,384]{1,0:T(8,128)(2,1)S(1)}, bf16[128,384]{1,0:T(8,128)(2,1)S(1)}, u32[]{:S(2)}, u32[]{:S(2)}) collective-permute-start(bf16[128,384]{1,0:T(8,128)(2,1)S(1)} %shard_map.95.own_ref), channel_id=1, source_target_pairs={{0,1},{1,0},{2,3},{3,2},{4,5},{5,4},{6,7},{7,6},{8,9},{9,8},{10,11... | collective-permute-start | bytes 294920 | tf_op jit(solution)/shard_map/ppermute | solution.py:218
  48.4 13.4 %collective-permute-start.15 = (bf16[640,128]{1,0:T(8,128)(2,1)S(1)}, bf16[640,128]{1,0:T(8,128)(2,1)S(1)}, u32[]{:S(2)}, u32[]{:S(2)}) collective-permute-start(bf16[640,128]{1,0:T(8,128)(2,1)S(1)} %shard_map.97), channel_id=1, source_target_pairs={{0,4},{1,5},{2,6},{3,7},{4,0},{5,1},{6,2},{7,3},{8,12},{9,13},{10,... | collective-permute-start | bytes 491528 | tf_op jit(solution)/shard_map/ppermute | solution.py:215
  53.2 9.4 %collective-permute-start.16 = (bf16[640,128]{1,0:T(8,128)(2,1)S(1)}, bf16[640,128]{1,0:T(8,128)(2,1)S(1)}, u32[]{:S(2)}, u32[]{:S(2)}) collective-permute-start(bf16[640,128]{1,0:T(8,128)(2,1)S(1)} %shard_map.98), channel_id=1, source_target_pairs={{0,2},{1,3},{2,0},{3,1},{4,6},{5,7},{6,4},{7,5},{8,10},{9,11},{10,... | collective-permute-start | bytes 491528 | tf_op jit(solution)/shard_map/ppermute | solution.py:215
  53.7 11.6 %collective-permute-start.17 = (bf16[640,128]{1,0:T(8,128)(2,1)S(1)}, bf16[640,128]{1,0:T(8,128)(2,1)S(1)}, u32[]{:S(2)}, u32[]{:S(2)}) collective-permute-start(bf16[640,128]{1,0:T(8,128)(2,1)S(1)} %shard_map.99), channel_id=1, source_target_pairs={{0,6},{1,7},{2,4},{3,5},{4,2},{5,3},{6,0},{7,1},{8,14},{9,15},{10,... | collective-permute-start | bytes 491528 | tf_op jit(solution)/shard_map/ppermute | solution.py:215
where the time goes:
time: 66.5 us; the launch traced here: 66.1 us
  waiting for transfers between devices  30.4 us (46%)
  starting transfers between devices  25.1 us (38%)
  Pallas kernels  5.94 us (9%)
  local copies, waits for them, and re-layouts  4.52 us (7%)
    ppermute x6, waiting for transfers between devices, to_chip(): return lax.ppermute(x, 'tp', [(t, t ^ 2 * step) for t in range(2 * chips)])  24.2 us
    ppermute x6, starting transfers between devices, to_chip(): return lax.ppermute(x, 'tp', [(t, t ^ 2 * step) for t in range(2 * chips)])  14.9 us
    ppermute x6, starting transfers between devices, to_slab(): return lax.ppermute(x, 'ctx', [(c, c ^ turn) for c in range(slabs)])  9.04 us
    pallas_call x10, Pallas kernels, call(): pl.pallas_call(kernel, in_specs=[SMEM if flag else VMEM for flag in ints]...  5.94 us
    ppermute x6, waiting for transfers between devices, to_slab(): return lax.ppermute(x, 'ctx', [(c, c ^ turn) for c in range(slabs)])  4.85 us
    unnamed x18, local copies, waits for them, and re-layouts  4.52 us
  transfers between devices with their start and end apart: 18, of which 11 were waited for; matrix products, arithmetic and copies ran while one was open for 0% of the time, Pallas kernels for 7%

commit v1 on v0

--- a/solution.py
+++ b/solution.py
@@ -64,22 +64,50 @@
     return lax.psum_scatter(feature_sum, "tp", scatter_dimension=0, tiled=True)
 
 
-def pack_kernel(query_ref, key_ref, value_ref, out_ref):
+def pack_kernel(query_ref, key_ref, value_ref, out_ref, sems):
     size = query_ref.shape[1]
-    out_ref[:, :size] = query_ref[...]
-    out_ref[:, size : 2 * size] = key_ref[...]
-    out_ref[:, 2 * size :] = value_ref[...]
-
-
-def attn_grad_kernel(chips, cols, *refs):
-    blocks = refs[:chips]
-    own_w, mate_w, own_ref, mate_ref = refs[chips:]
+    copies = [
+        pltpu.make_async_copy(
+            part, out_ref.at[:, place * size : (place + 1) * size], sems.at[place]
+        )
+        for place, part in enumerate((query_ref, key_ref, value_ref))
+    ]
+    for copy in copies:
+        copy.start()
+    for copy in copies:
+        copy.wait()
+
+
+def fetch_kernel(count, *refs):
+    sems = refs[2 * count]
+    copies = [
+        pltpu.make_async_copy(refs[place], refs[count + place], sems.at[place])
+        for place in range(count)
+    ]
+    for copy in copies:
+        copy.start()
+    for copy in copies:
+        copy.wait()
+
+
+def is_inner():
+    chip = lax.axis_index("tp") >> 1
+    return (chip == 1) | (chip == 2)
+
+
+def attn_grad_kernel(cols, own_block, near, cross_in, cross_out, mid, relay, own_w, mate_w, own_ref, mate_ref):
     index = lax.axis_index("tp")
+    inner = is_inner()
+    blocks = [
+        own_block[...],
+        near[...],
+        jnp.where(inner, cross_in[...], cross_out[...]),
+        jnp.where(inner, mid[...], relay[...]),
+    ]
     own = jnp.zeros(own_ref.shape, jnp.float32)
     mate = jnp.zeros(own_ref.shape, jnp.float32)
-    for step in range(chips):
+    for step, block in enumerate(blocks):
         start = pl.multiple_of((index ^ (2 * step)) * cols, 128)
-        block = blocks[step][...]
         own = own + dot_f32(block, own_w[:, pl.ds(start, cols)], CONTRACT_LAST)
         mate = mate + dot_f32(block, mate_w[:, pl.ds(start, cols)], CONTRACT_LAST)
     own_ref[...] = own
@@ -156,7 +184,7 @@
 
 
 def project_kernel(rows, step, own_ref, mate_ref, *refs):
-    weights, out_ref = refs[:6], refs[6]
+    weights, out_ref = refs[:6], refs[-1]
     start = pl.multiple_of((lax.axis_index("tp") ^ (2 * step)) * rows, 16)
     size = own_ref.shape[1] // 3
     total = None
@@ -165,37 +193,48 @@
         part = grads[:, (place % 3) * size : (place % 3 + 1) * size]
         term = dot_f32(weight[pl.ds(start, rows), :], part, CONTRACT_LAST)
         total = term if total is None else total + term
+    for fed in refs[6:-1]:
+        total = total + fed[...].astype(jnp.float32)
     out_ref[...] = total.astype(out_ref.dtype)
 
 
-def sum_kernel(own_ref, *refs):
-    total = own_ref[...]
-    for part in refs[:-1]:
-        total = total + part[...].astype(jnp.float32)
-    refs[-1][...] = total
-
-
-def call(kernel, args, outs, fast_out=True):
+def sum_kernel(own_ref, near, cross_in, cross_out, mid, out_ref):
+    full = jnp.float32
+    total = own_ref[...] + near[...].astype(full)
+    through = cross_in[...].astype(full) + mid[...].astype(full)
+    out_ref[...] = total + jnp.where(is_inner(), through, cross_out[...].astype(full))
+
+
+def call(kernel, args, outs, fast_out=True, raw=False, sems=0):
     ints = [x.dtype == jnp.int32 for x in args]
+    space = pltpu.HBM if raw else pltpu.VMEM
     args = [
-        x if flag else pltpu.with_memory_space_constraint(x, pltpu.VMEM)
-        for x, flag in zip(args, ints)
+        x if flag else pltpu.with_memory_space_constraint(x, space) for x, flag in zip(args, ints)
     ]
+    there = pl.BlockSpec(memory_space=space)
     return pl.pallas_call(
         kernel,
-        in_specs=[SMEM if flag else VMEM for flag in ints],
+        in_specs=[SMEM if flag else there for flag in ints],
         out_specs=[VMEM] * len(outs),
         out_shape=[
             pltpu.VMEM(shape, kind) if fast_out else jax.ShapeDtypeStruct(shape, kind)
             for shape, kind in outs
         ],
+        scratch_shapes=[pltpu.SemaphoreType.DMA((sems,))] if sems else [],
         compiler_params=pltpu.CompilerParams(vmem_limit_bytes=16 << 20),
     )(*args)
 
 
+FEED = ((0, 1), (3, 2))
+RELAY = ((2, 3), (1, 0))
+CROSS_IN = ((0, 2), (3, 1))
+CROSS_OUT = ((2, 0), (1, 3))
+MID = ((1, 2), (2, 1))
+NEAR = ((0, 1), (1, 0), (2, 3), (3, 2))
+
+
 def few_slabs(
     slabs,
-    chips,
     grad_out,
     w_out,
     query_proj,
@@ -209,32 +248,42 @@
     rows, cols = grad_out.shape
     size = query_proj.shape[1]
     half, full = jnp.bfloat16, jnp.float32
-    hops = sorted(range(1, chips), key=lambda step: (step & (step - 1) != 0, -step))
-
-    def to_chip(x, step):
-        return lax.ppermute(x, "tp", [(t, t ^ (2 * step)) for t in range(2 * chips)])
+
+    def along(x, way):
+        pairs = [(2 * a + core, 2 * b + core) for a, b in way for core in range(2)]
+        return lax.ppermute(x, "tp", pairs)
 
     def to_mate(x):
-        return lax.ppermute(x, "tp", [(t, t ^ 1) for t in range(2 * chips)])
+        return lax.ppermute(x, "tp", [(t, t ^ 1) for t in range(8)])
 
     def to_slab(x, turn):
         return lax.ppermute(x, "ctx", [(c, c ^ turn) for c in range(slabs)])
 
-    blocks = [grad_out] + [to_chip(grad_out, step) for step in range(1, chips)]
-    (pack,) = call(pack_kernel, [query_proj, key_proj, value_proj], [((rows, 3 * size), half)])
+    g_in = along(grad_out, CROSS_IN)
+    g_near = along(grad_out, NEAR)
+    g_out = along(grad_out, CROSS_OUT)
+    g_mid = along(grad_out, MID)
+    g_relay = along(g_in, RELAY)
+    (pack,) = call(
+        pack_kernel, [query_proj, key_proj, value_proj], [((rows, 3 * size), half)],
+        raw=True, sems=3,
+    )
     packs = [pack] + [to_slab(pack, turn) for turn in range(1, slabs)]
     mate_out = to_mate(w_out)
     own_w = [w_query, w_key, w_value]
     mate_w = [to_mate(w) for w in own_w]
-
+    near_out, near_grad = call(
+        functools.partial(fetch_kernel, 2), [w_out, grad_out],
+        [(w_out.shape, half), (grad_out.shape, half)], raw=True, sems=2,
+    )
     prob_row, prob_col, attn_out = call(
         functools.partial(softmax_kernel, slabs, tile_keys.shape[1]),
         [tile_keys, *packs],
         [((rows, slabs * rows), full), ((slabs * rows, rows), full), ((slabs * rows, size), full)],
     )
     own_part, mate_part = call(
-        functools.partial(attn_grad_kernel, chips, cols),
-        [*blocks, w_out, mate_out],
+        functools.partial(attn_grad_kernel, cols),
+        [near_grad, g_near, g_in, g_out, g_mid, g_relay, near_out, mate_out],
         [((rows, size), full), ((rows, size), full)],
     )
     grad = (own_part + to_mate(mate_part)).astype(half)
@@ -250,26 +299,35 @@
         [((rows, 3 * size), half)],
     )
     mate_grads = to_mate(own_grads)
-    arrived = []
-    for step in hops + [0]:
+
+    def project(step, kind, *fed):
         (part,) = call(
             functools.partial(project_kernel, cols, step),
-            [own_grads, mate_grads, *own_w, *mate_w],
-            [((cols, rows), half if step else full)],
+            [own_grads, mate_grads, *own_w, *mate_w, *fed],
+            [((cols, rows), kind)],
         )
-        if step:
-            arrived.append(to_chip(part, step))
-    (out,) = call(sum_kernel, [part, *arrived], [((cols, rows), full)], fast_out=False)
+        return part
+
+    third, second = project(3, half), project(2, half)
+    fed = along(third, FEED)
+    f_in = along(second, CROSS_IN)
+    f_mid = along(third, MID)
+    f_near = along(project(1, half), NEAR)
+    f_out = along(project(2, half, fed), CROSS_OUT)
+    (out,) = call(
+        sum_kernel,
+        [project(0, full), f_near, f_in, f_out, f_mid],
+        [((cols, rows), full)],
+        fast_out=False,
+    )
     return out
 
 
 def solution(mesh):
     slabs, shards = mesh.shape["ctx"], mesh.shape["tp"]
-    chips = shards // 2
-    few = 1 < slabs <= 8 and slabs & (slabs - 1) == 0
-    few = few and shards == 2 * chips and 2 <= chips <= 8 and chips & (chips - 1) == 0
+    few = slabs in (4, 8) and shards == 8
     return jax.shard_map(
-        functools.partial(few_slabs, slabs, chips) if few else many_slabs,
+        functools.partial(few_slabs, slabs) if few else many_slabs,
         mesh=mesh,
         in_specs=(
             P("ctx", "tp"),

time: 66.5 us -> 75.8 us (1.14)
  waiting for transfers between devices: 30.4 us -> 38.2 us
  local copies, waits for them, and re-layouts: 4.52 us -> 0.02 us
  starting transfers between devices: 25.1 us -> 28.3 us
  Pallas kernels: 5.94 us -> 8.55 us
    ppermute x12 -> x16, waiting for transfers between devices: 25.5 us -> 31.9 us  [the longest x10 30.6 us: along(): return lax.ppermute(x, 'tp', pairs)]
    unnamed x18 -> x8, local copies, waits for them, and re-layouts: 4.52 us -> 0.02 us
    ppermute x12 -> x16, starting transfers between devices: 16.1 us -> 20.1 us  [the longest x10 18.9 us: along(): return lax.ppermute(x, 'tp', pairs)]
    pallas_call x10 -> x12, Pallas kernels: 5.94 us -> 8.55 us  [call(): pl.pallas_call(kernel, in_specs=[SMEM if flag else there for flag in ints...]
    ppermute x6, waiting for transfers between devices: 4.85 us -> 6.35 us  [to_slab(): return lax.ppermute(x, 'ctx', [(c, c ^ turn) for c in range(slabs)])]
    ppermute x6, starting transfers between devices: 9.04 us -> 8.23 us  [to_slab(): return lax.ppermute(x, 'ctx', [(c, c ^ turn) for c in range(slabs)])]
  transfers between devices with their start and end apart: 18 -> 22, of which waited for: 11 -> 13; matrix products, arithmetic and copies ran while one was open for 0% -> 0% of each run, Pallas kernels for 7% -> 10%
where the time goes in v1:
time: 75.8 us; the launch traced here: 75.4 us
  waiting for transfers between devices  38.2 us (50%)
  starting transfers between devices  28.3 us (37%)
  Pallas kernels  8.55 us (11%)
    ppermute x10, waiting for transfers between devices, along(): return lax.ppermute(x, 'tp', pairs)  30.6 us
    ppermute x10, starting transfers between devices, along(): return lax.ppermute(x, 'tp', pairs)  18.9 us
    pallas_call x12, Pallas kernels, call(): pl.pallas_call(kernel, in_specs=[SMEM if flag else there for flag in ints...  8.55 us
    ppermute x6, starting transfers between devices, to_slab(): return lax.ppermute(x, 'ctx', [(c, c ^ turn) for c in range(slabs)])  8.23 us
    ppermute x6, waiting for transfers between devices, to_slab(): return lax.ppermute(x, 'ctx', [(c, c ^ turn) for c in range(slabs)])  6.35 us
  transfers between devices with their start and end apart: 22, of which 13 were waited for; matrix products, arithmetic and copies ran while one was open for 0% of the time, Pallas kernels for 10%

profile of v1, /device:TPU:0, one launch (start us, length us, event | category | flops | bytes accessed | tf_op | source)
XLA Modules:
  0.0 75.4 jit_solution(7728247957179893912)
XLA Ops:
  0.0 0.5 collective-permute-start.5
  0.5 0.0 collective-permute-start.14
  0.5 0.5 collective-permute-start.15
  1.0 0.0 collective-permute-start.16
  1.0 6.0 %collective-permute-start.1 = (bf16[128,640]{1,0:T(8,128)(2,1)}, bf16[128,640]{1,0:T(8,128)(2,1)S(1)}, u32[]{:S(2)}, u32[]{:S(2)}) collective-permute-start(bf16[128,640]{1,0:T(8,128)(2,1)} %refs_1_.6), channel_id=1, source_target_pairs={{0,4},{1,5},{6,2},{7,3},{8,12},{9,13},{14,10},{15,11},{16,20},{17,... | collective-permute-start | bytes 491528 | tf_op jit(solution)/shard_map/ppermute | solution.py:254
  7.0 3.9 %collective-permute-done.1.cross_in = bf16[128,640]{1,0:T(8,128)(2,1)S(1)} collective-permute-done((bf16[128,640]{1,0:T(8,128)(2,1)}, bf16[128,640]{1,0:T(8,128)(2,1)S(1)}, u32[]{:S(2)}, u32[]{:S(2)}) %collective-permute-start.1) | collective-permute-done | bytes 163872 | tf_op jit(solution)/shard_map/ppermute | solution.py:254
  10.9 2.3 %collective-permute-start = (bf16[128,640]{1,0:T(8,128)(2,1)}, bf16[128,640]{1,0:T(8,128)(2,1)S(1)}, u32[]{:S(2)}, u32[]{:S(2)}) collective-permute-start(bf16[128,640]{1,0:T(8,128)(2,1)} %refs_1_.6), channel_id=1, source_target_pairs={{0,2},{1,3},{2,0},{3,1},{4,6},{5,7},{6,4},{7,5},{8,10},{9,11},{10,... | collective-permute-start | bytes 491528 | tf_op jit(solution)/shard_map/ppermute | solution.py:254
  13.2 3.7 %collective-permute-done.near = bf16[128,640]{1,0:T(8,128)(2,1)S(1)} collective-permute-done((bf16[128,640]{1,0:T(8,128)(2,1)}, bf16[128,640]{1,0:T(8,128)(2,1)S(1)}, u32[]{:S(2)}, u32[]{:S(2)}) %collective-permute-start) | collective-permute-done | bytes 163872 | tf_op jit(solution)/shard_map/ppermute | solution.py:254
  16.9 1.3 %collective-permute-start.2 = (bf16[128,640]{1,0:T(8,128)(2,1)}, bf16[128,640]{1,0:T(8,128)(2,1)S(1)}, u32[]{:S(2)}, u32[]{:S(2)}) collective-permute-start(bf16[128,640]{1,0:T(8,128)(2,1)} %refs_1_.6), channel_id=1, source_target_pairs={{4,0},{5,1},{2,6},{3,7},{12,8},{13,9},{10,14},{11,15},{20,16},{21,... | collective-permute-start | bytes 491528 | tf_op jit(solution)/shard_map/ppermute | solution.py:254
  18.2 7.0 %collective-permute-done.2.cross_out = bf16[128,640]{1,0:T(8,128)(2,1)S(1)} collective-permute-done((bf16[128,640]{1,0:T(8,128)(2,1)}, bf16[128,640]{1,0:T(8,128)(2,1)S(1)}, u32[]{:S(2)}, u32[]{:S(2)}) %collective-permute-start.2) | collective-permute-done | bytes 163872 | tf_op jit(solution)/shard_map/ppermute | solution.py:254
  25.2 0.7 collective-permute-start.3
  25.9 0.0 collective-permute-done.3.mid
  25.9 1.3 %collective-permute-start.4 = (bf16[128,640]{1,0:T(8,128)(2,1)S(1)}, bf16[128,640]{1,0:T(8,128)(2,1)S(1)}, u32[]{:S(2)}, u32[]{:S(2)}) collective-permute-start(bf16[128,640]{1,0:T(8,128)(2,1)S(1)} %collective-permute-done.1.cross_in), channel_id=1, source_target_pairs={{4,6},{5,7},{2,0},{3,1},{12,14},{13,15},{10,8},{11,9},{20,22},{21,... | collective-permute-start | bytes 491528 | tf_op jit(solution)/shard_map/ppermute | solution.py:254
  27.2 0.8 %shard_map.93.refs_0_.refs_4_ = bf16[128,384]{1,0:T(8,128)(2,1)S(1)} custom-call(bf16[128,128]{1,0:T(8,128)(2,1)} %query_ref.1, bf16[128,128]{1,0:T(8,128)(2,1)} %key_ref.1, bf16[128,128]{1,0:T(8,128)(2,1)} %value_ref.1), custom_call_target="tpu_custom_call" | custom-call | tf_op jit(solution)/shard_map/pallas_call | solution.py:215
  28.0 8.9 %collective-permute-done.4.relay = bf16[128,640]{1,0:T(8,128)(2,1)S(1)} collective-permute-done((bf16[128,640]{1,0:T(8,128)(2,1)S(1)}, bf16[128,640]{1,0:T(8,128)(2,1)S(1)}, u32[]{:S(2)}, u32[]{:S(2)}) %collective-permute-start.4) | collective-permute-done | bytes 163872 | tf_op jit(solution)/shard_map/ppermute | solution.py:254
  36.9 1.5 %collective-permute-start.10 = (bf16[128,384]{1,0:T(8,128)(2,1)S(1)}, bf16[128,384]{1,0:T(8,128)(2,1)S(1)}, u32[]{:S(2)}, u32[]{:S(2)}) collective-permute-start(bf16[128,384]{1,0:T(8,128)(2,1)S(1)} %shard_map.93.refs_0_.refs_4_), channel_id=1, source_target_pairs={{0,8},{8,0},{16,24},{24,16},{1,9},{9,1},{17,25},{25,17},{2,10},{10... | collective-permute-start | bytes 294920 | tf_op jit(solution)/shard_map/ppermute | solution.py:260
  38.4 1.3 %shard_map.91 = (bf16[128,5120]{1,0:T(8,128)(2,1)S(1)}, bf16[128,640]{1,0:T(8,128)(2,1)S(1)}) custom-call(bf16[128,5120]{1,0:T(8,128)(2,1)} %refs_0_.6, bf16[128,640]{1,0:T(8,128)(2,1)} %refs_1_.6), custom_call_target="tpu_custom_call" | custom-call | tf_op jit(solution)/shard_map/pallas_call | solution.py:215
  39.8 0.0 collective-permute-done.5.mate_w
  39.8 0.0 copy-start.3
  39.8 0.0 copy-start.2
  39.8 0.6 shard_map.92
  40.4 0.1 collective-permute-start.6
  40.5 1.0 %collective-permute-done.10.refs_1_.refs_5_ = bf16[128,384]{1,0:T(8,128)(2,1)S(1)} collective-permute-done((bf16[128,384]{1,0:T(8,128)(2,1)S(1)}, bf16[128,384]{1,0:T(8,128)(2,1)S(1)}, u32[]{:S(2)}, u32[]{:S(2)}) %collective-permute-start.10) | collective-permute-done | bytes 98336 | tf_op jit(solution)/shard_map/ppermute | solution.py:260
  41.6 1.5 %collective-permute-start.11 = (bf16[128,384]{1,0:T(8,128)(2,1)S(1)}, bf16[128,384]{1,0:T(8,128)(2,1)S(1)}, u32[]{:S(2)}, u32[]{:S(2)}) collective-permute-start(bf16[128,384]{1,0:T(8,128)(2,1)S(1)} %shard_map.93.refs_0_.refs_4_), channel_id=1, source_target_pairs={{0,16},{8,24},{16,0},{24,8},{1,17},{9,25},{17,1},{25,9},{2,18},{10... | collective-permute-start | bytes 294920 | tf_op jit(solution)/shard_map/ppermute | solution.py:260
  43.1 0.0 collective-permute-done.6
  43.1 1.4 %collective-permute-start.12 = (bf16[128,384]{1,0:T(8,128)(2,1)S(1)}, bf16[128,384]{1,0:T(8,128)(2,1)S(1)}, u32[]{:S(2)}, u32[]{:S(2)}) collective-permute-start(bf16[128,384]{1,0:T(8,128)(2,1)S(1)} %shard_map.93.refs_0_.refs_4_), channel_id=1, source_target_pairs={{0,24},{8,16},{16,8},{24,0},{1,25},{9,17},{17,9},{25,1},{2,26},{10... | collective-permute-start | bytes 294920 | tf_op jit(solution)/shard_map/ppermute | solution.py:260
  44.5 0.0 copy-start.1
  44.5 0.0 copy-start
  44.5 2.8 %collective-permute-done.11.refs_2_.refs_6_ = bf16[128,384]{1,0:T(8,128)(2,1)S(1)} collective-permute-done((bf16[128,384]{1,0:T(8,128)(2,1)S(1)}, bf16[128,384]{1,0:T(8,128)(2,1)S(1)}, u32[]{:S(2)}, u32[]{:S(2)}) %collective-permute-start.11) | collective-permute-done | bytes 98336 | tf_op jit(solution)/shard_map/ppermute | solution.py:260
  47.4 1.0 %collective-permute-start.7 = (bf16[128,128]{1,0:T(8,128)(2,1)S(1)}, bf16[128,128]{1,0:T(8,128)(2,1)S(1)}, u32[]{:S(2)}, u32[]{:S(2)}) collective-permute-start(bf16[128,128]{1,0:T(8,128)(2,1)S(1)} %add_convert_fusion.grad_ref.refs_0_), channel_id=1, source_target_pairs={{0,8},{8,0},{16,24},{24,16},{1,9},{9,1},{17,25},{25,17},{2,10},{10... | collective-permute-start | bytes 98312 | tf_op jit(solution)/shard_map/ppermute | solution.py:260
  48.4 0.6 collective-permute-done.12.refs_3_.refs_7_
  49.0 0.9 %collective-permute-start.8 = (bf16[128,128]{1,0:T(8,128)(2,1)S(1)}, bf16[128,128]{1,0:T(8,128)(2,1)S(1)}, u32[]{:S(2)}, u32[]{:S(2)}) collective-permute-start(bf16[128,128]{1,0:T(8,128)(2,1)S(1)} %add_convert_fusion.grad_ref.refs_0_), channel_id=1, source_target_pairs={{0,16},{8,24},{16,0},{24,8},{1,17},{9,25},{17,1},{25,9},{2,18},{10... | collective-permute-start | bytes 98312 | tf_op jit(solution)/shard_map/ppermute | solution.py:260
  49.8 1.5 %collective-permute-done.7.refs_1_ = bf16[128,128]{1,0:T(8,128)(2,1)S(1)} collective-permute-done((bf16[128,128]{1,0:T(8,128)(2,1)S(1)}, bf16[128,128]{1,0:T(8,128)(2,1)S(1)}, u32[]{:S(2)}, u32[]{:S(2)}) %collective-permute-start.7) | collective-permute-done | bytes 32800 | tf_op jit(solution)/shard_map/ppermute | solution.py:260
  51.3 1.9 %collective-permute-start.9 = (bf16[128,128]{1,0:T(8,128)(2,1)S(1)}, bf16[128,128]{1,0:T(8,128)(2,1)S(1)}, u32[]{:S(2)}, u32[]{:S(2)}) collective-permute-start(bf16[128,128]{1,0:T(8,128)(2,1)S(1)} %add_convert_fusion.grad_ref.refs_0_), channel_id=1, source_target_pairs={{0,24},{8,16},{16,8},{24,0},{1,25},{9,17},{17,9},{25,1},{2,26},{10... | collective-permute-start | bytes 98312 | tf_op jit(solution)/shard_map/ppermute | solution.py:260
  53.2 0.0 copy-done.3
  53.2 2.1 %shard_map.94 = (f32[128,512]{1,0:T(8,128)S(1)}, f32[512,128]{1,0:T(8,128)S(1)}, f32[512,128]{1,0:T(8,128)S(1)}) custom-call(s32[4,3]{1,0:T(4,128)S(1)} %copy-done.3, bf16[128,384]{1,0:T(8,128)(2,1)S(1)} %shard_map.93.refs_0_.refs_4_, bf16[128,384]{1,0:T(8,128)(2,1)S(1)} %collective-permute-done.10.refs_1_.refs_5_, ...), custom_call_target="tpu_custom_call" | custom-call | tf_op jit(solution)/shard_map/pallas_call | solution.py:215
  55.3 0.3 shard_map.95.refs_8_
  55.6 0.0 collective-permute-done.8.refs_2_
  55.6 0.5 collective-permute-done.9.refs_3_
  56.1 0.5 shard_map.96.own_ref
  56.5 0.1 collective-permute-start.13
  56.6 0.0 collective-permute-done.14.refs_3_
  56.6 0.0 collective-permute-done.15.refs_4_
  56.6 0.0 collective-permute-done.16.refs_5_
  56.7 1.3 %collective-permute-done.13.mate_ref = bf16[128,384]{1,0:T(8,128)(2,1)S(1)} collective-permute-done((bf16[128,384]{1,0:T(8,128)(2,1)S(1)}, bf16[128,384]{1,0:T(8,128)(2,1)S(1)}, u32[]{:S(2)}, u32[]{:S(2)}) %collective-permute-start.13) | collective-permute-done | bytes 98336 | tf_op jit(solution)/shard_map/ppermute | solution.py:257
  57.9 0.0 copy-done.2
  57.9 0.0 copy-done.1
  57.9 0.0 copy-done
  57.9 0.4 shard_map.100
  58.4 1.5 %collective-permute-start.19 = (bf16[640,128]{1,0:T(8,128)(2,1)S(1)}, bf16[640,128]{1,0:T(8,128)(2,1)S(1)}, u32[]{:S(2)}, u32[]{:S(2)}) collective-permute-start(bf16[640,128]{1,0:T(8,128)(2,1)S(1)} %shard_map.100), channel_id=1, source_target_pairs={{0,2},{1,3},{6,4},{7,5},{8,10},{9,11},{14,12},{15,13},{16,18},{17,... | collective-permute-start | bytes 491528 | tf_op jit(solution)/shard_map/ppermute | solution.py:254
  59.8 0.7 collective-permute-start.21
  60.5 0.4 shard_map.99
  60.9 4.0 %collective-permute-start.18 = (bf16[640,128]{1,0:T(8,128)(2,1)S(1)}, bf16[640,128]{1,0:T(8,128)(2,1)S(1)}, u32[]{:S(2)}, u32[]{:S(2)}) collective-permute-start(bf16[640,128]{1,0:T(8,128)(2,1)S(1)} %shard_map.99), channel_id=1, source_target_pairs={{0,4},{1,5},{6,2},{7,3},{8,12},{9,13},{14,10},{15,11},{16,20},{17,... | collective-permute-start | bytes 491528 | tf_op jit(solution)/shard_map/ppermute | solution.py:254
  64.9 0.4 shard_map.98
  65.4 0.1 collective-permute-start.17
  65.4 0.0 collective-permute-done.19.refs_6_
  65.4 0.4 shard_map.101
  65.9 1.3 %collective-permute-start.20 = (bf16[640,128]{1,0:T(8,128)(2,1)S(1)}, bf16[640,128]{1,0:T(8,128)(2,1)S(1)}, u32[]{:S(2)}, u32[]{:S(2)}) collective-permute-start(bf16[640,128]{1,0:T(8,128)(2,1)S(1)} %shard_map.101), channel_id=1, source_target_pairs={{4,0},{5,1},{2,6},{3,7},{12,8},{13,9},{10,14},{11,15},{20,16},{21,... | collective-permute-start | bytes 491528 | tf_op jit(solution)/shard_map/ppermute | solution.py:254
  67.2 0.4 shard_map.97.own_ref
  67.6 0.0 collective-permute-done.21.mid
  67.6 1.9 %collective-permute-done.18.cross_in = bf16[640,128]{1,0:T(8,128)(2,1)S(1)} collective-permute-done((bf16[640,128]{1,0:T(8,128)(2,1)S(1)}, bf16[640,128]{1,0:T(8,128)(2,1)S(1)}, u32[]{:S(2)}, u32[]{:S(2)}) %collective-permute-start.18) | collective-permute-done | bytes 163872 | tf_op jit(solution)/shard_map/ppermute | solution.py:254
  69.5 2.4 %collective-permute-done.17.near = bf16[640,128]{1,0:T(8,128)(2,1)S(1)} collective-permute-done((bf16[640,128]{1,0:T(8,128)(2,1)S(1)}, bf16[640,128]{1,0:T(8,128)(2,1)S(1)}, u32[]{:S(2)}, u32[]{:S(2)}) %collective-permute-start.17) | collective-permute-done | bytes 163872 | tf_op jit(solution)/shard_map/ppermute | solution.py:254
  71.9 2.7 %collective-permute-done.20.cross_out = bf16[640,128]{1,0:T(8,128)(2,1)S(1)} collective-permute-done((bf16[640,128]{1,0:T(8,128)(2,1)S(1)}, bf16[640,128]{1,0:T(8,128)(2,1)S(1)}, u32[]{:S(2)}, u32[]{:S(2)}) %collective-permute-start.20) | collective-permute-done | bytes 163872 | tf_op jit(solution)/shard_map/ppermute | solution.py:254
  74.6 0.8 %shard_map.102 = f32[640,128]{1,0:T(8,128)} custom-call(f32[640,128]{1,0:T(8,128)S(1)} %shard_map.97.own_ref, bf16[640,128]{1,0:T(8,128)(2,1)S(1)} %collective-permute-done.17.near, bf16[640,128]{1,0:T(8,128)(2,1)S(1)} %collective-permute-done.18.cross_in, bf16[640,128]{1,0:T(8,128)(2,1)S(1)} %collective-permute-done.20.cross_out, ...), custom_call_target="tpu_custom_call" | custom-call | tf_op jit(solution)/shard_map/pallas_call | solution.py:215
  (1 shorter events, 0.0 us)
Async XLA Ops:
  0.0 39.8 %collective-permute-start.5 = (bf16[128,5120]{1,0:T(8,128)(2,1)}, bf16[128,5120]{1,0:T(8,128)(2,1)S(1)}, u32[]{:S(2)}, u32[]{:S(2)}) collective-permute-start(bf16[128,5120]{1,0:T(8,128)(2,1)} %refs_0_.6), channel_id=1, source_target_pairs={{0,1},{1,0},{2,3},{3,2},{4,5},{5,4},{6,7},{7,6},{8,9},{9,8},{10,11... | collective-permute-start | bytes 3932168 | tf_op jit(solution)/shard_map/ppermute | solution.py:257
  0.5 56.1 %collective-permute-start.14 = (bf16[5120,128]{1,0:T(8,128)(2,1)}, bf16[5120,128]{1,0:T(8,128)(2,1)S(1)}, u32[]{:S(2)}, u32[]{:S(2)}) collective-permute-start(bf16[5120,128]{1,0:T(8,128)(2,1)} %refs_0_.11), channel_id=1, source_target_pairs={{0,1},{1,0},{2,3},{3,2},{4,5},{5,4},{6,7},{7,6},{8,9},{9,8},{10,11... | collective-permute-start | bytes 3932168 | tf_op jit(solution)/shard_map/ppermute | solution.py:257
  0.5 56.1 %collective-permute-start.15 = (bf16[5120,128]{1,0:T(8,128)(2,1)}, bf16[5120,128]{1,0:T(8,128)(2,1)S(1)}, u32[]{:S(2)}, u32[]{:S(2)}) collective-permute-start(bf16[5120,128]{1,0:T(8,128)(2,1)} %refs_1_.11), channel_id=1, source_target_pairs={{0,1},{1,0},{2,3},{3,2},{4,5},{5,4},{6,7},{7,6},{8,9},{9,8},{10,11... | collective-permute-start | bytes 3932168 | tf_op jit(solution)/shard_map/ppermute | solution.py:257
  1.0 55.6 %collective-permute-start.16 = (bf16[5120,128]{1,0:T(8,128)(2,1)}, bf16[5120,128]{1,0:T(8,128)(2,1)S(1)}, u32[]{:S(2)}, u32[]{:S(2)}) collective-permute-start(bf16[5120,128]{1,0:T(8,128)(2,1)} %refs_2_.9), channel_id=1, source_target_pairs={{0,1},{1,0},{2,3},{3,2},{4,5},{5,4},{6,7},{7,6},{8,9},{9,8},{10,11... | collective-permute-start | bytes 3932168 | tf_op jit(solution)/shard_map/ppermute | solution.py:257
  1.0 9.9 %collective-permute-start.1 = (bf16[128,640]{1,0:T(8,128)(2,1)}, bf16[128,640]{1,0:T(8,128)(2,1)S(1)}, u32[]{:S(2)}, u32[]{:S(2)}) collective-permute-start(bf16[128,640]{1,0:T(8,128)(2,1)} %refs_1_.6), channel_id=1, source_target_pairs={{0,4},{1,5},{6,2},{7,3},{8,12},{9,13},{14,10},{15,11},{16,20},{17,... | collective-permute-start | bytes 491528 | tf_op jit(solution)/shard_map/ppermute | solution.py:254
  10.9 6.0 %collective-permute-start = (bf16[128,640]{1,0:T(8,128)(2,1)}, bf16[128,640]{1,0:T(8,128)(2,1)S(1)}, u32[]{:S(2)}, u32[]{:S(2)}) collective-permute-start(bf16[128,640]{1,0:T(8,128)(2,1)} %refs_1_.6), channel_id=1, source_target_pairs={{0,2},{1,3},{2,0},{3,1},{4,6},{5,7},{6,4},{7,5},{8,10},{9,11},{10,... | collective-permute-start | bytes 491528 | tf_op jit(solution)/shard_map/ppermute | solution.py:254
  16.9 8.3 %collective-permute-start.2 = (bf16[128,640]{1,0:T(8,128)(2,1)}, bf16[128,640]{1,0:T(8,128)(2,1)S(1)}, u32[]{:S(2)}, u32[]{:S(2)}) collective-permute-start(bf16[128,640]{1,0:T(8,128)(2,1)} %refs_1_.6), channel_id=1, source_target_pairs={{4,0},{5,1},{2,6},{3,7},{12,8},{13,9},{10,14},{11,15},{20,16},{21,... | collective-permute-start | bytes 491528 | tf_op jit(solution)/shard_map/ppermute | solution.py:254
  25.2 0.7 collective-permute-start.3
  25.9 11.1 %collective-permute-start.4 = (bf16[128,640]{1,0:T(8,128)(2,1)S(1)}, bf16[128,640]{1,0:T(8,128)(2,1)S(1)}, u32[]{:S(2)}, u32[]{:S(2)}) collective-permute-start(bf16[128,640]{1,0:T(8,128)(2,1)S(1)} %collective-permute-done.1.cross_in), channel_id=1, source_target_pairs={{4,6},{5,7},{2,0},{3,1},{12,14},{13,15},{10,8},{11,9},{20,22},{21,... | collective-permute-start | bytes 491528 | tf_op jit(solution)/shard_map/ppermute | solution.py:254
  36.9 4.6 %collective-permute-start.10 = (bf16[128,384]{1,0:T(8,128)(2,1)S(1)}, bf16[128,384]{1,0:T(8,128)(2,1)S(1)}, u32[]{:S(2)}, u32[]{:S(2)}) collective-permute-start(bf16[128,384]{1,0:T(8,128)(2,1)S(1)} %shard_map.93.refs_0_.refs_4_), channel_id=1, source_target_pairs={{0,8},{8,0},{16,24},{24,16},{1,9},{9,1},{17,25},{25,17},{2,10},{10... | collective-permute-start | bytes 294920 | tf_op jit(solution)/shard_map/ppermute | solution.py:260
  39.8 13.4 %copy-start.3 = (s32[4,3]{1,0:T(4,128)S(1)}, s32[4,3]{1,0:T(4,128)}, u32[]{:S(2)}) copy-start(s32[4,3]{1,0:T(4,128)} %lists_ref.1) | copy-start | bytes 148
  39.8 18.1 %copy-start.2 = (bf16[5120,128]{1,0:T(8,128)(2,1)S(1)}, bf16[5120,128]{1,0:T(8,128)(2,1)}, u32[]{:S(2)}) copy-start(bf16[5120,128]{1,0:T(8,128)(2,1)} %refs_2_.9) | copy-start | bytes 3932164
  40.4 2.6 %collective-permute-start.6 = (f32[128,128]{1,0:T(8,128)S(1)}, f32[128,128]{1,0:T(8,128)S(1)}, u32[]{:S(2)}, u32[]{:S(2)}) collective-permute-start(f32[128,128]{1,0:T(8,128)S(1)} %get-tuple-element.15), channel_id=1, source_target_pairs={{0,1},{1,0},{2,3},{3,2},{4,5},{5,4},{6,7},{7,6},{8,9},{9,8},{10,11... | collective-permute-start | bytes 196616 | tf_op jit(solution)/shard_map/ppermute | solution.py:257
  41.6 5.8 %collective-permute-start.11 = (bf16[128,384]{1,0:T(8,128)(2,1)S(1)}, bf16[128,384]{1,0:T(8,128)(2,1)S(1)}, u32[]{:S(2)}, u32[]{:S(2)}) collective-permute-start(bf16[128,384]{1,0:T(8,128)(2,1)S(1)} %shard_map.93.refs_0_.refs_4_), channel_id=1, source_target_pairs={{0,16},{8,24},{16,0},{24,8},{1,17},{9,25},{17,1},{25,9},{2,18},{10... | collective-permute-start | bytes 294920 | tf_op jit(solution)/shard_map/ppermute | solution.py:260
  43.1 5.9 %collective-permute-start.12 = (bf16[128,384]{1,0:T(8,128)(2,1)S(1)}, bf16[128,384]{1,0:T(8,128)(2,1)S(1)}, u32[]{:S(2)}, u32[]{:S(2)}) collective-permute-start(bf16[128,384]{1,0:T(8,128)(2,1)S(1)} %shard_map.93.refs_0_.refs_4_), channel_id=1, source_target_pairs={{0,24},{8,16},{16,8},{24,0},{1,25},{9,17},{17,9},{25,1},{2,26},{10... | collective-permute-start | bytes 294920 | tf_op jit(solution)/shard_map/ppermute | solution.py:260
  44.5 13.4 %copy-start.1 = (bf16[5120,128]{1,0:T(8,128)(2,1)S(1)}, bf16[5120,128]{1,0:T(8,128)(2,1)}, u32[]{:S(2)}) copy-start(bf16[5120,128]{1,0:T(8,128)(2,1)} %refs_1_.11) | copy-start | bytes 3932164
  44.5 13.4 %copy-start = (bf16[5120,128]{1,0:T(8,128)(2,1)S(1)}, bf16[5120,128]{1,0:T(8,128)(2,1)}, u32[]{:S(2)}) copy-start(bf16[5120,128]{1,0:T(8,128)(2,1)} %refs_0_.11) | copy-start | bytes 3932164
  47.4 3.9 %collective-permute-start.7 = (bf16[128,128]{1,0:T(8,128)(2,1)S(1)}, bf16[128,128]{1,0:T(8,128)(2,1)S(1)}, u32[]{:S(2)}, u32[]{:S(2)}) collective-permute-start(bf16[128,128]{1,0:T(8,128)(2,1)S(1)} %add_convert_fusion.grad_ref.refs_0_), channel_id=1, source_target_pairs={{0,8},{8,0},{16,24},{24,16},{1,9},{9,1},{17,25},{25,17},{2,10},{10... | collective-permute-start | bytes 98312 | tf_op jit(solution)/shard_map/ppermute | solution.py:260
  49.0 6.7 %collective-permute-start.8 = (bf16[128,128]{1,0:T(8,128)(2,1)S(1)}, bf16[128,128]{1,0:T(8,128)(2,1)S(1)}, u32[]{:S(2)}, u32[]{:S(2)}) collective-permute-start(bf16[128,128]{1,0:T(8,128)(2,1)S(1)} %add_convert_fusion.grad_ref.refs_0_), channel_id=1, source_target_pairs={{0,16},{8,24},{16,0},{24,8},{1,17},{9,25},{17,1},{25,9},{2,18},{10... | collective-permute-start | bytes 98312 | tf_op jit(solution)/shard_map/ppermute | solution.py:260
  51.3 4.8 %collective-permute-start.9 = (bf16[128,128]{1,0:T(8,128)(2,1)S(1)}, bf16[128,128]{1,0:T(8,128)(2,1)S(1)}, u32[]{:S(2)}, u32[]{:S(2)}) collective-permute-start(bf16[128,128]{1,0:T(8,128)(2,1)S(1)} %add_convert_fusion.grad_ref.refs_0_), channel_id=1, source_target_pairs={{0,24},{8,16},{16,8},{24,0},{1,25},{9,17},{17,9},{25,1},{2,26},{10... | collective-permute-start | bytes 98312 | tf_op jit(solution)/shard_map/ppermute | solution.py:260
  56.5 1.4 %collective-permute-start.13 = (bf16[128,384]{1,0:T(8,128)(2,1)S(1)}, bf16[128,384]{1,0:T(8,128)(2,1)S(1)}, u32[]{:S(2)}, u32[]{:S(2)}) collective-permute-start(bf16[128,384]{1,0:T(8,128)(2,1)S(1)} %shard_map.96.own_ref), channel_id=1, source_target_pairs={{0,1},{1,0},{2,3},{3,2},{4,5},{5,4},{6,7},{7,6},{8,9},{9,8},{10,11... | collective-permute-start | bytes 294920 | tf_op jit(solution)/shard_map/ppermute | solution.py:257
  58.4 7.1 %collective-permute-start.19 = (bf16[640,128]{1,0:T(8,128)(2,1)S(1)}, bf16[640,128]{1,0:T(8,128)(2,1)S(1)}, u32[]{:S(2)}, u32[]{:S(2)}) collective-permute-start(bf16[640,128]{1,0:T(8,128)(2,1)S(1)} %shard_map.100), channel_id=1, source_target_pairs={{0,2},{1,3},{6,4},{7,5},{8,10},{9,11},{14,12},{15,13},{16,18},{17,... | collective-permute-start | bytes 491528 | tf_op jit(solution)/shard_map/ppermute | solution.py:254
  59.8 7.8 %collective-permute-start.21 = (bf16[640,128]{1,0:T(8,128)(2,1)S(1)}, bf16[640,128]{1,0:T(8,128)(2,1)S(1)}, u32[]{:S(2)}, u32[]{:S(2)}) collective-permute-start(bf16[640,128]{1,0:T(8,128)(2,1)S(1)} %shard_map.100), channel_id=1, source_target_pairs={{2,4},{3,5},{4,2},{5,3},{10,12},{11,13},{12,10},{13,11},{18,20},{1... | collective-permute-start | bytes 491528 | tf_op jit(solution)/shard_map/ppermute | solution.py:254
  60.9 8.6 %collective-permute-start.18 = (bf16[640,128]{1,0:T(8,128)(2,1)S(1)}, bf16[640,128]{1,0:T(8,128)(2,1)S(1)}, u32[]{:S(2)}, u32[]{:S(2)}) collective-permute-start(bf16[640,128]{1,0:T(8,128)(2,1)S(1)} %shard_map.99), channel_id=1, source_target_pairs={{0,4},{1,5},{6,2},{7,3},{8,12},{9,13},{14,10},{15,11},{16,20},{17,... | collective-permute-start | bytes 491528 | tf_op jit(solution)/shard_map/ppermute | solution.py:254
  65.4 6.5 %collective-permute-start.17 = (bf16[640,128]{1,0:T(8,128)(2,1)S(1)}, bf16[640,128]{1,0:T(8,128)(2,1)S(1)}, u32[]{:S(2)}, u32[]{:S(2)}) collective-permute-start(bf16[640,128]{1,0:T(8,128)(2,1)S(1)} %shard_map.98), channel_id=1, source_target_pairs={{0,2},{1,3},{2,0},{3,1},{4,6},{5,7},{6,4},{7,5},{8,10},{9,11},{10,... | collective-permute-start | bytes 491528 | tf_op jit(solution)/shard_map/ppermute | solution.py:254
  65.9 8.8 %collective-permute-start.20 = (bf16[640,128]{1,0:T(8,128)(2,1)S(1)}, bf16[640,128]{1,0:T(8,128)(2,1)S(1)}, u32[]{:S(2)}, u32[]{:S(2)}) collective-permute-start(bf16[640,128]{1,0:T(8,128)(2,1)S(1)} %shard_map.101), channel_id=1, source_target_pairs={{4,0},{5,1},{2,6},{3,7},{12,8},{13,9},{10,14},{11,15},{20,16},{21,... | collective-permute-start | bytes 491528 | tf_op jit(solution)/shard_map/ppermute | solution.py:254

commit v2 on v0

--- a/solution.py
+++ b/solution.py
@@ -64,11 +64,30 @@
     return lax.psum_scatter(feature_sum, "tp", scatter_dimension=0, tiled=True)
 
 
-def pack_kernel(query_ref, key_ref, value_ref, out_ref):
+def pack_kernel(query_ref, key_ref, value_ref, out_ref, sems):
     size = query_ref.shape[1]
-    out_ref[:, :size] = query_ref[...]
-    out_ref[:, size : 2 * size] = key_ref[...]
-    out_ref[:, 2 * size :] = value_ref[...]
+    copies = [
+        pltpu.make_async_copy(
+            part, out_ref.at[:, place * size : (place + 1) * size], sems.at[place]
+        )
+        for place, part in enumerate((query_ref, key_ref, value_ref))
+    ]
+    for copy in copies:
+        copy.start()
+    for copy in copies:
+        copy.wait()
+
+
+def fetch_kernel(count, *refs):
+    sems = refs[2 * count]
+    copies = [
+        pltpu.make_async_copy(refs[place], refs[count + place], sems.at[place])
+        for place in range(count)
+    ]
+    for copy in copies:
+        copy.start()
+    for copy in copies:
+        copy.wait()
 
 
 def attn_grad_kernel(chips, cols, *refs):
@@ -156,7 +175,7 @@
 
 
 def project_kernel(rows, step, own_ref, mate_ref, *refs):
-    weights, out_ref = refs[:6], refs[6]
+    weights, out_ref = refs[:6], refs[-1]
     start = pl.multiple_of((lax.axis_index("tp") ^ (2 * step)) * rows, 16)
     size = own_ref.shape[1] // 3
     total = None
@@ -165,6 +184,8 @@
         part = grads[:, (place % 3) * size : (place % 3 + 1) * size]
         term = dot_f32(weight[pl.ds(start, rows), :], part, CONTRACT_LAST)
         total = term if total is None else total + term
+    for fed in refs[6:-1]:
+        total = total + fed[...].astype(jnp.float32)
     out_ref[...] = total.astype(out_ref.dtype)
 
 
@@ -175,20 +196,22 @@
     refs[-1][...] = total
 
 
-def call(kernel, args, outs, fast_out=True):
+def call(kernel, args, outs, fast_out=True, raw=False, sems=0):
     ints = [x.dtype == jnp.int32 for x in args]
+    space = pltpu.HBM if raw else pltpu.VMEM
     args = [
-        x if flag else pltpu.with_memory_space_constraint(x, pltpu.VMEM)
-        for x, flag in zip(args, ints)
+        x if flag else pltpu.with_memory_space_constraint(x, space) for x, flag in zip(args, ints)
     ]
+    there = pl.BlockSpec(memory_space=space)
     return pl.pallas_call(
         kernel,
-        in_specs=[SMEM if flag else VMEM for flag in ints],
+        in_specs=[SMEM if flag else there for flag in ints],
         out_specs=[VMEM] * len(outs),
         out_shape=[
             pltpu.VMEM(shape, kind) if fast_out else jax.ShapeDtypeStruct(shape, kind)
             for shape, kind in outs
         ],
+        scratch_shapes=[pltpu.SemaphoreType.DMA((sems,))] if sems else [],
         compiler_params=pltpu.CompilerParams(vmem_limit_bytes=16 << 20),
     )(*args)
 
@@ -220,13 +243,19 @@
     def to_slab(x, turn):
         return lax.ppermute(x, "ctx", [(c, c ^ turn) for c in range(slabs)])
 
-    blocks = [grad_out] + [to_chip(grad_out, step) for step in range(1, chips)]
-    (pack,) = call(pack_kernel, [query_proj, key_proj, value_proj], [((rows, 3 * size), half)])
+    blocks = [to_chip(grad_out, step) for step in range(1, chips)]
+    (pack,) = call(
+        pack_kernel, [query_proj, key_proj, value_proj], [((rows, 3 * size), half)],
+        raw=True, sems=3,
+    )
     packs = [pack] + [to_slab(pack, turn) for turn in range(1, slabs)]
     mate_out = to_mate(w_out)
     own_w = [w_query, w_key, w_value]
     mate_w = [to_mate(w) for w in own_w]
-
+    near_out, near_grad = call(
+        functools.partial(fetch_kernel, 2), [w_out, grad_out],
+        [(w_out.shape, half), (grad_out.shape, half)], raw=True, sems=2,
+    )
     prob_row, prob_col, attn_out = call(
         functools.partial(softmax_kernel, slabs, tile_keys.shape[1]),
         [tile_keys, *packs],
@@ -234,7 +263,7 @@
     )
     own_part, mate_part = call(
         functools.partial(attn_grad_kernel, chips, cols),
-        [*blocks, w_out, mate_out],
+        [near_grad, *blocks, near_out, mate_out],
         [((rows, size), full), ((rows, size), full)],
     )
     grad = (own_part + to_mate(mate_part)).astype(half)
@@ -250,6 +279,7 @@
         [((rows, 3 * size), half)],
     )
     mate_grads = to_mate(own_grads)
+
     arrived = []
     for step in hops + [0]:
         (part,) = call(
@@ -266,8 +296,7 @@
 def solution(mesh):
     slabs, shards = mesh.shape["ctx"], mesh.shape["tp"]
     chips = shards // 2
-    few = 1 < slabs <= 8 and slabs & (slabs - 1) == 0
-    few = few and shards == 2 * chips and 2 <= chips <= 8 and chips & (chips - 1) == 0
+    few = slabs in (4, 8) and shards == 2 * chips and chips in (2, 4, 8)
     return jax.shard_map(
         functools.partial(few_slabs, slabs, chips) if few else many_slabs,
         mesh=mesh,

time: 66.5 us -> 68.1 us (1.024)
  local copies, waits for them, and re-layouts: 4.52 us -> 0.02 us
  waiting for transfers between devices: 30.4 us -> 33.2 us
  Pallas kernels: 5.94 us -> 8.08 us
  starting transfers between devices: 25.1 us -> 26.3 us
    unnamed x18 -> x8, local copies, waits for them, and re-layouts: 4.52 us -> 0.02 us
    ppermute x6, waiting for transfers between devices: 24.2 us -> 28.6 us  [to_chip(): return lax.ppermute(x, 'tp', [(t, t ^ 2 * step) for t in range(2 * chips)])]
    ppermute x6, starting transfers between devices: 9.04 us -> 11.4 us  [to_slab(): return lax.ppermute(x, 'ctx', [(c, c ^ turn) for c in range(slabs)])]
    pallas_call x10 -> x11, Pallas kernels: 5.94 us -> 8.08 us  [call(): pl.pallas_call(kernel, in_specs=[SMEM if flag else there for flag in ints...]
    ppermute x6, waiting for transfers between devices: 4.85 us -> 3.32 us  [to_slab(): return lax.ppermute(x, 'ctx', [(c, c ^ turn) for c in range(slabs)])]
    ppermute x6, starting transfers between devices: 14.9 us -> 13.8 us  [to_chip(): return lax.ppermute(x, 'tp', [(t, t ^ 2 * step) for t in range(2 * chips)])]
  transfers between devices with their start and end apart: 18 -> 18, of which waited for: 11 -> 10; matrix products, arithmetic and copies ran while one was open for 0% -> 0% of each run, Pallas kernels for 7% -> 10%
where the time goes in v2:
time: 68.1 us; the launch traced here: 67.9 us
  waiting for transfers between devices  33.2 us (49%)
  starting transfers between devices  26.3 us (39%)
  Pallas kernels  8.08 us (12%)
    ppermute x6, waiting for transfers between devices, to_chip(): return lax.ppermute(x, 'tp', [(t, t ^ 2 * step) for t in range(2 * chips)])  28.6 us
    ppermute x6, starting transfers between devices, to_chip(): return lax.ppermute(x, 'tp', [(t, t ^ 2 * step) for t in range(2 * chips)])  13.8 us
    ppermute x6, starting transfers between devices, to_slab(): return lax.ppermute(x, 'ctx', [(c, c ^ turn) for c in range(slabs)])  11.4 us
    pallas_call x11, Pallas kernels, call(): pl.pallas_call(kernel, in_specs=[SMEM if flag else there for flag in ints...  8.08 us
    ppermute x6, waiting for transfers between devices, to_slab(): return lax.ppermute(x, 'ctx', [(c, c ^ turn) for c in range(slabs)])  3.32 us
  transfers between devices with their start and end apart: 18, of which 10 were waited for; matrix products, arithmetic and copies ran while one was open for 0% of the time, Pallas kernels for 10%

profile of v2, /device:TPU:0, one launch (start us, length us, event | category | flops | bytes accessed | tf_op | source)
XLA Modules:
  0.0 67.9 jit_solution(12653438221031692832)
XLA Ops:
  0.0 0.5 collective-permute-start.3
  0.5 0.0 collective-permute-start.12
  0.5 0.5 collective-permute-start.13
  1.0 0.0 collective-permute-start.14
  1.0 3.1 %collective-permute-start = (bf16[128,640]{1,0:T(8,128)(2,1)}, bf16[128,640]{1,0:T(8,128)(2,1)S(1)}, u32[]{:S(2)}, u32[]{:S(2)}) collective-permute-start(bf16[128,640]{1,0:T(8,128)(2,1)} %refs_1_.5), channel_id=1, source_target_pairs={{0,2},{1,3},{2,0},{3,1},{4,6},{5,7},{6,4},{7,5},{8,10},{9,11},{10,... | collective-permute-start | bytes 491528 | tf_op jit(solution)/shard_map/ppermute | solution.py:238
  4.1 4.6 %collective-permute-done.refs_1_ = bf16[128,640]{1,0:T(8,128)(2,1)S(1)} collective-permute-done((bf16[128,640]{1,0:T(8,128)(2,1)}, bf16[128,640]{1,0:T(8,128)(2,1)S(1)}, u32[]{:S(2)}, u32[]{:S(2)}) %collective-permute-start) | collective-permute-done | bytes 163872 | tf_op jit(solution)/shard_map/ppermute | solution.py:238
  8.7 2.8 %collective-permute-start.1 = (bf16[128,640]{1,0:T(8,128)(2,1)}, bf16[128,640]{1,0:T(8,128)(2,1)S(1)}, u32[]{:S(2)}, u32[]{:S(2)}) collective-permute-start(bf16[128,640]{1,0:T(8,128)(2,1)} %refs_1_.5), channel_id=1, source_target_pairs={{0,4},{1,5},{2,6},{3,7},{4,0},{5,1},{6,2},{7,3},{8,12},{9,13},{10,... | collective-permute-start | bytes 491528 | tf_op jit(solution)/shard_map/ppermute | solution.py:238
  11.4 7.4 %collective-permute-done.1.refs_2_ = bf16[128,640]{1,0:T(8,128)(2,1)S(1)} collective-permute-done((bf16[128,640]{1,0:T(8,128)(2,1)}, bf16[128,640]{1,0:T(8,128)(2,1)S(1)}, u32[]{:S(2)}, u32[]{:S(2)}) %collective-permute-start.1) | collective-permute-done | bytes 163872 | tf_op jit(solution)/shard_map/ppermute | solution.py:238
  18.8 3.4 %collective-permute-start.2 = (bf16[128,640]{1,0:T(8,128)(2,1)}, bf16[128,640]{1,0:T(8,128)(2,1)S(1)}, u32[]{:S(2)}, u32[]{:S(2)}) collective-permute-start(bf16[128,640]{1,0:T(8,128)(2,1)} %refs_1_.5), channel_id=1, source_target_pairs={{0,6},{1,7},{2,4},{3,5},{4,2},{5,3},{6,0},{7,1},{8,14},{9,15},{10,... | collective-permute-start | bytes 491528 | tf_op jit(solution)/shard_map/ppermute | solution.py:238
  22.2 0.8 %shard_map.93.refs_0_.refs_4_ = bf16[128,384]{1,0:T(8,128)(2,1)S(1)} custom-call(bf16[128,128]{1,0:T(8,128)(2,1)} %query_ref.1, bf16[128,128]{1,0:T(8,128)(2,1)} %key_ref.1, bf16[128,128]{1,0:T(8,128)(2,1)} %value_ref.1), custom_call_target="tpu_custom_call" | custom-call | tf_op jit(solution)/shard_map/pallas_call | solution.py:206
  23.0 3.9 %collective-permute-done.2.refs_3_ = bf16[128,640]{1,0:T(8,128)(2,1)S(1)} collective-permute-done((bf16[128,640]{1,0:T(8,128)(2,1)}, bf16[128,640]{1,0:T(8,128)(2,1)S(1)}, u32[]{:S(2)}, u32[]{:S(2)}) %collective-permute-start.2) | collective-permute-done | bytes 163872 | tf_op jit(solution)/shard_map/ppermute | solution.py:238
  26.9 2.4 %collective-permute-start.10 = (bf16[128,384]{1,0:T(8,128)(2,1)S(1)}, bf16[128,384]{1,0:T(8,128)(2,1)S(1)}, u32[]{:S(2)}, u32[]{:S(2)}) collective-permute-start(bf16[128,384]{1,0:T(8,128)(2,1)S(1)} %shard_map.93.refs_0_.refs_4_), channel_id=1, source_target_pairs={{0,24},{8,16},{16,8},{24,0},{1,25},{9,17},{17,9},{25,1},{2,26},{10... | collective-permute-start | bytes 294920 | tf_op jit(solution)/shard_map/ppermute | solution.py:244
  29.3 1.3 %shard_map.91 = (bf16[128,5120]{1,0:T(8,128)(2,1)S(1)}, bf16[128,640]{1,0:T(8,128)(2,1)S(1)}) custom-call(bf16[128,5120]{1,0:T(8,128)(2,1)} %refs_0_.5, bf16[128,640]{1,0:T(8,128)(2,1)} %refs_1_.5), custom_call_target="tpu_custom_call" | custom-call | tf_op jit(solution)/shard_map/pallas_call | solution.py:206
  30.7 0.0 collective-permute-done.3.refs_5_
  30.7 0.0 copy-start.3
  30.7 0.0 copy-start.2
  30.7 0.6 shard_map.92
  31.3 0.1 collective-permute-start.4
  31.4 1.0 %collective-permute-done.10.refs_3_.refs_7_ = bf16[128,384]{1,0:T(8,128)(2,1)S(1)} collective-permute-done((bf16[128,384]{1,0:T(8,128)(2,1)S(1)}, bf16[128,384]{1,0:T(8,128)(2,1)S(1)}, u32[]{:S(2)}, u32[]{:S(2)}) %collective-permute-start.10) | collective-permute-done | bytes 98336 | tf_op jit(solution)/shard_map/ppermute | solution.py:244
  32.4 1.5 %collective-permute-start.8 = (bf16[128,384]{1,0:T(8,128)(2,1)S(1)}, bf16[128,384]{1,0:T(8,128)(2,1)S(1)}, u32[]{:S(2)}, u32[]{:S(2)}) collective-permute-start(bf16[128,384]{1,0:T(8,128)(2,1)S(1)} %shard_map.93.refs_0_.refs_4_), channel_id=1, source_target_pairs={{0,8},{8,0},{16,24},{24,16},{1,9},{9,1},{17,25},{25,17},{2,10},{10... | collective-permute-start | bytes 294920 | tf_op jit(solution)/shard_map/ppermute | solution.py:244
  33.9 0.0 collective-permute-done.4
  33.9 1.5 %collective-permute-start.9 = (bf16[128,384]{1,0:T(8,128)(2,1)S(1)}, bf16[128,384]{1,0:T(8,128)(2,1)S(1)}, u32[]{:S(2)}, u32[]{:S(2)}) collective-permute-start(bf16[128,384]{1,0:T(8,128)(2,1)S(1)} %shard_map.93.refs_0_.refs_4_), channel_id=1, source_target_pairs={{0,16},{8,24},{16,0},{24,8},{1,17},{9,25},{17,1},{25,9},{2,18},{10... | collective-permute-start | bytes 294920 | tf_op jit(solution)/shard_map/ppermute | solution.py:244
  35.4 0.0 copy-start.1
  35.4 0.0 copy-start
  35.4 1.6 %collective-permute-done.8.refs_1_.refs_5_ = bf16[128,384]{1,0:T(8,128)(2,1)S(1)} collective-permute-done((bf16[128,384]{1,0:T(8,128)(2,1)S(1)}, bf16[128,384]{1,0:T(8,128)(2,1)S(1)}, u32[]{:S(2)}, u32[]{:S(2)}) %collective-permute-start.8) | collective-permute-done | bytes 98336 | tf_op jit(solution)/shard_map/ppermute | solution.py:244
  37.0 1.5 %collective-permute-start.5 = (bf16[128,128]{1,0:T(8,128)(2,1)S(1)}, bf16[128,128]{1,0:T(8,128)(2,1)S(1)}, u32[]{:S(2)}, u32[]{:S(2)}) collective-permute-start(bf16[128,128]{1,0:T(8,128)(2,1)S(1)} %add_convert_fusion.grad_ref.refs_0_), channel_id=1, source_target_pairs={{0,8},{8,0},{16,24},{24,16},{1,9},{9,1},{17,25},{25,17},{2,10},{10... | collective-permute-start | bytes 98312 | tf_op jit(solution)/shard_map/ppermute | solution.py:244
  38.5 0.0 collective-permute-done.9.refs_2_.refs_6_
  38.5 1.9 %collective-permute-start.6 = (bf16[128,128]{1,0:T(8,128)(2,1)S(1)}, bf16[128,128]{1,0:T(8,128)(2,1)S(1)}, u32[]{:S(2)}, u32[]{:S(2)}) collective-permute-start(bf16[128,128]{1,0:T(8,128)(2,1)S(1)} %add_convert_fusion.grad_ref.refs_0_), channel_id=1, source_target_pairs={{0,16},{8,24},{16,0},{24,8},{1,17},{9,25},{17,1},{25,9},{2,18},{10... | collective-permute-start | bytes 98312 | tf_op jit(solution)/shard_map/ppermute | solution.py:244
  40.4 0.7 %collective-permute-done.5.refs_1_ = bf16[128,128]{1,0:T(8,128)(2,1)S(1)} collective-permute-done((bf16[128,128]{1,0:T(8,128)(2,1)S(1)}, bf16[128,128]{1,0:T(8,128)(2,1)S(1)}, u32[]{:S(2)}, u32[]{:S(2)}) %collective-permute-start.5) | collective-permute-done | bytes 32800 | tf_op jit(solution)/shard_map/ppermute | solution.py:244
  41.1 2.6 %collective-permute-start.7 = (bf16[128,128]{1,0:T(8,128)(2,1)S(1)}, bf16[128,128]{1,0:T(8,128)(2,1)S(1)}, u32[]{:S(2)}, u32[]{:S(2)}) collective-permute-start(bf16[128,128]{1,0:T(8,128)(2,1)S(1)} %add_convert_fusion.grad_ref.refs_0_), channel_id=1, source_target_pairs={{0,24},{8,16},{16,8},{24,0},{1,25},{9,17},{17,9},{25,1},{2,26},{10... | collective-permute-start | bytes 98312 | tf_op jit(solution)/shard_map/ppermute | solution.py:244
  43.7 0.0 copy-done.3
  43.7 2.1 %shard_map.94 = (f32[128,512]{1,0:T(8,128)S(1)}, f32[512,128]{1,0:T(8,128)S(1)}, f32[512,128]{1,0:T(8,128)S(1)}) custom-call(s32[4,3]{1,0:T(4,128)S(1)} %copy-done.3, bf16[128,384]{1,0:T(8,128)(2,1)S(1)} %shard_map.93.refs_0_.refs_4_, bf16[128,384]{1,0:T(8,128)(2,1)S(1)} %collective-permute-done.8.refs_1_.refs_5_, ...), custom_call_target="tpu_custom_call" | custom-call | tf_op jit(solution)/shard_map/pallas_call | solution.py:206
  45.8 0.3 shard_map.95.refs_8_
  46.1 0.0 collective-permute-done.6.refs_2_
  46.2 0.0 collective-permute-done.7.refs_3_
  46.2 0.5 shard_map.96.own_ref
  46.6 0.1 collective-permute-start.11
  46.7 0.0 collective-permute-done.12.refs_3_
  46.7 0.0 collective-permute-done.13.refs_4_
  46.7 0.0 collective-permute-done.14.refs_5_
  46.7 1.3 %collective-permute-done.11.mate_ref = bf16[128,384]{1,0:T(8,128)(2,1)S(1)} collective-permute-done((bf16[128,384]{1,0:T(8,128)(2,1)S(1)}, bf16[128,384]{1,0:T(8,128)(2,1)S(1)}, u32[]{:S(2)}, u32[]{:S(2)}) %collective-permute-start.11) | collective-permute-done | bytes 98336 | tf_op jit(solution)/shard_map/ppermute | solution.py:241
  48.0 0.0 copy-done.2
  48.0 0.0 copy-done.1
  48.0 0.0 copy-done
  48.0 0.4 shard_map.100
  48.4 3.5 %collective-permute-start.17 = (bf16[640,128]{1,0:T(8,128)(2,1)S(1)}, bf16[640,128]{1,0:T(8,128)(2,1)S(1)}, u32[]{:S(2)}, u32[]{:S(2)}) collective-permute-start(bf16[640,128]{1,0:T(8,128)(2,1)S(1)} %shard_map.100), channel_id=1, source_target_pairs={{0,6},{1,7},{2,4},{3,5},{4,2},{5,3},{6,0},{7,1},{8,14},{9,15},{10,... | collective-permute-start | bytes 491528 | tf_op jit(solution)/shard_map/ppermute | solution.py:238
  51.9 0.4 shard_map.99
  52.4 0.1 collective-permute-start.16
  52.4 0.4 shard_map.98
  52.9 1.0 %collective-permute-start.15 = (bf16[640,128]{1,0:T(8,128)(2,1)S(1)}, bf16[640,128]{1,0:T(8,128)(2,1)S(1)}, u32[]{:S(2)}, u32[]{:S(2)}) collective-permute-start(bf16[640,128]{1,0:T(8,128)(2,1)S(1)} %shard_map.98), channel_id=1, source_target_pairs={{0,4},{1,5},{2,6},{3,7},{4,0},{5,1},{6,2},{7,3},{8,12},{9,13},{10,... | collective-permute-start | bytes 491528 | tf_op jit(solution)/shard_map/ppermute | solution.py:238
  53.9 0.4 shard_map.97.own_ref
  54.3 3.1 %collective-permute-done.17.refs_2_ = bf16[640,128]{1,0:T(8,128)(2,1)S(1)} collective-permute-done((bf16[640,128]{1,0:T(8,128)(2,1)S(1)}, bf16[640,128]{1,0:T(8,128)(2,1)S(1)}, u32[]{:S(2)}, u32[]{:S(2)}) %collective-permute-start.17) | collective-permute-done | bytes 163872 | tf_op jit(solution)/shard_map/ppermute | solution.py:238
  57.4 2.7 %collective-permute-done.16.refs_1_ = bf16[640,128]{1,0:T(8,128)(2,1)S(1)} collective-permute-done((bf16[640,128]{1,0:T(8,128)(2,1)S(1)}, bf16[640,128]{1,0:T(8,128)(2,1)S(1)}, u32[]{:S(2)}, u32[]{:S(2)}) %collective-permute-start.16) | collective-permute-done | bytes 163872 | tf_op jit(solution)/shard_map/ppermute | solution.py:238
  60.2 6.9 %collective-permute-done.15.refs_0_ = bf16[640,128]{1,0:T(8,128)(2,1)S(1)} collective-permute-done((bf16[640,128]{1,0:T(8,128)(2,1)S(1)}, bf16[640,128]{1,0:T(8,128)(2,1)S(1)}, u32[]{:S(2)}, u32[]{:S(2)}) %collective-permute-start.15) | collective-permute-done | bytes 163872 | tf_op jit(solution)/shard_map/ppermute | solution.py:238
  67.1 0.8 %shard_map.101 = f32[640,128]{1,0:T(8,128)} custom-call(f32[640,128]{1,0:T(8,128)S(1)} %shard_map.97.own_ref, bf16[640,128]{1,0:T(8,128)(2,1)S(1)} %collective-permute-done.15.refs_0_, bf16[640,128]{1,0:T(8,128)(2,1)S(1)} %collective-permute-done.16.refs_1_, bf16[640,128]{1,0:T(8,128)(2,1)S(1)} %collective-permute-done.17.refs_2_), custom_call_target="tpu_custom_call" | custom-call | tf_op jit(solution)/shard_map/pallas_call | solution.py:206
  (1 shorter events, 0.0 us)
Async XLA Ops:
  0.0 30.7 %collective-permute-start.3 = (bf16[128,5120]{1,0:T(8,128)(2,1)}, bf16[128,5120]{1,0:T(8,128)(2,1)S(1)}, u32[]{:S(2)}, u32[]{:S(2)}) collective-permute-start(bf16[128,5120]{1,0:T(8,128)(2,1)} %refs_0_.5), channel_id=1, source_target_pairs={{0,1},{1,0},{2,3},{3,2},{4,5},{5,4},{6,7},{7,6},{8,9},{9,8},{10,11... | collective-permute-start | bytes 3932168 | tf_op jit(solution)/shard_map/ppermute | solution.py:241
  0.5 46.2 %collective-permute-start.12 = (bf16[5120,128]{1,0:T(8,128)(2,1)}, bf16[5120,128]{1,0:T(8,128)(2,1)S(1)}, u32[]{:S(2)}, u32[]{:S(2)}) collective-permute-start(bf16[5120,128]{1,0:T(8,128)(2,1)} %refs_0_.9), channel_id=1, source_target_pairs={{0,1},{1,0},{2,3},{3,2},{4,5},{5,4},{6,7},{7,6},{8,9},{9,8},{10,11... | collective-permute-start | bytes 3932168 | tf_op jit(solution)/shard_map/ppermute | solution.py:241
  0.5 46.2 %collective-permute-start.13 = (bf16[5120,128]{1,0:T(8,128)(2,1)}, bf16[5120,128]{1,0:T(8,128)(2,1)S(1)}, u32[]{:S(2)}, u32[]{:S(2)}) collective-permute-start(bf16[5120,128]{1,0:T(8,128)(2,1)} %refs_1_.9), channel_id=1, source_target_pairs={{0,1},{1,0},{2,3},{3,2},{4,5},{5,4},{6,7},{7,6},{8,9},{9,8},{10,11... | collective-permute-start | bytes 3932168 | tf_op jit(solution)/shard_map/ppermute | solution.py:241
  1.0 45.7 %collective-permute-start.14 = (bf16[5120,128]{1,0:T(8,128)(2,1)}, bf16[5120,128]{1,0:T(8,128)(2,1)S(1)}, u32[]{:S(2)}, u32[]{:S(2)}) collective-permute-start(bf16[5120,128]{1,0:T(8,128)(2,1)} %refs_2_.7), channel_id=1, source_target_pairs={{0,1},{1,0},{2,3},{3,2},{4,5},{5,4},{6,7},{7,6},{8,9},{9,8},{10,11... | collective-permute-start | bytes 3932168 | tf_op jit(solution)/shard_map/ppermute | solution.py:241
  1.0 7.6 %collective-permute-start = (bf16[128,640]{1,0:T(8,128)(2,1)}, bf16[128,640]{1,0:T(8,128)(2,1)S(1)}, u32[]{:S(2)}, u32[]{:S(2)}) collective-permute-start(bf16[128,640]{1,0:T(8,128)(2,1)} %refs_1_.5), channel_id=1, source_target_pairs={{0,2},{1,3},{2,0},{3,1},{4,6},{5,7},{6,4},{7,5},{8,10},{9,11},{10,... | collective-permute-start | bytes 491528 | tf_op jit(solution)/shard_map/ppermute | solution.py:238
  8.7 10.1 %collective-permute-start.1 = (bf16[128,640]{1,0:T(8,128)(2,1)}, bf16[128,640]{1,0:T(8,128)(2,1)S(1)}, u32[]{:S(2)}, u32[]{:S(2)}) collective-permute-start(bf16[128,640]{1,0:T(8,128)(2,1)} %refs_1_.5), channel_id=1, source_target_pairs={{0,4},{1,5},{2,6},{3,7},{4,0},{5,1},{6,2},{7,3},{8,12},{9,13},{10,... | collective-permute-start | bytes 491528 | tf_op jit(solution)/shard_map/ppermute | solution.py:238
  18.8 8.1 %collective-permute-start.2 = (bf16[128,640]{1,0:T(8,128)(2,1)}, bf16[128,640]{1,0:T(8,128)(2,1)S(1)}, u32[]{:S(2)}, u32[]{:S(2)}) collective-permute-start(bf16[128,640]{1,0:T(8,128)(2,1)} %refs_1_.5), channel_id=1, source_target_pairs={{0,6},{1,7},{2,4},{3,5},{4,2},{5,3},{6,0},{7,1},{8,14},{9,15},{10,... | collective-permute-start | bytes 491528 | tf_op jit(solution)/shard_map/ppermute | solution.py:238
  26.9 5.5 %collective-permute-start.10 = (bf16[128,384]{1,0:T(8,128)(2,1)S(1)}, bf16[128,384]{1,0:T(8,128)(2,1)S(1)}, u32[]{:S(2)}, u32[]{:S(2)}) collective-permute-start(bf16[128,384]{1,0:T(8,128)(2,1)S(1)} %shard_map.93.refs_0_.refs_4_), channel_id=1, source_target_pairs={{0,24},{8,16},{16,8},{24,0},{1,25},{9,17},{17,9},{25,1},{2,26},{10... | collective-permute-start | bytes 294920 | tf_op jit(solution)/shard_map/ppermute | solution.py:244
  30.7 13.0 %copy-start.3 = (s32[4,3]{1,0:T(4,128)S(1)}, s32[4,3]{1,0:T(4,128)}, u32[]{:S(2)}) copy-start(s32[4,3]{1,0:T(4,128)} %lists_ref.1) | copy-start | bytes 148
  30.7 17.3 %copy-start.2 = (bf16[5120,128]{1,0:T(8,128)(2,1)S(1)}, bf16[5120,128]{1,0:T(8,128)(2,1)}, u32[]{:S(2)}) copy-start(bf16[5120,128]{1,0:T(8,128)(2,1)} %refs_2_.7) | copy-start | bytes 3932164
  31.3 2.6 %collective-permute-start.4 = (f32[128,128]{1,0:T(8,128)S(1)}, f32[128,128]{1,0:T(8,128)S(1)}, u32[]{:S(2)}, u32[]{:S(2)}) collective-permute-start(f32[128,128]{1,0:T(8,128)S(1)} %get-tuple-element.15), channel_id=1, source_target_pairs={{0,1},{1,0},{2,3},{3,2},{4,5},{5,4},{6,7},{7,6},{8,9},{9,8},{10,11... | collective-permute-start | bytes 196616 | tf_op jit(solution)/shard_map/ppermute | solution.py:241
  32.4 4.6 %collective-permute-start.8 = (bf16[128,384]{1,0:T(8,128)(2,1)S(1)}, bf16[128,384]{1,0:T(8,128)(2,1)S(1)}, u32[]{:S(2)}, u32[]{:S(2)}) collective-permute-start(bf16[128,384]{1,0:T(8,128)(2,1)S(1)} %shard_map.93.refs_0_.refs_4_), channel_id=1, source_target_pairs={{0,8},{8,0},{16,24},{24,16},{1,9},{9,1},{17,25},{25,17},{2,10},{10... | collective-permute-start | bytes 294920 | tf_op jit(solution)/shard_map/ppermute | solution.py:244
  33.9 4.6 %collective-permute-start.9 = (bf16[128,384]{1,0:T(8,128)(2,1)S(1)}, bf16[128,384]{1,0:T(8,128)(2,1)S(1)}, u32[]{:S(2)}, u32[]{:S(2)}) collective-permute-start(bf16[128,384]{1,0:T(8,128)(2,1)S(1)} %shard_map.93.refs_0_.refs_4_), channel_id=1, source_target_pairs={{0,16},{8,24},{16,0},{24,8},{1,17},{9,25},{17,1},{25,9},{2,18},{10... | collective-permute-start | bytes 294920 | tf_op jit(solution)/shard_map/ppermute | solution.py:244
  35.4 12.6 %copy-start.1 = (bf16[5120,128]{1,0:T(8,128)(2,1)S(1)}, bf16[5120,128]{1,0:T(8,128)(2,1)}, u32[]{:S(2)}) copy-start(bf16[5120,128]{1,0:T(8,128)(2,1)} %refs_1_.9) | copy-start | bytes 3932164
  35.4 12.6 %copy-start = (bf16[5120,128]{1,0:T(8,128)(2,1)S(1)}, bf16[5120,128]{1,0:T(8,128)(2,1)}, u32[]{:S(2)}) copy-start(bf16[5120,128]{1,0:T(8,128)(2,1)} %refs_0_.9) | copy-start | bytes 3932164
  37.0 4.1 %collective-permute-start.5 = (bf16[128,128]{1,0:T(8,128)(2,1)S(1)}, bf16[128,128]{1,0:T(8,128)(2,1)S(1)}, u32[]{:S(2)}, u32[]{:S(2)}) collective-permute-start(bf16[128,128]{1,0:T(8,128)(2,1)S(1)} %add_convert_fusion.grad_ref.refs_0_), channel_id=1, source_target_pairs={{0,8},{8,0},{16,24},{24,16},{1,9},{9,1},{17,25},{25,17},{2,10},{10... | collective-permute-start | bytes 98312 | tf_op jit(solution)/shard_map/ppermute | solution.py:244
  38.5 7.6 %collective-permute-start.6 = (bf16[128,128]{1,0:T(8,128)(2,1)S(1)}, bf16[128,128]{1,0:T(8,128)(2,1)S(1)}, u32[]{:S(2)}, u32[]{:S(2)}) collective-permute-start(bf16[128,128]{1,0:T(8,128)(2,1)S(1)} %add_convert_fusion.grad_ref.refs_0_), channel_id=1, source_target_pairs={{0,16},{8,24},{16,0},{24,8},{1,17},{9,25},{17,1},{25,9},{2,18},{10... | collective-permute-start | bytes 98312 | tf_op jit(solution)/shard_map/ppermute | solution.py:244
  41.1 5.1 %collective-permute-start.7 = (bf16[128,128]{1,0:T(8,128)(2,1)S(1)}, bf16[128,128]{1,0:T(8,128)(2,1)S(1)}, u32[]{:S(2)}, u32[]{:S(2)}) collective-permute-start(bf16[128,128]{1,0:T(8,128)(2,1)S(1)} %add_convert_fusion.grad_ref.refs_0_), channel_id=1, source_target_pairs={{0,24},{8,16},{16,8},{24,0},{1,25},{9,17},{17,9},{25,1},{2,26},{10... | collective-permute-start | bytes 98312 | tf_op jit(solution)/shard_map/ppermute | solution.py:244
  46.6 1.4 %collective-permute-start.11 = (bf16[128,384]{1,0:T(8,128)(2,1)S(1)}, bf16[128,384]{1,0:T(8,128)(2,1)S(1)}, u32[]{:S(2)}, u32[]{:S(2)}) collective-permute-start(bf16[128,384]{1,0:T(8,128)(2,1)S(1)} %shard_map.96.own_ref), channel_id=1, source_target_pairs={{0,1},{1,0},{2,3},{3,2},{4,5},{5,4},{6,7},{7,6},{8,9},{9,8},{10,11... | collective-permute-start | bytes 294920 | tf_op jit(solution)/shard_map/ppermute | solution.py:241
  48.4 9.0 %collective-permute-start.17 = (bf16[640,128]{1,0:T(8,128)(2,1)S(1)}, bf16[640,128]{1,0:T(8,128)(2,1)S(1)}, u32[]{:S(2)}, u32[]{:S(2)}) collective-permute-start(bf16[640,128]{1,0:T(8,128)(2,1)S(1)} %shard_map.100), channel_id=1, source_target_pairs={{0,6},{1,7},{2,4},{3,5},{4,2},{5,3},{6,0},{7,1},{8,14},{9,15},{10,... | collective-permute-start | bytes 491528 | tf_op jit(solution)/shard_map/ppermute | solution.py:238
  52.4 7.8 %collective-permute-start.16 = (bf16[640,128]{1,0:T(8,128)(2,1)S(1)}, bf16[640,128]{1,0:T(8,128)(2,1)S(1)}, u32[]{:S(2)}, u32[]{:S(2)}) collective-permute-start(bf16[640,128]{1,0:T(8,128)(2,1)S(1)} %shard_map.99), channel_id=1, source_target_pairs={{0,2},{1,3},{2,0},{3,1},{4,6},{5,7},{6,4},{7,5},{8,10},{9,11},{10,... | collective-permute-start | bytes 491528 | tf_op jit(solution)/shard_map/ppermute | solution.py:238
  52.9 14.2 %collective-permute-start.15 = (bf16[640,128]{1,0:T(8,128)(2,1)S(1)}, bf16[640,128]{1,0:T(8,128)(2,1)S(1)}, u32[]{:S(2)}, u32[]{:S(2)}) collective-permute-start(bf16[640,128]{1,0:T(8,128)(2,1)S(1)} %shard_map.98), channel_id=1, source_target_pairs={{0,4},{1,5},{2,6},{3,7},{4,0},{5,1},{6,2},{7,3},{8,12},{9,13},{10,... | collective-permute-start | bytes 491528 | tf_op jit(solution)/shard_map/ppermute | solution.py:238

commit v3 on v1

--- a/solution.py
+++ b/solution.py
@@ -78,31 +78,26 @@
         copy.wait()
 
 
-def fetch_kernel(count, *refs):
-    sems = refs[2 * count]
-    copies = [
-        pltpu.make_async_copy(refs[place], refs[count + place], sems.at[place])
-        for place in range(count)
-    ]
+def split_kernel(whole_ref, *refs):
+    outs, sems = refs[:-1], refs[-1]
+    copies, start = [], 0
+    for place, out in enumerate(outs):
+        span = pl.ds(start, out.shape[0])
+        copies.append(pltpu.make_async_copy(whole_ref.at[span], out, sems.at[place]))
+        start += out.shape[0]
     for copy in copies:
         copy.start()
     for copy in copies:
         copy.wait()
 
 
-def is_inner():
-    chip = lax.axis_index("tp") >> 1
-    return (chip == 1) | (chip == 2)
-
-
-def attn_grad_kernel(cols, own_block, near, cross_in, cross_out, mid, relay, own_w, mate_w, own_ref, mate_ref):
+def attn_grad_kernel(cols, top, low, near, top2, low2, top3, low3, own_w, mate_w, own_ref, mate_ref):
     index = lax.axis_index("tp")
-    inner = is_inner()
     blocks = [
-        own_block[...],
+        jnp.concatenate([top[...], low[...]], axis=0),
         near[...],
-        jnp.where(inner, cross_in[...], cross_out[...]),
-        jnp.where(inner, mid[...], relay[...]),
+        jnp.concatenate([top2[...], low2[...]], axis=0),
+        jnp.concatenate([top3[...], low3[...]], axis=0),
     ]
     own = jnp.zeros(own_ref.shape, jnp.float32)
     mate = jnp.zeros(own_ref.shape, jnp.float32)
@@ -183,9 +178,10 @@
     )
 
 
-def project_kernel(rows, step, own_ref, mate_ref, *refs):
+def project_kernel(block, step, first, own_ref, mate_ref, *refs):
     weights, out_ref = refs[:6], refs[-1]
-    start = pl.multiple_of((lax.axis_index("tp") ^ (2 * step)) * rows, 16)
+    rows = out_ref.shape[0]
+    start = pl.multiple_of((lax.axis_index("tp") ^ (2 * step)) * block + first, 16)
     size = own_ref.shape[1] // 3
     total = None
     for place, weight in enumerate(weights):
@@ -198,11 +194,12 @@
     out_ref[...] = total.astype(out_ref.dtype)
 
 
-def sum_kernel(own_ref, near, cross_in, cross_out, mid, out_ref):
+def sum_kernel(own_ref, near, top2, low2, low3, out_ref):
     full = jnp.float32
-    total = own_ref[...] + near[...].astype(full)
-    through = cross_in[...].astype(full) + mid[...].astype(full)
-    out_ref[...] = total + jnp.where(is_inner(), through, cross_out[...].astype(full))
+    cut = top2.shape[0]
+    out_ref[:cut, :] = own_ref[:cut, :] + near[:cut, :].astype(full) + top2[...].astype(full)
+    low = low2[...].astype(full) + low3[...].astype(full)
+    out_ref[cut:, :] = own_ref[cut:, :] + near[cut:, :].astype(full) + low
 
 
 def call(kernel, args, outs, fast_out=True, raw=False, sems=0):
@@ -225,14 +222,6 @@
     )(*args)
 
 
-FEED = ((0, 1), (3, 2))
-RELAY = ((2, 3), (1, 0))
-CROSS_IN = ((0, 2), (3, 1))
-CROSS_OUT = ((2, 0), (1, 3))
-MID = ((1, 2), (2, 1))
-NEAR = ((0, 1), (1, 0), (2, 3), (3, 2))
-
-
 def few_slabs(
     slabs,
     grad_out,
@@ -248,10 +237,10 @@
     rows, cols = grad_out.shape
     size = query_proj.shape[1]
     half, full = jnp.bfloat16, jnp.float32
-
-    def along(x, way):
-        pairs = [(2 * a + core, 2 * b + core) for a, b in way for core in range(2)]
-        return lax.ppermute(x, "tp", pairs)
+    cut, feature_cut = rows // 2, cols // 2
+
+    def to_chip(x, step):
+        return lax.ppermute(x, "tp", [(t, t ^ (2 * step)) for t in range(8)])
 
     def to_mate(x):
         return lax.ppermute(x, "tp", [(t, t ^ 1) for t in range(8)])
@@ -259,11 +248,15 @@
     def to_slab(x, turn):
         return lax.ppermute(x, "ctx", [(c, c ^ turn) for c in range(slabs)])
 
-    g_in = along(grad_out, CROSS_IN)
-    g_near = along(grad_out, NEAR)
-    g_out = along(grad_out, CROSS_OUT)
-    g_mid = along(grad_out, MID)
-    g_relay = along(g_in, RELAY)
+    top, low = call(
+        split_kernel, [grad_out], [((cut, cols), half), ((rows - cut, cols), half)],
+        raw=True, sems=2,
+    )
+    top2 = to_chip(top, 2)
+    near = to_chip(grad_out, 1)
+    low2 = to_chip(low, 2)
+    low3 = to_chip(low, 3)
+    top3 = to_chip(top2, 1)
     (pack,) = call(
         pack_kernel, [query_proj, key_proj, value_proj], [((rows, 3 * size), half)],
         raw=True, sems=3,
@@ -272,10 +265,7 @@
     mate_out = to_mate(w_out)
     own_w = [w_query, w_key, w_value]
     mate_w = [to_mate(w) for w in own_w]
-    near_out, near_grad = call(
-        functools.partial(fetch_kernel, 2), [w_out, grad_out],
-        [(w_out.shape, half), (grad_out.shape, half)], raw=True, sems=2,
-    )
+    (near_out,) = call(split_kernel, [w_out], [(w_out.shape, half)], raw=True, sems=1)
     prob_row, prob_col, attn_out = call(
         functools.partial(softmax_kernel, slabs, tile_keys.shape[1]),
         [tile_keys, *packs],
@@ -283,7 +273,7 @@
     )
     own_part, mate_part = call(
         functools.partial(attn_grad_kernel, cols),
-        [near_grad, g_near, g_in, g_out, g_mid, g_relay, near_out, mate_out],
+        [top, low, near, top2, low2, top3, low3, near_out, mate_out],
         [((rows, size), full), ((rows, size), full)],
     )
     grad = (own_part + to_mate(mate_part)).astype(half)
@@ -300,23 +290,24 @@
     )
     mate_grads = to_mate(own_grads)
 
-    def project(step, kind, *fed):
+
+    def project(step, first, count, kind, *fed):
         (part,) = call(
-            functools.partial(project_kernel, cols, step),
+            functools.partial(project_kernel, cols, step, first),
             [own_grads, mate_grads, *own_w, *mate_w, *fed],
-            [((cols, rows), kind)],
+            [((count, rows), kind)],
         )
         return part
 
-    third, second = project(3, half), project(2, half)
-    fed = along(third, FEED)
-    f_in = along(second, CROSS_IN)
-    f_mid = along(third, MID)
-    f_near = along(project(1, half), NEAR)
-    f_out = along(project(2, half, fed), CROSS_OUT)
+    rest = cols - feature_cut
+    fed = to_chip(project(3, 0, feature_cut, half), 1)
+    low3 = to_chip(project(3, feature_cut, rest, half), 3)
+    low2 = to_chip(project(2, feature_cut, rest, half), 2)
+    near = to_chip(project(1, 0, cols, half), 1)
+    top2 = to_chip(project(2, 0, feature_cut, half, fed), 2)
     (out,) = call(
         sum_kernel,
-        [project(0, full), f_near, f_in, f_out, f_mid],
+        [project(0, 0, cols, full), near, top2, low2, low3],
         [((cols, rows), full)],
         fast_out=False,
     )

time: 75.8 us -> 72.7 us (0.959)
  starting transfers between devices: 28.3 us -> 25.7 us
  waiting for transfers between devices: 38.2 us -> 37.3 us
  Pallas kernels: 8.55 us -> 9.31 us
    ppermute x10, starting transfers between devices: 18.9 us -> 14.1 us  [to_chip(): return lax.ppermute(x, 'tp', [(t, t ^ 2 * step) for t in range(8)])]
    ppermute x6, waiting for transfers between devices: 6.35 us -> 4.11 us  [to_slab(): return lax.ppermute(x, 'ctx', [(c, c ^ turn) for c in range(slabs)])]
    ppermute x6, starting transfers between devices: 8.23 us -> 10.4 us  [to_slab(): return lax.ppermute(x, 'ctx', [(c, c ^ turn) for c in range(slabs)])]
    ppermute x10, waiting for transfers between devices: 30.6 us -> 31.9 us  [to_chip(): return lax.ppermute(x, 'tp', [(t, t ^ 2 * step) for t in range(8)])]
    pallas_call x12 -> x14, Pallas kernels: 8.55 us -> 9.31 us  [call(): pl.pallas_call(kernel, in_specs=[SMEM if flag else there for flag in ints...]
  transfers between devices with their start and end apart: 22 -> 22, of which waited for: 13 -> 11; matrix products, arithmetic and copies ran while one was open for 0% -> 0% of each run, Pallas kernels for 10% -> 11%
where the time goes in v3:
time: 72.7 us; the launch traced here: 72.5 us
  waiting for transfers between devices  37.3 us (51%)
  starting transfers between devices  25.7 us (35%)
  Pallas kernels  9.31 us (13%)
    ppermute x10, waiting for transfers between devices, to_chip(): return lax.ppermute(x, 'tp', [(t, t ^ 2 * step) for t in range(8)])  31.9 us
    ppermute x10, starting transfers between devices, to_chip(): return lax.ppermute(x, 'tp', [(t, t ^ 2 * step) for t in range(8)])  14.1 us
    ppermute x6, starting transfers between devices, to_slab(): return lax.ppermute(x, 'ctx', [(c, c ^ turn) for c in range(slabs)])  10.4 us
    pallas_call x14, Pallas kernels, call(): pl.pallas_call(kernel, in_specs=[SMEM if flag else there for flag in ints...  9.31 us
    ppermute x6, waiting for transfers between devices, to_slab(): return lax.ppermute(x, 'ctx', [(c, c ^ turn) for c in range(slabs)])  4.11 us
  transfers between devices with their start and end apart: 22, of which 11 were waited for; matrix products, arithmetic and copies ran while one was open for 0% of the time, Pallas kernels for 11%

profile of v3, /device:TPU:0, one launch (start us, length us, event | category | flops | bytes accessed | tf_op | source)
XLA Modules:
  0.0 72.5 jit_solution(15020936852549714829)
XLA Ops:
  0.0 0.5 collective-permute-start.5
  0.5 0.0 collective-permute-start.14
  0.5 0.5 collective-permute-start.15
  1.0 0.0 collective-permute-start.16
  1.0 0.9 %shard_map.91 = (bf16[64,640]{1,0:T(8,128)(2,1)S(1)}, bf16[64,640]{1,0:T(8,128)(2,1)S(1)}) custom-call(bf16[128,640]{1,0:T(8,128)(2,1)} %whole_ref.2), custom_call_target="tpu_custom_call" | custom-call | tf_op jit(solution)/shard_map/pallas_call | solution.py:212
  2.0 4.1 %collective-permute-start.1 = (bf16[64,640]{1,0:T(8,128)(2,1)S(1)}, bf16[64,640]{1,0:T(8,128)(2,1)S(1)}, u32[]{:S(2)}, u32[]{:S(2)}) collective-permute-start(bf16[64,640]{1,0:T(8,128)(2,1)S(1)} %get-tuple-element.12.top), channel_id=1, source_target_pairs={{0,4},{1,5},{2,6},{3,7},{4,0},{5,1},{6,2},{7,3},{8,12},{9,13},{10,... | collective-permute-start | bytes 245768 | tf_op jit(solution)/shard_map/ppermute | solution.py:243
  6.1 4.4 %collective-permute-done.1.top2 = bf16[64,640]{1,0:T(8,128)(2,1)S(1)} collective-permute-done((bf16[64,640]{1,0:T(8,128)(2,1)S(1)}, bf16[64,640]{1,0:T(8,128)(2,1)S(1)}, u32[]{:S(2)}, u32[]{:S(2)}) %collective-permute-start.1) | collective-permute-done | bytes 81952 | tf_op jit(solution)/shard_map/ppermute | solution.py:243
  10.5 3.5 %collective-permute-start.4 = (bf16[64,640]{1,0:T(8,128)(2,1)S(1)}, bf16[64,640]{1,0:T(8,128)(2,1)S(1)}, u32[]{:S(2)}, u32[]{:S(2)}) collective-permute-start(bf16[64,640]{1,0:T(8,128)(2,1)S(1)} %get-tuple-element.13.low), channel_id=1, source_target_pairs={{0,6},{1,7},{2,4},{3,5},{4,2},{5,3},{6,0},{7,1},{8,14},{9,15},{10,... | collective-permute-start | bytes 245768 | tf_op jit(solution)/shard_map/ppermute | solution.py:243
  14.0 2.7 %collective-permute-done.4.low3 = bf16[64,640]{1,0:T(8,128)(2,1)S(1)} collective-permute-done((bf16[64,640]{1,0:T(8,128)(2,1)S(1)}, bf16[64,640]{1,0:T(8,128)(2,1)S(1)}, u32[]{:S(2)}, u32[]{:S(2)}) %collective-permute-start.4) | collective-permute-done | bytes 81952 | tf_op jit(solution)/shard_map/ppermute | solution.py:243
  16.7 0.0 collective-permute-start.2
  16.7 6.3 %collective-permute-done.2.low2 = bf16[64,640]{1,0:T(8,128)(2,1)S(1)} collective-permute-done((bf16[64,640]{1,0:T(8,128)(2,1)S(1)}, bf16[64,640]{1,0:T(8,128)(2,1)S(1)}, u32[]{:S(2)}, u32[]{:S(2)}) %collective-permute-start.2) | collective-permute-done | bytes 81952 | tf_op jit(solution)/shard_map/ppermute | solution.py:243
  23.1 0.3 collective-permute-start.3
  23.3 5.0 %collective-permute-done.3.top3 = bf16[64,640]{1,0:T(8,128)(2,1)S(1)} collective-permute-done((bf16[64,640]{1,0:T(8,128)(2,1)S(1)}, bf16[64,640]{1,0:T(8,128)(2,1)S(1)}, u32[]{:S(2)}, u32[]{:S(2)}) %collective-permute-start.3) | collective-permute-done | bytes 81952 | tf_op jit(solution)/shard_map/ppermute | solution.py:243
  28.4 0.0 collective-permute-start
  28.4 0.8 %shard_map.94.refs_0_.refs_4_ = bf16[128,384]{1,0:T(8,128)(2,1)S(1)} custom-call(bf16[128,128]{1,0:T(8,128)(2,1)} %query_ref.1, bf16[128,128]{1,0:T(8,128)(2,1)} %key_ref.1, bf16[128,128]{1,0:T(8,128)(2,1)} %value_ref.1), custom_call_target="tpu_custom_call" | custom-call | tf_op jit(solution)/shard_map/pallas_call | solution.py:212
  29.2 4.7 %collective-permute-done.near = bf16[128,640]{1,0:T(8,128)(2,1)S(1)} collective-permute-done((bf16[128,640]{1,0:T(8,128)(2,1)}, bf16[128,640]{1,0:T(8,128)(2,1)S(1)}, u32[]{:S(2)}, u32[]{:S(2)}) %collective-permute-start) | collective-permute-done | bytes 163872 | tf_op jit(solution)/shard_map/ppermute | solution.py:243
  33.9 2.6 %collective-permute-start.12 = (bf16[128,384]{1,0:T(8,128)(2,1)S(1)}, bf16[128,384]{1,0:T(8,128)(2,1)S(1)}, u32[]{:S(2)}, u32[]{:S(2)}) collective-permute-start(bf16[128,384]{1,0:T(8,128)(2,1)S(1)} %shard_map.94.refs_0_.refs_4_), channel_id=1, source_target_pairs={{0,24},{8,16},{16,8},{24,0},{1,25},{9,17},{17,9},{25,1},{2,26},{10... | collective-permute-start | bytes 294920 | tf_op jit(solution)/shard_map/ppermute | solution.py:249
  36.5 1.3 %shard_map.92.own_w = bf16[128,5120]{1,0:T(8,128)(2,1)S(1)} custom-call(bf16[128,5120]{1,0:T(8,128)(2,1)} %whole_ref.3), custom_call_target="tpu_custom_call" | custom-call | tf_op jit(solution)/shard_map/pallas_call | solution.py:212
  37.8 0.0 copy-start.3
  37.8 0.0 collective-permute-done.5.mate_w
  37.8 0.0 copy-start.2
  37.8 0.6 shard_map.93
  38.4 0.1 collective-permute-start.6
  38.5 0.9 %collective-permute-done.12.refs_3_.refs_7_ = bf16[128,384]{1,0:T(8,128)(2,1)S(1)} collective-permute-done((bf16[128,384]{1,0:T(8,128)(2,1)S(1)}, bf16[128,384]{1,0:T(8,128)(2,1)S(1)}, u32[]{:S(2)}, u32[]{:S(2)}) %collective-permute-start.12) | collective-permute-done | bytes 98336 | tf_op jit(solution)/shard_map/ppermute | solution.py:249
  39.4 1.6 %collective-permute-start.11 = (bf16[128,384]{1,0:T(8,128)(2,1)S(1)}, bf16[128,384]{1,0:T(8,128)(2,1)S(1)}, u32[]{:S(2)}, u32[]{:S(2)}) collective-permute-start(bf16[128,384]{1,0:T(8,128)(2,1)S(1)} %shard_map.94.refs_0_.refs_4_), channel_id=1, source_target_pairs={{0,16},{8,24},{16,0},{24,8},{1,17},{9,25},{17,1},{25,9},{2,18},{10... | collective-permute-start | bytes 294920 | tf_op jit(solution)/shard_map/ppermute | solution.py:249
  41.1 0.0 collective-permute-done.6
  41.1 1.5 %collective-permute-start.10 = (bf16[128,384]{1,0:T(8,128)(2,1)S(1)}, bf16[128,384]{1,0:T(8,128)(2,1)S(1)}, u32[]{:S(2)}, u32[]{:S(2)}) collective-permute-start(bf16[128,384]{1,0:T(8,128)(2,1)S(1)} %shard_map.94.refs_0_.refs_4_), channel_id=1, source_target_pairs={{0,8},{8,0},{16,24},{24,16},{1,9},{9,1},{17,25},{25,17},{2,10},{10... | collective-permute-start | bytes 294920 | tf_op jit(solution)/shard_map/ppermute | solution.py:249
  42.6 0.0 copy-start
  42.6 1.5 %collective-permute-done.11.refs_2_.refs_6_ = bf16[128,384]{1,0:T(8,128)(2,1)S(1)} collective-permute-done((bf16[128,384]{1,0:T(8,128)(2,1)S(1)}, bf16[128,384]{1,0:T(8,128)(2,1)S(1)}, u32[]{:S(2)}, u32[]{:S(2)}) %collective-permute-start.11) | collective-permute-done | bytes 98336 | tf_op jit(solution)/shard_map/ppermute | solution.py:249
  44.0 2.9 %collective-permute-start.9 = (bf16[128,128]{1,0:T(8,128)(2,1)S(1)}, bf16[128,128]{1,0:T(8,128)(2,1)S(1)}, u32[]{:S(2)}, u32[]{:S(2)}) collective-permute-start(bf16[128,128]{1,0:T(8,128)(2,1)S(1)} %add_convert_fusion.grad_ref.refs_0_), channel_id=1, source_target_pairs={{0,24},{8,16},{16,8},{24,0},{1,25},{9,17},{17,9},{25,1},{2,26},{10... | collective-permute-start | bytes 98312 | tf_op jit(solution)/shard_map/ppermute | solution.py:249
  46.9 0.0 collective-permute-done.10.refs_1_.refs_5_
  47.0 0.2 collective-permute-start.8
  47.1 1.7 %collective-permute-done.9.refs_3_ = bf16[128,128]{1,0:T(8,128)(2,1)S(1)} collective-permute-done((bf16[128,128]{1,0:T(8,128)(2,1)S(1)}, bf16[128,128]{1,0:T(8,128)(2,1)S(1)}, u32[]{:S(2)}, u32[]{:S(2)}) %collective-permute-start.9) | collective-permute-done | bytes 32800 | tf_op jit(solution)/shard_map/ppermute | solution.py:249
  48.9 1.6 %collective-permute-start.7 = (bf16[128,128]{1,0:T(8,128)(2,1)S(1)}, bf16[128,128]{1,0:T(8,128)(2,1)S(1)}, u32[]{:S(2)}, u32[]{:S(2)}) collective-permute-start(bf16[128,128]{1,0:T(8,128)(2,1)S(1)} %add_convert_fusion.grad_ref.refs_0_), channel_id=1, source_target_pairs={{0,8},{8,0},{16,24},{24,16},{1,9},{9,1},{17,25},{25,17},{2,10},{10... | collective-permute-start | bytes 98312 | tf_op jit(solution)/shard_map/ppermute | solution.py:249
  50.5 0.0 copy-done.3
  50.5 2.1 %shard_map.95 = (f32[128,512]{1,0:T(8,128)S(1)}, f32[512,128]{1,0:T(8,128)S(1)}, f32[512,128]{1,0:T(8,128)S(1)}) custom-call(s32[4,3]{1,0:T(4,128)S(1)} %copy-done.3, bf16[128,384]{1,0:T(8,128)(2,1)S(1)} %shard_map.94.refs_0_.refs_4_, bf16[128,384]{1,0:T(8,128)(2,1)S(1)} %collective-permute-done.10.refs_1_.refs_5_, ...), custom_call_target="tpu_custom_call" | custom-call | tf_op jit(solution)/shard_map/pallas_call | solution.py:212
  52.6 0.3 shard_map.96.refs_8_
  52.9 0.0 collective-permute-done.8.refs_2_
  52.9 0.0 collective-permute-done.7.refs_1_
  52.9 0.5 shard_map.97.own_ref
  53.4 0.1 collective-permute-start.13
  53.5 0.0 collective-permute-done.14.refs_3_
  53.5 0.0 collective-permute-done.15.refs_4_
  53.5 0.0 collective-permute-done.16.refs_5_
  53.5 1.3 %collective-permute-done.13.mate_ref = bf16[128,384]{1,0:T(8,128)(2,1)S(1)} collective-permute-done((bf16[128,384]{1,0:T(8,128)(2,1)S(1)}, bf16[128,384]{1,0:T(8,128)(2,1)S(1)}, u32[]{:S(2)}, u32[]{:S(2)}) %collective-permute-start.13) | collective-permute-done | bytes 98336 | tf_op jit(solution)/shard_map/ppermute | solution.py:246
  54.8 0.0 copy-done.2
  54.8 0.0 copy-done
  54.8 0.3 shard_map.100
  55.1 0.1 collective-permute-start.18
  55.1 0.4 shard_map.99
  55.6 2.1 %collective-permute-start.17 = (bf16[640,128]{1,0:T(8,128)(2,1)S(1)}, bf16[640,128]{1,0:T(8,128)(2,1)S(1)}, u32[]{:S(2)}, u32[]{:S(2)}) collective-permute-start(bf16[640,128]{1,0:T(8,128)(2,1)S(1)} %shard_map.99), channel_id=1, source_target_pairs={{0,2},{1,3},{2,0},{3,1},{4,6},{5,7},{6,4},{7,5},{8,10},{9,11},{10,... | collective-permute-start | bytes 491528 | tf_op jit(solution)/shard_map/ppermute | solution.py:243
  57.6 0.3 shard_map.102
  57.9 0.4 collective-permute-start.20
  58.3 0.3 shard_map.103
  58.6 2.1 %collective-permute-start.21 = (bf16[320,128]{1,0:T(8,128)(2,1)S(1)}, bf16[320,128]{1,0:T(8,128)(2,1)S(1)}, u32[]{:S(2)}, u32[]{:S(2)}) collective-permute-start(bf16[320,128]{1,0:T(8,128)(2,1)S(1)} %shard_map.103), channel_id=1, source_target_pairs={{0,6},{1,7},{2,4},{3,5},{4,2},{5,3},{6,0},{7,1},{8,14},{9,15},{10,... | collective-permute-start | bytes 245768 | tf_op jit(solution)/shard_map/ppermute | solution.py:243
  60.7 0.0 collective-permute-done.18.refs_6_
  60.7 0.3 shard_map.101
  61.0 1.5 %collective-permute-start.19 = (bf16[320,128]{1,0:T(8,128)(2,1)S(1)}, bf16[320,128]{1,0:T(8,128)(2,1)S(1)}, u32[]{:S(2)}, u32[]{:S(2)}) collective-permute-start(bf16[320,128]{1,0:T(8,128)(2,1)S(1)} %shard_map.101), channel_id=1, source_target_pairs={{0,4},{1,5},{2,6},{3,7},{4,0},{5,1},{6,2},{7,3},{8,12},{9,13},{10,... | collective-permute-start | bytes 245768 | tf_op jit(solution)/shard_map/ppermute | solution.py:243
  62.5 0.4 shard_map.98.own_ref
  63.0 6.4 %collective-permute-done.20.low2 = bf16[320,128]{1,0:T(8,128)(2,1)S(1)} collective-permute-done((bf16[320,128]{1,0:T(8,128)(2,1)S(1)}, bf16[320,128]{1,0:T(8,128)(2,1)S(1)}, u32[]{:S(2)}, u32[]{:S(2)}) %collective-permute-start.20) | collective-permute-done | bytes 81952 | tf_op jit(solution)/shard_map/ppermute | solution.py:243
  69.4 0.0 collective-permute-done.21.low3
  69.4 2.3 %collective-permute-done.19.top2 = bf16[320,128]{1,0:T(8,128)(2,1)S(1)} collective-permute-done((bf16[320,128]{1,0:T(8,128)(2,1)S(1)}, bf16[320,128]{1,0:T(8,128)(2,1)S(1)}, u32[]{:S(2)}, u32[]{:S(2)}) %collective-permute-start.19) | collective-permute-done | bytes 81952 | tf_op jit(solution)/shard_map/ppermute | solution.py:243
  71.7 0.0 collective-permute-done.17.near
  71.7 0.8 %shard_map.104 = f32[640,128]{1,0:T(8,128)} custom-call(f32[640,128]{1,0:T(8,128)S(1)} %shard_map.98.own_ref, bf16[640,128]{1,0:T(8,128)(2,1)S(1)} %collective-permute-done.17.near, bf16[320,128]{1,0:T(8,128)(2,1)S(1)} %collective-permute-done.19.top2, bf16[320,128]{1,0:T(8,128)(2,1)S(1)} %collective-permute-done.20.low2, ...), custom_call_target="tpu_custom_call" | custom-call | tf_op jit(solution)/shard_map/pallas_call | solution.py:212
  (3 shorter events, 0.0 us)
Async XLA Ops:
  0.0 37.8 %collective-permute-start.5 = (bf16[128,5120]{1,0:T(8,128)(2,1)}, bf16[128,5120]{1,0:T(8,128)(2,1)S(1)}, u32[]{:S(2)}, u32[]{:S(2)}) collective-permute-start(bf16[128,5120]{1,0:T(8,128)(2,1)} %whole_ref.3), channel_id=1, source_target_pairs={{0,1},{1,0},{2,3},{3,2},{4,5},{5,4},{6,7},{7,6},{8,9},{9,8},{10,11... | collective-permute-start | bytes 3932168 | tf_op jit(solution)/shard_map/ppermute | solution.py:246
  0.5 53.0 %collective-permute-start.14 = (bf16[5120,128]{1,0:T(8,128)(2,1)}, bf16[5120,128]{1,0:T(8,128)(2,1)S(1)}, u32[]{:S(2)}, u32[]{:S(2)}) collective-permute-start(bf16[5120,128]{1,0:T(8,128)(2,1)} %refs_0_.11), channel_id=1, source_target_pairs={{0,1},{1,0},{2,3},{3,2},{4,5},{5,4},{6,7},{7,6},{8,9},{9,8},{10,11... | collective-permute-start | bytes 3932168 | tf_op jit(solution)/shard_map/ppermute | solution.py:246
  0.5 53.0 %collective-permute-start.15 = (bf16[5120,128]{1,0:T(8,128)(2,1)}, bf16[5120,128]{1,0:T(8,128)(2,1)S(1)}, u32[]{:S(2)}, u32[]{:S(2)}) collective-permute-start(bf16[5120,128]{1,0:T(8,128)(2,1)} %refs_1_.11), channel_id=1, source_target_pairs={{0,1},{1,0},{2,3},{3,2},{4,5},{5,4},{6,7},{7,6},{8,9},{9,8},{10,11... | collective-permute-start | bytes 3932168 | tf_op jit(solution)/shard_map/ppermute | solution.py:246
  1.0 52.5 %collective-permute-start.16 = (bf16[5120,128]{1,0:T(8,128)(2,1)}, bf16[5120,128]{1,0:T(8,128)(2,1)S(1)}, u32[]{:S(2)}, u32[]{:S(2)}) collective-permute-start(bf16[5120,128]{1,0:T(8,128)(2,1)} %refs_2_.11), channel_id=1, source_target_pairs={{0,1},{1,0},{2,3},{3,2},{4,5},{5,4},{6,7},{7,6},{8,9},{9,8},{10,11... | collective-permute-start | bytes 3932168 | tf_op jit(solution)/shard_map/ppermute | solution.py:246
  2.0 8.5 %collective-permute-start.1 = (bf16[64,640]{1,0:T(8,128)(2,1)S(1)}, bf16[64,640]{1,0:T(8,128)(2,1)S(1)}, u32[]{:S(2)}, u32[]{:S(2)}) collective-permute-start(bf16[64,640]{1,0:T(8,128)(2,1)S(1)} %get-tuple-element.12.top), channel_id=1, source_target_pairs={{0,4},{1,5},{2,6},{3,7},{4,0},{5,1},{6,2},{7,3},{8,12},{9,13},{10,... | collective-permute-start | bytes 245768 | tf_op jit(solution)/shard_map/ppermute | solution.py:243
  10.5 6.3 %collective-permute-start.4 = (bf16[64,640]{1,0:T(8,128)(2,1)S(1)}, bf16[64,640]{1,0:T(8,128)(2,1)S(1)}, u32[]{:S(2)}, u32[]{:S(2)}) collective-permute-start(bf16[64,640]{1,0:T(8,128)(2,1)S(1)} %get-tuple-element.13.low), channel_id=1, source_target_pairs={{0,6},{1,7},{2,4},{3,5},{4,2},{5,3},{6,0},{7,1},{8,14},{9,15},{10,... | collective-permute-start | bytes 245768 | tf_op jit(solution)/shard_map/ppermute | solution.py:243
  16.7 6.3 %collective-permute-start.2 = (bf16[64,640]{1,0:T(8,128)(2,1)S(1)}, bf16[64,640]{1,0:T(8,128)(2,1)S(1)}, u32[]{:S(2)}, u32[]{:S(2)}) collective-permute-start(bf16[64,640]{1,0:T(8,128)(2,1)S(1)} %get-tuple-element.13.low), channel_id=1, source_target_pairs={{0,4},{1,5},{2,6},{3,7},{4,0},{5,1},{6,2},{7,3},{8,12},{9,13},{10,... | collective-permute-start | bytes 245768 | tf_op jit(solution)/shard_map/ppermute | solution.py:243
  23.1 5.3 %collective-permute-start.3 = (bf16[64,640]{1,0:T(8,128)(2,1)S(1)}, bf16[64,640]{1,0:T(8,128)(2,1)S(1)}, u32[]{:S(2)}, u32[]{:S(2)}) collective-permute-start(bf16[64,640]{1,0:T(8,128)(2,1)S(1)} %collective-permute-done.1.top2), channel_id=1, source_target_pairs={{0,2},{1,3},{2,0},{3,1},{4,6},{5,7},{6,4},{7,5},{8,10},{9,11},{10,... | collective-permute-start | bytes 245768 | tf_op jit(solution)/shard_map/ppermute | solution.py:243
  28.4 5.5 %collective-permute-start = (bf16[128,640]{1,0:T(8,128)(2,1)}, bf16[128,640]{1,0:T(8,128)(2,1)S(1)}, u32[]{:S(2)}, u32[]{:S(2)}) collective-permute-start(bf16[128,640]{1,0:T(8,128)(2,1)} %whole_ref.2), channel_id=1, source_target_pairs={{0,2},{1,3},{2,0},{3,1},{4,6},{5,7},{6,4},{7,5},{8,10},{9,11},{10,... | collective-permute-start | bytes 491528 | tf_op jit(solution)/shard_map/ppermute | solution.py:243
  33.9 5.5 %collective-permute-start.12 = (bf16[128,384]{1,0:T(8,128)(2,1)S(1)}, bf16[128,384]{1,0:T(8,128)(2,1)S(1)}, u32[]{:S(2)}, u32[]{:S(2)}) collective-permute-start(bf16[128,384]{1,0:T(8,128)(2,1)S(1)} %shard_map.94.refs_0_.refs_4_), channel_id=1, source_target_pairs={{0,24},{8,16},{16,8},{24,0},{1,25},{9,17},{17,9},{25,1},{2,26},{10... | collective-permute-start | bytes 294920 | tf_op jit(solution)/shard_map/ppermute | solution.py:249
  37.8 12.7 %copy-start.3 = (s32[4,3]{1,0:T(4,128)S(1)}, s32[4,3]{1,0:T(4,128)}, u32[]{:S(2)}) copy-start(s32[4,3]{1,0:T(4,128)} %lists_ref.1) | copy-start | bytes 148
  37.8 16.9 %copy-start.2 = (bf16[5120,128]{1,0:T(8,128)(2,1)S(1)}, bf16[5120,128]{1,0:T(8,128)(2,1)}, u32[]{:S(2)}) copy-start(bf16[5120,128]{1,0:T(8,128)(2,1)} %refs_2_.11) | copy-start | bytes 3932164
  38.4 2.6 %collective-permute-start.6 = (f32[128,128]{1,0:T(8,128)S(1)}, f32[128,128]{1,0:T(8,128)S(1)}, u32[]{:S(2)}, u32[]{:S(2)}) collective-permute-start(f32[128,128]{1,0:T(8,128)S(1)} %get-tuple-element.15), channel_id=1, source_target_pairs={{0,1},{1,0},{2,3},{3,2},{4,5},{5,4},{6,7},{7,6},{8,9},{9,8},{10,11... | collective-permute-start | bytes 196616 | tf_op jit(solution)/shard_map/ppermute | solution.py:246
  39.4 4.6 %collective-permute-start.11 = (bf16[128,384]{1,0:T(8,128)(2,1)S(1)}, bf16[128,384]{1,0:T(8,128)(2,1)S(1)}, u32[]{:S(2)}, u32[]{:S(2)}) collective-permute-start(bf16[128,384]{1,0:T(8,128)(2,1)S(1)} %shard_map.94.refs_0_.refs_4_), channel_id=1, source_target_pairs={{0,16},{8,24},{16,0},{24,8},{1,17},{9,25},{17,1},{25,9},{2,18},{10... | collective-permute-start | bytes 294920 | tf_op jit(solution)/shard_map/ppermute | solution.py:249
  41.1 5.9 %collective-permute-start.10 = (bf16[128,384]{1,0:T(8,128)(2,1)S(1)}, bf16[128,384]{1,0:T(8,128)(2,1)S(1)}, u32[]{:S(2)}, u32[]{:S(2)}) collective-permute-start(bf16[128,384]{1,0:T(8,128)(2,1)S(1)} %shard_map.94.refs_0_.refs_4_), channel_id=1, source_target_pairs={{0,8},{8,0},{16,24},{24,16},{1,9},{9,1},{17,25},{25,17},{2,10},{10... | collective-permute-start | bytes 294920 | tf_op jit(solution)/shard_map/ppermute | solution.py:249
  42.5 12.2 %copy-start.1 = (bf16[5120,128]{1,0:T(8,128)(2,1)S(1)}, bf16[5120,128]{1,0:T(8,128)(2,1)}, u32[]{:S(2)}) copy-start(bf16[5120,128]{1,0:T(8,128)(2,1)} %refs_1_.11) | copy-start | bytes 3932164
  42.6 12.2 %copy-start = (bf16[5120,128]{1,0:T(8,128)(2,1)S(1)}, bf16[5120,128]{1,0:T(8,128)(2,1)}, u32[]{:S(2)}) copy-start(bf16[5120,128]{1,0:T(8,128)(2,1)} %refs_0_.11) | copy-start | bytes 3932164
  44.0 4.8 %collective-permute-start.9 = (bf16[128,128]{1,0:T(8,128)(2,1)S(1)}, bf16[128,128]{1,0:T(8,128)(2,1)S(1)}, u32[]{:S(2)}, u32[]{:S(2)}) collective-permute-start(bf16[128,128]{1,0:T(8,128)(2,1)S(1)} %add_convert_fusion.grad_ref.refs_0_), channel_id=1, source_target_pairs={{0,24},{8,16},{16,8},{24,0},{1,25},{9,17},{17,9},{25,1},{2,26},{10... | collective-permute-start | bytes 98312 | tf_op jit(solution)/shard_map/ppermute | solution.py:249
  47.0 5.9 %collective-permute-start.8 = (bf16[128,128]{1,0:T(8,128)(2,1)S(1)}, bf16[128,128]{1,0:T(8,128)(2,1)S(1)}, u32[]{:S(2)}, u32[]{:S(2)}) collective-permute-start(bf16[128,128]{1,0:T(8,128)(2,1)S(1)} %add_convert_fusion.grad_ref.refs_0_), channel_id=1, source_target_pairs={{0,16},{8,24},{16,0},{24,8},{1,17},{9,25},{17,1},{25,9},{2,18},{10... | collective-permute-start | bytes 98312 | tf_op jit(solution)/shard_map/ppermute | solution.py:249
  48.9 4.1 %collective-permute-start.7 = (bf16[128,128]{1,0:T(8,128)(2,1)S(1)}, bf16[128,128]{1,0:T(8,128)(2,1)S(1)}, u32[]{:S(2)}, u32[]{:S(2)}) collective-permute-start(bf16[128,128]{1,0:T(8,128)(2,1)S(1)} %add_convert_fusion.grad_ref.refs_0_), channel_id=1, source_target_pairs={{0,8},{8,0},{16,24},{24,16},{1,9},{9,1},{17,25},{25,17},{2,10},{10... | collective-permute-start | bytes 98312 | tf_op jit(solution)/shard_map/ppermute | solution.py:249
  53.4 1.4 %collective-permute-start.13 = (bf16[128,384]{1,0:T(8,128)(2,1)S(1)}, bf16[128,384]{1,0:T(8,128)(2,1)S(1)}, u32[]{:S(2)}, u32[]{:S(2)}) collective-permute-start(bf16[128,384]{1,0:T(8,128)(2,1)S(1)} %shard_map.97.own_ref), channel_id=1, source_target_pairs={{0,1},{1,0},{2,3},{3,2},{4,5},{5,4},{6,7},{7,6},{8,9},{9,8},{10,11... | collective-permute-start | bytes 294920 | tf_op jit(solution)/shard_map/ppermute | solution.py:246
  55.1 5.7 %collective-permute-start.18 = (bf16[320,128]{1,0:T(8,128)(2,1)S(1)}, bf16[320,128]{1,0:T(8,128)(2,1)S(1)}, u32[]{:S(2)}, u32[]{:S(2)}) collective-permute-start(bf16[320,128]{1,0:T(8,128)(2,1)S(1)} %shard_map.100), channel_id=1, source_target_pairs={{0,2},{1,3},{2,0},{3,1},{4,6},{5,7},{6,4},{7,5},{8,10},{9,11},{10,... | collective-permute-start | bytes 245768 | tf_op jit(solution)/shard_map/ppermute | solution.py:243
  55.6 16.2 %collective-permute-start.17 = (bf16[640,128]{1,0:T(8,128)(2,1)S(1)}, bf16[640,128]{1,0:T(8,128)(2,1)S(1)}, u32[]{:S(2)}, u32[]{:S(2)}) collective-permute-start(bf16[640,128]{1,0:T(8,128)(2,1)S(1)} %shard_map.99), channel_id=1, source_target_pairs={{0,2},{1,3},{2,0},{3,1},{4,6},{5,7},{6,4},{7,5},{8,10},{9,11},{10,... | collective-permute-start | bytes 491528 | tf_op jit(solution)/shard_map/ppermute | solution.py:243
  57.9 11.5 %collective-permute-start.20 = (bf16[320,128]{1,0:T(8,128)(2,1)S(1)}, bf16[320,128]{1,0:T(8,128)(2,1)S(1)}, u32[]{:S(2)}, u32[]{:S(2)}) collective-permute-start(bf16[320,128]{1,0:T(8,128)(2,1)S(1)} %shard_map.102), channel_id=1, source_target_pairs={{0,4},{1,5},{2,6},{3,7},{4,0},{5,1},{6,2},{7,3},{8,12},{9,13},{10,... | collective-permute-start | bytes 245768 | tf_op jit(solution)/shard_map/ppermute | solution.py:243
  58.6 10.8 %collective-permute-start.21 = (bf16[320,128]{1,0:T(8,128)(2,1)S(1)}, bf16[320,128]{1,0:T(8,128)(2,1)S(1)}, u32[]{:S(2)}, u32[]{:S(2)}) collective-permute-start(bf16[320,128]{1,0:T(8,128)(2,1)S(1)} %shard_map.103), channel_id=1, source_target_pairs={{0,6},{1,7},{2,4},{3,5},{4,2},{5,3},{6,0},{7,1},{8,14},{9,15},{10,... | collective-permute-start | bytes 245768 | tf_op jit(solution)/shard_map/ppermute | solution.py:243
  61.0 10.7 %collective-permute-start.19 = (bf16[320,128]{1,0:T(8,128)(2,1)S(1)}, bf16[320,128]{1,0:T(8,128)(2,1)S(1)}, u32[]{:S(2)}, u32[]{:S(2)}) collective-permute-start(bf16[320,128]{1,0:T(8,128)(2,1)S(1)} %shard_map.101), channel_id=1, source_target_pairs={{0,4},{1,5},{2,6},{3,7},{4,0},{5,1},{6,2},{7,3},{8,12},{9,13},{10,... | collective-permute-start | bytes 245768 | tf_op jit(solution)/shard_map/ppermute | solution.py:243

commit v4 on v3

--- a/solution.py
+++ b/solution.py
@@ -64,7 +64,7 @@
     return lax.psum_scatter(feature_sum, "tp", scatter_dimension=0, tiled=True)
 
 
-def pack_kernel(query_ref, key_ref, value_ref, out_ref, sems):
+def pack_kernel(query_ref, key_ref, value_ref, w_ref, out_ref, w_out_ref, sems):
     size = query_ref.shape[1]
     copies = [
         pltpu.make_async_copy(
@@ -72,6 +72,7 @@
         )
         for place, part in enumerate((query_ref, key_ref, value_ref))
     ]
+    copies.append(pltpu.make_async_copy(w_ref, w_out_ref, sems.at[3]))
     for copy in copies:
         copy.start()
     for copy in copies:
@@ -91,7 +92,7 @@
         copy.wait()
 
 
-def attn_grad_kernel(cols, top, low, near, top2, low2, top3, low3, own_w, mate_w, own_ref, mate_ref):
+def attn_grad_kernel(cols, top, low, near, top2, low2, top3, low3, own_w, mate_w, out_ref):
     index = lax.axis_index("tp")
     blocks = [
         jnp.concatenate([top[...], low[...]], axis=0),
@@ -99,14 +100,23 @@
         jnp.concatenate([top2[...], low2[...]], axis=0),
         jnp.concatenate([top3[...], low3[...]], axis=0),
     ]
-    own = jnp.zeros(own_ref.shape, jnp.float32)
-    mate = jnp.zeros(own_ref.shape, jnp.float32)
+    total = None
     for step, block in enumerate(blocks):
         start = pl.multiple_of((index ^ (2 * step)) * cols, 128)
-        own = own + dot_f32(block, own_w[:, pl.ds(start, cols)], CONTRACT_LAST)
-        mate = mate + dot_f32(block, mate_w[:, pl.ds(start, cols)], CONTRACT_LAST)
-    own_ref[...] = own
-    mate_ref[...] = mate
+        weight = jnp.concatenate(
+            [own_w[:, pl.ds(start, cols)], mate_w[:, pl.ds(start, cols)]], axis=0
+        )
+        term = dot_f32(block, weight, CONTRACT_LAST)
+        total = term if total is None else total + term
+    out_ref[...] = total
+
+
+def merge_kernel(own_ref, mate_ref, out_ref, own_out_ref):
+    size = own_out_ref.shape[1]
+    own = (own_ref[:, :size] + mate_ref[:, size:]).astype(jnp.bfloat16)
+    out_ref[:, :size] = own
+    out_ref[:, size:] = (own_ref[:, size:] + mate_ref[:, :size]).astype(jnp.bfloat16)
+    own_out_ref[...] = own
 
 
 def softmax_kernel(slabs, keep, lists_ref, *refs):
@@ -135,7 +145,7 @@
                 parts.append(jnp.where(listed, part, -jnp.inf))
             scores = jnp.concatenate(parts, axis=1)
             exponent = jnp.exp(scores - jnp.max(scores, axis=1, keepdims=True))
-            prob = exponent / jnp.sum(exponent, axis=1, keepdims=True)
+            prob = exponent * (1.0 / jnp.sum(exponent, axis=1, keepdims=True))
             attn_ref[span, :] = jnp.dot(
                 prob.astype(jnp.bfloat16), values, preferred_element_type=jnp.float32
             )
@@ -159,14 +169,16 @@
     out_ref[...] = jnp.dot(d_score, keys, preferred_element_type=jnp.float32).astype(jnp.bfloat16)
 
 
-def key_grad_kernel(slabs, *refs):
-    grads = refs[:slabs]
-    packs = refs[slabs : 2 * slabs]
-    query_ref, col_ref, attn_ref, out_ref = refs[2 * slabs :]
+def key_grad_kernel(slabs, own, beside, swapped, across, *refs):
+    packs = refs[:slabs]
+    query_ref, col_ref, attn_ref, out_ref = refs[slabs:]
     size = packs[0].shape[1] // 3
     scale = size ** (-0.5)
+    even = (lax.axis_index("tp") & 1) == 0
+    near, far = beside[:, :size], swapped[:, size:]
+    first, second = jnp.where(even, near, far), jnp.where(even, far, near)
     queries = jnp.concatenate([pack[:, :size] for pack in packs], axis=0)
-    grad = jnp.concatenate([part[...] for part in grads], axis=0)
+    grad = jnp.concatenate([own[...], first, second, across[...]], axis=0)
     prob = col_ref[...]
     delta = jnp.sum(grad.astype(jnp.float32) * attn_ref[...], axis=1, keepdims=True)
     d_prob = dot_f32(grad, packs[0][:, 2 * size :], CONTRACT_LAST)
@@ -237,7 +249,7 @@
     rows, cols = grad_out.shape
     size = query_proj.shape[1]
     half, full = jnp.bfloat16, jnp.float32
-    cut, feature_cut = rows // 2, cols // 2
+    cut, feature_cut = rows // 2, cols * 3 // 5 // 16 * 16
 
     def to_chip(x, step):
         return lax.ppermute(x, "tp", [(t, t ^ (2 * step)) for t in range(8)])
@@ -247,6 +259,10 @@
 
     def to_slab(x, turn):
         return lax.ppermute(x, "ctx", [(c, c ^ turn) for c in range(slabs)])
+
+    def to_beside(x):
+        pairs = [(c * 8 + t, (c ^ (1 + t % 2)) * 8 + t) for c in range(slabs) for t in range(8)]
+        return lax.ppermute(x, ("ctx", "tp"), pairs)
 
     top, low = call(
         split_kernel, [grad_out], [((cut, cols), half), ((rows - cut, cols), half)],
@@ -257,27 +273,31 @@
     low2 = to_chip(low, 2)
     low3 = to_chip(low, 3)
     top3 = to_chip(top2, 1)
-    (pack,) = call(
-        pack_kernel, [query_proj, key_proj, value_proj], [((rows, 3 * size), half)],
-        raw=True, sems=3,
+    pack, near_out = call(
+        pack_kernel, [query_proj, key_proj, value_proj, w_out],
+        [((rows, 3 * size), half), (w_out.shape, half)], raw=True, sems=4,
     )
     packs = [pack] + [to_slab(pack, turn) for turn in range(1, slabs)]
     mate_out = to_mate(w_out)
     own_w = [w_query, w_key, w_value]
     mate_w = [to_mate(w) for w in own_w]
-    (near_out,) = call(split_kernel, [w_out], [(w_out.shape, half)], raw=True, sems=1)
     prob_row, prob_col, attn_out = call(
         functools.partial(softmax_kernel, slabs, tile_keys.shape[1]),
         [tile_keys, *packs],
         [((rows, slabs * rows), full), ((slabs * rows, rows), full), ((slabs * rows, size), full)],
     )
-    own_part, mate_part = call(
+    (part,) = call(
         functools.partial(attn_grad_kernel, cols),
         [top, low, near, top2, low2, top3, low3, near_out, mate_out],
-        [((rows, size), full), ((rows, size), full)],
-    )
-    grad = (own_part + to_mate(mate_part)).astype(half)
-    grads = [grad] + [to_slab(grad, turn) for turn in range(1, slabs)]
+        [((rows, 2 * size), full)],
+    )
+    both, grad = call(
+        merge_kernel, [part, to_mate(part)],
+        [((rows, 2 * size), half), ((rows, size), half)],
+    )
+    beside = to_beside(both)
+    across = to_slab(grad, 3)
+    swapped = to_mate(beside)
     (d_query,) = call(
         functools.partial(query_grad_kernel, slabs),
         [grad, *packs, prob_row, attn_out],
@@ -285,7 +305,7 @@
     )
     (own_grads,) = call(
         functools.partial(key_grad_kernel, slabs),
-        [*grads, *packs, d_query, prob_col, attn_out],
+        [grad, beside, swapped, across, *packs, d_query, prob_col, attn_out],
         [((rows, 3 * size), half)],
     )
     mate_grads = to_mate(own_grads)
@@ -316,7 +336,7 @@
 
 def solution(mesh):
     slabs, shards = mesh.shape["ctx"], mesh.shape["tp"]
-    few = slabs in (4, 8) and shards == 8
+    few = slabs == 4 and shards == 8
     return jax.shard_map(
         functools.partial(few_slabs, slabs) if few else many_slabs,
         mesh=mesh,

time: 72.7 us -> 73.2 us (level)
  waiting for transfers between devices: 37.3 us -> 41.8 us
  starting transfers between devices: 25.7 us -> 22.4 us
  Pallas kernels: 9.31 us -> 8.51 us
    ppermute x0 -> x1, waiting for transfers between devices: none -> 3.73 us  [to_beside(): return lax.ppermute(x, ('ctx', 'tp'), pairs)]
    ppermute x6 -> x4, starting transfers between devices: 10.4 us -> 6.86 us  [to_slab(): return lax.ppermute(x, 'ctx', [(c, c ^ turn) for c in range(slabs)])]
    ppermute x10, waiting for transfers between devices: 31.9 us -> 33.6 us  [to_chip(): return lax.ppermute(x, 'tp', [(t, t ^ 2 * step) for t in range(8)])]
    ppermute x6 -> x4, waiting for transfers between devices: 4.11 us -> 3.22 us  [to_slab(): return lax.ppermute(x, 'ctx', [(c, c ^ turn) for c in range(slabs)])]
    pallas_call x14, Pallas kernels: 9.31 us -> 8.51 us  [call(): pl.pallas_call(kernel, in_specs=[SMEM if flag else there for flag in ints...]
  transfers between devices with their start and end apart: 22 -> 22, of which waited for: 11 -> 12; matrix products, arithmetic and copies ran while one was open for 0% -> 0% of each run, Pallas kernels for 11% -> 10%
where the time goes in v4:
time: 73.2 us; the launch traced here: 73 us
  waiting for transfers between devices  41.8 us (57%)
  starting transfers between devices  22.4 us (31%)
  Pallas kernels  8.51 us (12%)
    ppermute x10, waiting for transfers between devices, to_chip(): return lax.ppermute(x, 'tp', [(t, t ^ 2 * step) for t in range(8)])  33.6 us
    ppermute x10, starting transfers between devices, to_chip(): return lax.ppermute(x, 'tp', [(t, t ^ 2 * step) for t in range(8)])  13.9 us
    pallas_call x14, Pallas kernels, call(): pl.pallas_call(kernel, in_specs=[SMEM if flag else there for flag in ints...  8.51 us
    ppermute x4, starting transfers between devices, to_slab(): return lax.ppermute(x, 'ctx', [(c, c ^ turn) for c in range(slabs)])  6.86 us
    ppermute x1, waiting for transfers between devices, to_beside(): return lax.ppermute(x, ('ctx', 'tp'), pairs)  3.73 us
    ppermute x4, waiting for transfers between devices, to_slab(): return lax.ppermute(x, 'ctx', [(c, c ^ turn) for c in range(slabs)])  3.22 us
  transfers between devices with their start and end apart: 22, of which 12 were waited for; matrix products, arithmetic and copies ran while one was open for 0% of the time, Pallas kernels for 10%

profile of v4, /device:TPU:0, one launch (start us, length us, event | category | flops | bytes accessed | tf_op | source)
XLA Modules:
  0.0 73.0 jit_solution(17203610868914732377)
XLA Ops:
  0.0 0.5 collective-permute-start.5
  0.5 0.0 collective-permute-start.14
  0.5 0.5 collective-permute-start.15
  1.0 0.0 collective-permute-start.16
  1.0 0.9 %shard_map.91 = (bf16[64,640]{1,0:T(8,128)(2,1)S(1)}, bf16[64,640]{1,0:T(8,128)(2,1)S(1)}) custom-call(bf16[128,640]{1,0:T(8,128)(2,1)} %whole_ref.1), custom_call_target="tpu_custom_call" | custom-call | tf_op jit(solution)/shard_map/pallas_call | solution.py:224
  2.0 4.1 %collective-permute-start.1 = (bf16[64,640]{1,0:T(8,128)(2,1)S(1)}, bf16[64,640]{1,0:T(8,128)(2,1)S(1)}, u32[]{:S(2)}, u32[]{:S(2)}) collective-permute-start(bf16[64,640]{1,0:T(8,128)(2,1)S(1)} %get-tuple-element.14.top), channel_id=1, source_target_pairs={{0,4},{1,5},{2,6},{3,7},{4,0},{5,1},{6,2},{7,3},{8,12},{9,13},{10,... | collective-permute-start | bytes 245768 | tf_op jit(solution)/shard_map/ppermute | solution.py:255
  6.1 4.4 %collective-permute-done.1.top2 = bf16[64,640]{1,0:T(8,128)(2,1)S(1)} collective-permute-done((bf16[64,640]{1,0:T(8,128)(2,1)S(1)}, bf16[64,640]{1,0:T(8,128)(2,1)S(1)}, u32[]{:S(2)}, u32[]{:S(2)}) %collective-permute-start.1) | collective-permute-done | bytes 81952 | tf_op jit(solution)/shard_map/ppermute | solution.py:255
  10.5 1.0 %collective-permute-start.2 = (bf16[64,640]{1,0:T(8,128)(2,1)S(1)}, bf16[64,640]{1,0:T(8,128)(2,1)S(1)}, u32[]{:S(2)}, u32[]{:S(2)}) collective-permute-start(bf16[64,640]{1,0:T(8,128)(2,1)S(1)} %get-tuple-element.15.low), channel_id=1, source_target_pairs={{0,4},{1,5},{2,6},{3,7},{4,0},{5,1},{6,2},{7,3},{8,12},{9,13},{10,... | collective-permute-start | bytes 245768 | tf_op jit(solution)/shard_map/ppermute | solution.py:255
  11.5 6.1 %collective-permute-done.2.low2 = bf16[64,640]{1,0:T(8,128)(2,1)S(1)} collective-permute-done((bf16[64,640]{1,0:T(8,128)(2,1)S(1)}, bf16[64,640]{1,0:T(8,128)(2,1)S(1)}, u32[]{:S(2)}, u32[]{:S(2)}) %collective-permute-start.2) | collective-permute-done | bytes 81952 | tf_op jit(solution)/shard_map/ppermute | solution.py:255
  17.5 1.9 %collective-permute-start.4 = (bf16[64,640]{1,0:T(8,128)(2,1)S(1)}, bf16[64,640]{1,0:T(8,128)(2,1)S(1)}, u32[]{:S(2)}, u32[]{:S(2)}) collective-permute-start(bf16[64,640]{1,0:T(8,128)(2,1)S(1)} %get-tuple-element.15.low), channel_id=1, source_target_pairs={{0,6},{1,7},{2,4},{3,5},{4,2},{5,3},{6,0},{7,1},{8,14},{9,15},{10,... | collective-permute-start | bytes 245768 | tf_op jit(solution)/shard_map/ppermute | solution.py:255
  19.4 4.4 %collective-permute-done.4.low3 = bf16[64,640]{1,0:T(8,128)(2,1)S(1)} collective-permute-done((bf16[64,640]{1,0:T(8,128)(2,1)S(1)}, bf16[64,640]{1,0:T(8,128)(2,1)S(1)}, u32[]{:S(2)}, u32[]{:S(2)}) %collective-permute-start.4) | collective-permute-done | bytes 81952 | tf_op jit(solution)/shard_map/ppermute | solution.py:255
  23.8 0.0 collective-permute-start.3
  23.8 5.3 %collective-permute-done.3.top3 = bf16[64,640]{1,0:T(8,128)(2,1)S(1)} collective-permute-done((bf16[64,640]{1,0:T(8,128)(2,1)S(1)}, bf16[64,640]{1,0:T(8,128)(2,1)S(1)}, u32[]{:S(2)}, u32[]{:S(2)}) %collective-permute-start.3) | collective-permute-done | bytes 81952 | tf_op jit(solution)/shard_map/ppermute | solution.py:255
  29.2 0.0 collective-permute-start
  29.2 1.4 %shard_map.92 = (bf16[128,384]{1,0:T(8,128)(2,1)S(1)}, bf16[128,5120]{1,0:T(8,128)(2,1)S(1)}) custom-call(bf16[128,128]{1,0:T(8,128)(2,1)} %query_ref.1, bf16[128,128]{1,0:T(8,128)(2,1)} %key_ref.1, bf16[128,128]{1,0:T(8,128)(2,1)} %value_ref.1, bf16[128,5120]{1,0:T(8,128)(2,1)} %w_ref.1), custom_call_target="tpu_custom_call" | custom-call | tf_op jit(solution)/shard_map/pallas_call | solution.py:224
  30.6 4.1 %collective-permute-done.near = bf16[128,640]{1,0:T(8,128)(2,1)S(1)} collective-permute-done((bf16[128,640]{1,0:T(8,128)(2,1)}, bf16[128,640]{1,0:T(8,128)(2,1)S(1)}, u32[]{:S(2)}, u32[]{:S(2)}) %collective-permute-start) | collective-permute-done | bytes 163872 | tf_op jit(solution)/shard_map/ppermute | solution.py:255
  34.7 0.0 collective-permute-done.5.mate_w
  34.7 0.0 copy-start.2
  34.7 0.5 shard_map.93.own_ref
  35.2 0.1 collective-permute-start.6
  35.3 1.6 %collective-permute-start.10 = (bf16[128,384]{1,0:T(8,128)(2,1)S(1)}, bf16[128,384]{1,0:T(8,128)(2,1)S(1)}, u32[]{:S(2)}, u32[]{:S(2)}) collective-permute-start(bf16[128,384]{1,0:T(8,128)(2,1)S(1)} %get-tuple-element.19.refs_0_), channel_id=1, source_target_pairs={{0,8},{8,0},{16,24},{24,16},{1,9},{9,1},{17,25},{25,17},{2,10},{10... | collective-permute-start | bytes 294920 | tf_op jit(solution)/shard_map/ppermute | solution.py:261
  36.9 0.0 collective-permute-done.6.mate_ref
  36.9 1.5 %collective-permute-start.11 = (bf16[128,384]{1,0:T(8,128)(2,1)S(1)}, bf16[128,384]{1,0:T(8,128)(2,1)S(1)}, u32[]{:S(2)}, u32[]{:S(2)}) collective-permute-start(bf16[128,384]{1,0:T(8,128)(2,1)S(1)} %get-tuple-element.19.refs_0_), channel_id=1, source_target_pairs={{0,16},{8,24},{16,0},{24,8},{1,17},{9,25},{17,1},{25,9},{2,18},{10... | collective-permute-start | bytes 294920 | tf_op jit(solution)/shard_map/ppermute | solution.py:261
  38.4 2.1 %collective-permute-done.10.refs_1_ = bf16[128,384]{1,0:T(8,128)(2,1)S(1)} collective-permute-done((bf16[128,384]{1,0:T(8,128)(2,1)S(1)}, bf16[128,384]{1,0:T(8,128)(2,1)S(1)}, u32[]{:S(2)}, u32[]{:S(2)}) %collective-permute-start.10) | collective-permute-done | bytes 98336 | tf_op jit(solution)/shard_map/ppermute | solution.py:261
  40.5 2.4 %collective-permute-start.12 = (bf16[128,384]{1,0:T(8,128)(2,1)S(1)}, bf16[128,384]{1,0:T(8,128)(2,1)S(1)}, u32[]{:S(2)}, u32[]{:S(2)}) collective-permute-start(bf16[128,384]{1,0:T(8,128)(2,1)S(1)} %get-tuple-element.19.refs_0_), channel_id=1, source_target_pairs={{0,24},{8,16},{16,8},{24,0},{1,25},{9,17},{17,9},{25,1},{2,26},{10... | collective-permute-start | bytes 294920 | tf_op jit(solution)/shard_map/ppermute | solution.py:261
  43.0 0.0 collective-permute-done.11.refs_2_
  43.0 0.5 collective-permute-start.7
  43.5 3.7 %collective-permute-done.7.beside = bf16[128,256]{1,0:T(8,128)(2,1)S(1)} collective-permute-done((bf16[128,256]{1,0:T(8,128)(2,1)S(1)}, bf16[128,256]{1,0:T(8,128)(2,1)S(1)}, u32[]{:S(2)}, u32[]{:S(2)}) %collective-permute-start.7) | collective-permute-done | bytes 65568 | tf_op jit(solution)/shard_map/ppermute | solution.py:265
  47.2 0.0 collective-permute-start.8
  47.2 0.0 collective-permute-done.12.refs_3_
  47.2 0.0 copy-start
  47.2 0.0 copy-start.1
  47.2 1.3 %collective-permute-start.9 = (bf16[128,128]{1,0:T(8,128)(2,1)S(1)}, bf16[128,128]{1,0:T(8,128)(2,1)S(1)}, u32[]{:S(2)}, u32[]{:S(2)}) collective-permute-start(bf16[128,128]{1,0:T(8,128)(2,1)S(1)} %get-tuple-element.17.grad_ref.own), channel_id=1, source_target_pairs={{0,24},{8,16},{16,8},{24,0},{1,25},{9,17},{17,9},{25,1},{2,26},{10... | collective-permute-start | bytes 98312 | tf_op jit(solution)/shard_map/ppermute | solution.py:261
  48.6 0.0 copy-done.3
  48.6 2.1 %shard_map.95 = (f32[128,512]{1,0:T(8,128)S(1)}, f32[512,128]{1,0:T(8,128)S(1)}, f32[512,128]{1,0:T(8,128)S(1)}) custom-call(s32[4,3]{1,0:T(4,128)S(1)} %copy-done.3, bf16[128,384]{1,0:T(8,128)(2,1)S(1)} %get-tuple-element.19.refs_0_, bf16[128,384]{1,0:T(8,128)(2,1)S(1)} %collective-permute-done.10.refs_1_, ...), custom_call_target="tpu_custom_call" | custom-call | tf_op jit(solution)/shard_map/pallas_call | solution.py:224
  50.7 0.3 shard_map.96.refs_4_
  51.0 1.1 %collective-permute-done.9.across = bf16[128,128]{1,0:T(8,128)(2,1)S(1)} collective-permute-done((bf16[128,128]{1,0:T(8,128)(2,1)S(1)}, bf16[128,128]{1,0:T(8,128)(2,1)S(1)}, u32[]{:S(2)}, u32[]{:S(2)}) %collective-permute-start.9) | collective-permute-done | bytes 32800 | tf_op jit(solution)/shard_map/ppermute | solution.py:261
  52.1 0.0 collective-permute-done.8.swapped
  52.1 0.5 shard_map.97.own_ref
  52.6 0.1 collective-permute-start.13
  52.7 0.0 collective-permute-done.14.refs_3_
  52.7 0.0 collective-permute-done.15.refs_4_
  52.7 0.0 collective-permute-done.16.refs_5_
  52.7 1.3 %collective-permute-done.13.mate_ref = bf16[128,384]{1,0:T(8,128)(2,1)S(1)} collective-permute-done((bf16[128,384]{1,0:T(8,128)(2,1)S(1)}, bf16[128,384]{1,0:T(8,128)(2,1)S(1)}, u32[]{:S(2)}, u32[]{:S(2)}) %collective-permute-start.13) | collective-permute-done | bytes 98336 | tf_op jit(solution)/shard_map/ppermute | solution.py:258
  54.0 0.0 copy-done.2
  54.0 0.0 copy-done
  54.0 0.0 copy-done.1
  54.0 0.3 shard_map.100
  54.3 0.1 collective-permute-start.18
  54.4 0.4 shard_map.99
  54.8 2.1 %collective-permute-start.17 = (bf16[640,128]{1,0:T(8,128)(2,1)S(1)}, bf16[640,128]{1,0:T(8,128)(2,1)S(1)}, u32[]{:S(2)}, u32[]{:S(2)}) collective-permute-start(bf16[640,128]{1,0:T(8,128)(2,1)S(1)} %shard_map.99), channel_id=1, source_target_pairs={{0,2},{1,3},{2,0},{3,1},{4,6},{5,7},{6,4},{7,5},{8,10},{9,11},{10,... | collective-permute-start | bytes 491528 | tf_op jit(solution)/shard_map/ppermute | solution.py:255
  56.9 3.1 %collective-permute-done.18.refs_6_ = bf16[384,128]{1,0:T(8,128)(2,1)S(1)} collective-permute-done((bf16[384,128]{1,0:T(8,128)(2,1)S(1)}, bf16[384,128]{1,0:T(8,128)(2,1)S(1)}, u32[]{:S(2)}, u32[]{:S(2)}) %collective-permute-start.18) | collective-permute-done | bytes 98336 | tf_op jit(solution)/shard_map/ppermute | solution.py:255
  60.0 0.3 shard_map.101
  60.3 0.7 collective-permute-start.19
  61.0 0.3 shard_map.103
  61.3 1.9 %collective-permute-start.21 = (bf16[256,128]{1,0:T(8,128)(2,1)S(1)}, bf16[256,128]{1,0:T(8,128)(2,1)S(1)}, u32[]{:S(2)}, u32[]{:S(2)}) collective-permute-start(bf16[256,128]{1,0:T(8,128)(2,1)S(1)} %shard_map.103), channel_id=1, source_target_pairs={{0,6},{1,7},{2,4},{3,5},{4,2},{5,3},{6,0},{7,1},{8,14},{9,15},{10,... | collective-permute-start | bytes 196616 | tf_op jit(solution)/shard_map/ppermute | solution.py:255
  63.2 0.3 shard_map.102
  63.5 2.1 %collective-permute-start.20 = (bf16[256,128]{1,0:T(8,128)(2,1)S(1)}, bf16[256,128]{1,0:T(8,128)(2,1)S(1)}, u32[]{:S(2)}, u32[]{:S(2)}) collective-permute-start(bf16[256,128]{1,0:T(8,128)(2,1)S(1)} %shard_map.102), channel_id=1, source_target_pairs={{0,4},{1,5},{2,6},{3,7},{4,0},{5,1},{6,2},{7,3},{8,12},{9,13},{10,... | collective-permute-start | bytes 196616 | tf_op jit(solution)/shard_map/ppermute | solution.py:255
  65.6 0.4 shard_map.98.own_ref
  66.0 1.8 %collective-permute-done.21.low3 = bf16[256,128]{1,0:T(8,128)(2,1)S(1)} collective-permute-done((bf16[256,128]{1,0:T(8,128)(2,1)S(1)}, bf16[256,128]{1,0:T(8,128)(2,1)S(1)}, u32[]{:S(2)}, u32[]{:S(2)}) %collective-permute-start.21) | collective-permute-done | bytes 65568 | tf_op jit(solution)/shard_map/ppermute | solution.py:255
  67.7 4.5 %collective-permute-done.20.low2 = bf16[256,128]{1,0:T(8,128)(2,1)S(1)} collective-permute-done((bf16[256,128]{1,0:T(8,128)(2,1)S(1)}, bf16[256,128]{1,0:T(8,128)(2,1)S(1)}, u32[]{:S(2)}, u32[]{:S(2)}) %collective-permute-start.20) | collective-permute-done | bytes 65568 | tf_op jit(solution)/shard_map/ppermute | solution.py:255
  72.2 0.0 collective-permute-done.17.near
  72.2 0.0 collective-permute-done.19.top2
  72.2 0.8 %shard_map.104 = f32[640,128]{1,0:T(8,128)} custom-call(f32[640,128]{1,0:T(8,128)S(1)} %shard_map.98.own_ref, bf16[640,128]{1,0:T(8,128)(2,1)S(1)} %collective-permute-done.17.near, bf16[384,128]{1,0:T(8,128)(2,1)S(1)} %collective-permute-done.19.top2, bf16[256,128]{1,0:T(8,128)(2,1)S(1)} %collective-permute-done.20.low2, ...), custom_call_target="tpu_custom_call" | custom-call | tf_op jit(solution)/shard_map/pallas_call | solution.py:224
  (2 shorter events, 0.0 us)
Async XLA Ops:
  0.0 34.7 %collective-permute-start.5 = (bf16[128,5120]{1,0:T(8,128)(2,1)}, bf16[128,5120]{1,0:T(8,128)(2,1)S(1)}, u32[]{:S(2)}, u32[]{:S(2)}) collective-permute-start(bf16[128,5120]{1,0:T(8,128)(2,1)} %w_ref.1), channel_id=1, source_target_pairs={{0,1},{1,0},{2,3},{3,2},{4,5},{5,4},{6,7},{7,6},{8,9},{9,8},{10,11... | collective-permute-start | bytes 3932168 | tf_op jit(solution)/shard_map/ppermute | solution.py:258
  0.5 52.2 %collective-permute-start.14 = (bf16[5120,128]{1,0:T(8,128)(2,1)}, bf16[5120,128]{1,0:T(8,128)(2,1)S(1)}, u32[]{:S(2)}, u32[]{:S(2)}) collective-permute-start(bf16[5120,128]{1,0:T(8,128)(2,1)} %refs_0_.11), channel_id=1, source_target_pairs={{0,1},{1,0},{2,3},{3,2},{4,5},{5,4},{6,7},{7,6},{8,9},{9,8},{10,11... | collective-permute-start | bytes 3932168 | tf_op jit(solution)/shard_map/ppermute | solution.py:258
  0.5 52.2 %collective-permute-start.15 = (bf16[5120,128]{1,0:T(8,128)(2,1)}, bf16[5120,128]{1,0:T(8,128)(2,1)S(1)}, u32[]{:S(2)}, u32[]{:S(2)}) collective-permute-start(bf16[5120,128]{1,0:T(8,128)(2,1)} %refs_1_.11), channel_id=1, source_target_pairs={{0,1},{1,0},{2,3},{3,2},{4,5},{5,4},{6,7},{7,6},{8,9},{9,8},{10,11... | collective-permute-start | bytes 3932168 | tf_op jit(solution)/shard_map/ppermute | solution.py:258
  1.0 51.7 %collective-permute-start.16 = (bf16[5120,128]{1,0:T(8,128)(2,1)}, bf16[5120,128]{1,0:T(8,128)(2,1)S(1)}, u32[]{:S(2)}, u32[]{:S(2)}) collective-permute-start(bf16[5120,128]{1,0:T(8,128)(2,1)} %refs_2_.11), channel_id=1, source_target_pairs={{0,1},{1,0},{2,3},{3,2},{4,5},{5,4},{6,7},{7,6},{8,9},{9,8},{10,11... | collective-permute-start | bytes 3932168 | tf_op jit(solution)/shard_map/ppermute | solution.py:258
  2.0 8.5 %collective-permute-start.1 = (bf16[64,640]{1,0:T(8,128)(2,1)S(1)}, bf16[64,640]{1,0:T(8,128)(2,1)S(1)}, u32[]{:S(2)}, u32[]{:S(2)}) collective-permute-start(bf16[64,640]{1,0:T(8,128)(2,1)S(1)} %get-tuple-element.14.top), channel_id=1, source_target_pairs={{0,4},{1,5},{2,6},{3,7},{4,0},{5,1},{6,2},{7,3},{8,12},{9,13},{10,... | collective-permute-start | bytes 245768 | tf_op jit(solution)/shard_map/ppermute | solution.py:255
  10.5 7.0 %collective-permute-start.2 = (bf16[64,640]{1,0:T(8,128)(2,1)S(1)}, bf16[64,640]{1,0:T(8,128)(2,1)S(1)}, u32[]{:S(2)}, u32[]{:S(2)}) collective-permute-start(bf16[64,640]{1,0:T(8,128)(2,1)S(1)} %get-tuple-element.15.low), channel_id=1, source_target_pairs={{0,4},{1,5},{2,6},{3,7},{4,0},{5,1},{6,2},{7,3},{8,12},{9,13},{10,... | collective-permute-start | bytes 245768 | tf_op jit(solution)/shard_map/ppermute | solution.py:255
  17.5 6.3 %collective-permute-start.4 = (bf16[64,640]{1,0:T(8,128)(2,1)S(1)}, bf16[64,640]{1,0:T(8,128)(2,1)S(1)}, u32[]{:S(2)}, u32[]{:S(2)}) collective-permute-start(bf16[64,640]{1,0:T(8,128)(2,1)S(1)} %get-tuple-element.15.low), channel_id=1, source_target_pairs={{0,6},{1,7},{2,4},{3,5},{4,2},{5,3},{6,0},{7,1},{8,14},{9,15},{10,... | collective-permute-start | bytes 245768 | tf_op jit(solution)/shard_map/ppermute | solution.py:255
  23.8 5.3 %collective-permute-start.3 = (bf16[64,640]{1,0:T(8,128)(2,1)S(1)}, bf16[64,640]{1,0:T(8,128)(2,1)S(1)}, u32[]{:S(2)}, u32[]{:S(2)}) collective-permute-start(bf16[64,640]{1,0:T(8,128)(2,1)S(1)} %collective-permute-done.1.top2), channel_id=1, source_target_pairs={{0,2},{1,3},{2,0},{3,1},{4,6},{5,7},{6,4},{7,5},{8,10},{9,11},{10,... | collective-permute-start | bytes 245768 | tf_op jit(solution)/shard_map/ppermute | solution.py:255
  29.2 5.5 %collective-permute-start = (bf16[128,640]{1,0:T(8,128)(2,1)}, bf16[128,640]{1,0:T(8,128)(2,1)S(1)}, u32[]{:S(2)}, u32[]{:S(2)}) collective-permute-start(bf16[128,640]{1,0:T(8,128)(2,1)} %whole_ref.1), channel_id=1, source_target_pairs={{0,2},{1,3},{2,0},{3,1},{4,6},{5,7},{6,4},{7,5},{8,10},{9,11},{10,... | collective-permute-start | bytes 491528 | tf_op jit(solution)/shard_map/ppermute | solution.py:255
  34.7 13.9 %copy-start.3 = (s32[4,3]{1,0:T(4,128)S(1)}, s32[4,3]{1,0:T(4,128)}, u32[]{:S(2)}) copy-start(s32[4,3]{1,0:T(4,128)} %lists_ref.1) | copy-start | bytes 148
  34.7 19.3 %copy-start.2 = (bf16[5120,128]{1,0:T(8,128)(2,1)S(1)}, bf16[5120,128]{1,0:T(8,128)(2,1)}, u32[]{:S(2)}) copy-start(bf16[5120,128]{1,0:T(8,128)(2,1)} %refs_2_.11) | copy-start | bytes 3932164
  35.2 1.6 %collective-permute-start.6 = (f32[128,256]{1,0:T(8,128)S(1)}, f32[128,256]{1,0:T(8,128)S(1)}, u32[]{:S(2)}, u32[]{:S(2)}) collective-permute-start(f32[128,256]{1,0:T(8,128)S(1)} %shard_map.93.own_ref), channel_id=1, source_target_pairs={{0,1},{1,0},{2,3},{3,2},{4,5},{5,4},{6,7},{7,6},{8,9},{9,8},{10,11... | collective-permute-start | bytes 393224 | tf_op jit(solution)/shard_map/ppermute | solution.py:258
  35.3 5.2 %collective-permute-start.10 = (bf16[128,384]{1,0:T(8,128)(2,1)S(1)}, bf16[128,384]{1,0:T(8,128)(2,1)S(1)}, u32[]{:S(2)}, u32[]{:S(2)}) collective-permute-start(bf16[128,384]{1,0:T(8,128)(2,1)S(1)} %get-tuple-element.19.refs_0_), channel_id=1, source_target_pairs={{0,8},{8,0},{16,24},{24,16},{1,9},{9,1},{17,25},{25,17},{2,10},{10... | collective-permute-start | bytes 294920 | tf_op jit(solution)/shard_map/ppermute | solution.py:261
  36.9 6.1 %collective-permute-start.11 = (bf16[128,384]{1,0:T(8,128)(2,1)S(1)}, bf16[128,384]{1,0:T(8,128)(2,1)S(1)}, u32[]{:S(2)}, u32[]{:S(2)}) collective-permute-start(bf16[128,384]{1,0:T(8,128)(2,1)S(1)} %get-tuple-element.19.refs_0_), channel_id=1, source_target_pairs={{0,16},{8,24},{16,0},{24,8},{1,17},{9,25},{17,1},{25,9},{2,18},{10... | collective-permute-start | bytes 294920 | tf_op jit(solution)/shard_map/ppermute | solution.py:261
  40.5 6.7 %collective-permute-start.12 = (bf16[128,384]{1,0:T(8,128)(2,1)S(1)}, bf16[128,384]{1,0:T(8,128)(2,1)S(1)}, u32[]{:S(2)}, u32[]{:S(2)}) collective-permute-start(bf16[128,384]{1,0:T(8,128)(2,1)S(1)} %get-tuple-element.19.refs_0_), channel_id=1, source_target_pairs={{0,24},{8,16},{16,8},{24,0},{1,25},{9,17},{17,9},{25,1},{2,26},{10... | collective-permute-start | bytes 294920 | tf_op jit(solution)/shard_map/ppermute | solution.py:261
  43.0 4.3 %collective-permute-start.7 = (bf16[128,256]{1,0:T(8,128)(2,1)S(1)}, bf16[128,256]{1,0:T(8,128)(2,1)S(1)}, u32[]{:S(2)}, u32[]{:S(2)}) collective-permute-start(bf16[128,256]{1,0:T(8,128)(2,1)S(1)} %get-tuple-element.18), channel_id=1, source_target_pairs={{0,8},{1,17},{2,10},{3,19},{4,12},{5,21},{6,14},{7,23},{8,0},{9,25... | collective-permute-start | bytes 196616 | tf_op jit(solution)/shard_map/ppermute | solution.py:265
  47.2 4.9 %collective-permute-start.8 = (bf16[128,256]{1,0:T(8,128)(2,1)S(1)}, bf16[128,256]{1,0:T(8,128)(2,1)S(1)}, u32[]{:S(2)}, u32[]{:S(2)}) collective-permute-start(bf16[128,256]{1,0:T(8,128)(2,1)S(1)} %collective-permute-done.7.beside), channel_id=1, source_target_pairs={{0,1},{1,0},{2,3},{3,2},{4,5},{5,4},{6,7},{7,6},{8,9},{9,8},{10,11... | collective-permute-start | bytes 196616 | tf_op jit(solution)/shard_map/ppermute | solution.py:258
  47.2 6.7 %copy-start = (bf16[5120,128]{1,0:T(8,128)(2,1)S(1)}, bf16[5120,128]{1,0:T(8,128)(2,1)}, u32[]{:S(2)}) copy-start(bf16[5120,128]{1,0:T(8,128)(2,1)} %refs_0_.11) | copy-start | bytes 3932164
  47.2 6.7 %copy-start.1 = (bf16[5120,128]{1,0:T(8,128)(2,1)S(1)}, bf16[5120,128]{1,0:T(8,128)(2,1)}, u32[]{:S(2)}) copy-start(bf16[5120,128]{1,0:T(8,128)(2,1)} %refs_1_.11) | copy-start | bytes 3932164
  47.2 4.9 %collective-permute-start.9 = (bf16[128,128]{1,0:T(8,128)(2,1)S(1)}, bf16[128,128]{1,0:T(8,128)(2,1)S(1)}, u32[]{:S(2)}, u32[]{:S(2)}) collective-permute-start(bf16[128,128]{1,0:T(8,128)(2,1)S(1)} %get-tuple-element.17.grad_ref.own), channel_id=1, source_target_pairs={{0,24},{8,16},{16,8},{24,0},{1,25},{9,17},{17,9},{25,1},{2,26},{10... | collective-permute-start | bytes 98312 | tf_op jit(solution)/shard_map/ppermute | solution.py:261
  52.6 1.4 %collective-permute-start.13 = (bf16[128,384]{1,0:T(8,128)(2,1)S(1)}, bf16[128,384]{1,0:T(8,128)(2,1)S(1)}, u32[]{:S(2)}, u32[]{:S(2)}) collective-permute-start(bf16[128,384]{1,0:T(8,128)(2,1)S(1)} %shard_map.97.own_ref), channel_id=1, source_target_pairs={{0,1},{1,0},{2,3},{3,2},{4,5},{5,4},{6,7},{7,6},{8,9},{9,8},{10,11... | collective-permute-start | bytes 294920 | tf_op jit(solution)/shard_map/ppermute | solution.py:258
  54.3 5.7 %collective-permute-start.18 = (bf16[384,128]{1,0:T(8,128)(2,1)S(1)}, bf16[384,128]{1,0:T(8,128)(2,1)S(1)}, u32[]{:S(2)}, u32[]{:S(2)}) collective-permute-start(bf16[384,128]{1,0:T(8,128)(2,1)S(1)} %shard_map.100), channel_id=1, source_target_pairs={{0,2},{1,3},{2,0},{3,1},{4,6},{5,7},{6,4},{7,5},{8,10},{9,11},{10,... | collective-permute-start | bytes 294920 | tf_op jit(solution)/shard_map/ppermute | solution.py:255
  54.8 17.4 %collective-permute-start.17 = (bf16[640,128]{1,0:T(8,128)(2,1)S(1)}, bf16[640,128]{1,0:T(8,128)(2,1)S(1)}, u32[]{:S(2)}, u32[]{:S(2)}) collective-permute-start(bf16[640,128]{1,0:T(8,128)(2,1)S(1)} %shard_map.99), channel_id=1, source_target_pairs={{0,2},{1,3},{2,0},{3,1},{4,6},{5,7},{6,4},{7,5},{8,10},{9,11},{10,... | collective-permute-start | bytes 491528 | tf_op jit(solution)/shard_map/ppermute | solution.py:255
  60.3 11.9 %collective-permute-start.19 = (bf16[384,128]{1,0:T(8,128)(2,1)S(1)}, bf16[384,128]{1,0:T(8,128)(2,1)S(1)}, u32[]{:S(2)}, u32[]{:S(2)}) collective-permute-start(bf16[384,128]{1,0:T(8,128)(2,1)S(1)} %shard_map.101), channel_id=1, source_target_pairs={{0,4},{1,5},{2,6},{3,7},{4,0},{5,1},{6,2},{7,3},{8,12},{9,13},{10,... | collective-permute-start | bytes 294920 | tf_op jit(solution)/shard_map/ppermute | solution.py:255
  61.3 6.5 %collective-permute-start.21 = (bf16[256,128]{1,0:T(8,128)(2,1)S(1)}, bf16[256,128]{1,0:T(8,128)(2,1)S(1)}, u32[]{:S(2)}, u32[]{:S(2)}) collective-permute-start(bf16[256,128]{1,0:T(8,128)(2,1)S(1)} %shard_map.103), channel_id=1, source_target_pairs={{0,6},{1,7},{2,4},{3,5},{4,2},{5,3},{6,0},{7,1},{8,14},{9,15},{10,... | collective-permute-start | bytes 196616 | tf_op jit(solution)/shard_map/ppermute | solution.py:255
  63.5 8.7 %collective-permute-start.20 = (bf16[256,128]{1,0:T(8,128)(2,1)S(1)}, bf16[256,128]{1,0:T(8,128)(2,1)S(1)}, u32[]{:S(2)}, u32[]{:S(2)}) collective-permute-start(bf16[256,128]{1,0:T(8,128)(2,1)S(1)} %shard_map.102), channel_id=1, source_target_pairs={{0,4},{1,5},{2,6},{3,7},{4,0},{5,1},{6,2},{7,3},{8,12},{9,13},{10,... | collective-permute-start | bytes 196616 | tf_op jit(solution)/shard_map/ppermute | solution.py:255

commit v5 on v4

--- a/solution.py
+++ b/solution.py
@@ -9,6 +9,7 @@
 
 
 TILE = 128
+EARLY = (0, 1, 2)
 CONTRACT_LAST = (((1,), (1,)), ((), ()))
 CONTRACT_FIRST = (((0,), (0,)), ((), ()))
 VMEM = pl.BlockSpec(memory_space=pltpu.VMEM)
@@ -72,7 +73,16 @@
         )
         for place, part in enumerate((query_ref, key_ref, value_ref))
     ]
-    copies.append(pltpu.make_async_copy(w_ref, w_out_ref, sems.at[3]))
+    cols = w_out_ref.shape[1] // 4
+    for step in range(4):
+        start = pl.multiple_of((lax.axis_index("tp") ^ (2 * step)) * cols, 128)
+        copies.append(
+            pltpu.make_async_copy(
+                w_ref.at[:, pl.ds(start, cols)],
+                w_out_ref.at[:, step * cols : (step + 1) * cols],
+                sems.at[3 + step],
+            )
+        )
     for copy in copies:
         copy.start()
     for copy in copies:
@@ -92,20 +102,18 @@
         copy.wait()
 
 
-def attn_grad_kernel(cols, top, low, near, top2, low2, top3, low3, own_w, mate_w, out_ref):
+def attn_grad_kernel(cols, steps, *refs):
     index = lax.axis_index("tp")
-    blocks = [
-        jnp.concatenate([top[...], low[...]], axis=0),
-        near[...],
-        jnp.concatenate([top2[...], low2[...]], axis=0),
-        jnp.concatenate([top3[...], low3[...]], axis=0),
-    ]
-    total = None
-    for step, block in enumerate(blocks):
+    count = sum(1 if step == 1 else 2 for step in steps)
+    parts, own_w, mate_w, out_ref = list(refs[:count]), refs[count], refs[count + 1], refs[-1]
+    total = refs[-2][...] if len(refs) > count + 3 else None
+    for step in steps:
         start = pl.multiple_of((index ^ (2 * step)) * cols, 128)
         weight = jnp.concatenate(
-            [own_w[:, pl.ds(start, cols)], mate_w[:, pl.ds(start, cols)]], axis=0
+            [own_w[:, step * cols : (step + 1) * cols], mate_w[:, pl.ds(start, cols)]], axis=0
         )
+        pieces = [parts.pop(0)[...] for _ in range(1 if step == 1 else 2)]
+        block = jnp.concatenate(pieces, axis=0)
         term = dot_f32(block, weight, CONTRACT_LAST)
         total = term if total is None else total + term
     out_ref[...] = total
@@ -190,18 +198,29 @@
     )
 
 
+def project_own_kernel(block, own_ref, *refs):
+    weights, out_ref = refs[:3], refs[3]
+    size = own_ref.shape[1] // 3
+    for step in range(out_ref.shape[0] // block):
+        start = pl.multiple_of((lax.axis_index("tp") ^ (2 * step)) * block, 16)
+        total = None
+        for place, weight in enumerate(weights):
+            part = own_ref[:, place * size : (place + 1) * size]
+            term = dot_f32(weight[pl.ds(start, block), :], part, CONTRACT_LAST)
+            total = term if total is None else total + term
+        out_ref[step * block : (step + 1) * block, :] = total
+
+
 def project_kernel(block, step, first, own_ref, mate_ref, *refs):
-    weights, out_ref = refs[:6], refs[-1]
+    weights, out_ref = refs[:3], refs[-1]
     rows = out_ref.shape[0]
     start = pl.multiple_of((lax.axis_index("tp") ^ (2 * step)) * block + first, 16)
-    size = own_ref.shape[1] // 3
-    total = None
+    size = mate_ref.shape[1] // 3
+    total = own_ref[step * block + first : step * block + first + rows, :]
     for place, weight in enumerate(weights):
-        grads = own_ref if place < 3 else mate_ref
-        part = grads[:, (place % 3) * size : (place % 3 + 1) * size]
-        term = dot_f32(weight[pl.ds(start, rows), :], part, CONTRACT_LAST)
-        total = term if total is None else total + term
-    for fed in refs[6:-1]:
+        part = mate_ref[:, place * size : (place + 1) * size]
+        total = total + dot_f32(weight[pl.ds(start, rows), :], part, CONTRACT_LAST)
+    for fed in refs[3:-1]:
         total = total + fed[...].astype(jnp.float32)
     out_ref[...] = total.astype(out_ref.dtype)
 
@@ -249,7 +268,7 @@
     rows, cols = grad_out.shape
     size = query_proj.shape[1]
     half, full = jnp.bfloat16, jnp.float32
-    cut, feature_cut = rows // 2, cols * 3 // 5 // 16 * 16
+    cut, feature_cut = rows // 2, 448
 
     def to_chip(x, step):
         return lax.ppermute(x, "tp", [(t, t ^ (2 * step)) for t in range(8)])
@@ -275,7 +294,7 @@
     top3 = to_chip(top2, 1)
     pack, near_out = call(
         pack_kernel, [query_proj, key_proj, value_proj, w_out],
-        [((rows, 3 * size), half), (w_out.shape, half)], raw=True, sems=4,
+        [((rows, 3 * size), half), ((size, 4 * cols), half)], raw=True, sems=7,
     )
     packs = [pack] + [to_slab(pack, turn) for turn in range(1, slabs)]
     mate_out = to_mate(w_out)
@@ -286,9 +305,15 @@
         [tile_keys, *packs],
         [((rows, slabs * rows), full), ((slabs * rows, rows), full), ((slabs * rows, size), full)],
     )
+    (early,) = call(
+        functools.partial(attn_grad_kernel, cols, EARLY),
+        [top, low, near] + ([top2, low2] if 2 in EARLY else []) + [near_out, mate_out],
+        [((rows, 2 * size), full)],
+    )
+    late = tuple(step for step in range(4) if step not in EARLY)
     (part,) = call(
-        functools.partial(attn_grad_kernel, cols),
-        [top, low, near, top2, low2, top3, low3, near_out, mate_out],
+        functools.partial(attn_grad_kernel, cols, late),
+        ([] if 2 in EARLY else [top2, low2]) + [top3, low3, near_out, mate_out, early],
         [((rows, 2 * size), full)],
     )
     both, grad = call(
@@ -309,12 +334,15 @@
         [((rows, 3 * size), half)],
     )
     mate_grads = to_mate(own_grads)
+    (own_sums,) = call(
+        functools.partial(project_own_kernel, cols), [own_grads, *own_w], [((4 * cols, rows), full)]
+    )
 
 
     def project(step, first, count, kind, *fed):
         (part,) = call(
             functools.partial(project_kernel, cols, step, first),
-            [own_grads, mate_grads, *own_w, *mate_w, *fed],
+            [own_sums, mate_grads, *mate_w, *fed],
             [((count, rows), kind)],
         )
         return part

time: 73.2 us -> 68 us (0.929)
  waiting for transfers between devices: 41.8 us -> 34.5 us
  starting transfers between devices: 22.4 us -> 24.3 us
    ppermute x10, waiting for transfers between devices: 33.6 us -> 27.7 us  [to_chip(): return lax.ppermute(x, 'tp', [(t, t ^ 2 * step) for t in range(8)])]
    ppermute x1, waiting for transfers between devices: 3.73 us -> 2.77 us  [to_beside(): return lax.ppermute(x, ('ctx', 'tp'), pairs)]
    ppermute x1, starting transfers between devices: 0.54 us -> 1.5 us  [to_beside(): return lax.ppermute(x, ('ctx', 'tp'), pairs)]
    ppermute x7, waiting for transfers between devices: 1.27 us -> 0.46 us  [to_mate(): return lax.ppermute(x, 'tp', [(t, t ^ 1) for t in range(8)])]
    pallas_call x14 -> x16, Pallas kernels: 8.51 us -> 8.72 us  [call(): pl.pallas_call(kernel, in_specs=[SMEM if flag else there for flag in ints...]
  transfers between devices with their start and end apart: 22 -> 22, of which waited for: 12 -> 11; matrix products, arithmetic and copies ran while one was open for 0% -> 0% of each run, Pallas kernels for 10% -> 11%
where the time goes in v5:
time: 68 us; the launch traced here: 67.8 us
  waiting for transfers between devices  34.5 us (51%)
  starting transfers between devices  24.3 us (36%)
  Pallas kernels  8.72 us (13%)
    ppermute x10, waiting for transfers between devices, to_chip(): return lax.ppermute(x, 'tp', [(t, t ^ 2 * step) for t in range(8)])  27.7 us
    ppermute x10, starting transfers between devices, to_chip(): return lax.ppermute(x, 'tp', [(t, t ^ 2 * step) for t in range(8)])  14.5 us
    pallas_call x16, Pallas kernels, call(): pl.pallas_call(kernel, in_specs=[SMEM if flag else there for flag in ints...  8.72 us
    ppermute x4, starting transfers between devices, to_slab(): return lax.ppermute(x, 'ctx', [(c, c ^ turn) for c in range(slabs)])  7.05 us
    ppermute x4, waiting for transfers between devices, to_slab(): return lax.ppermute(x, 'ctx', [(c, c ^ turn) for c in range(slabs)])  3.65 us
    ppermute x1, waiting for transfers between devices, to_beside(): return lax.ppermute(x, ('ctx', 'tp'), pairs)  2.77 us
    ppermute x1, starting transfers between devices, to_beside(): return lax.ppermute(x, ('ctx', 'tp'), pairs)  1.5 us
  transfers between devices with their start and end apart: 22, of which 11 were waited for; matrix products, arithmetic and copies ran while one was open for 0% of the time, Pallas kernels for 11%

profile of v5, /device:TPU:0, one launch (start us, length us, event | category | flops | bytes accessed | tf_op | source)
XLA Modules:
  0.0 67.8 jit_solution(2449683187108717079)
XLA Ops:
  0.0 0.5 collective-permute-start.3
  0.5 0.0 collective-permute-start.14
  0.5 0.5 collective-permute-start.15
  1.0 0.0 collective-permute-start.16
  1.0 0.9 %shard_map.91 = (bf16[64,640]{1,0:T(8,128)(2,1)S(1)}, bf16[64,640]{1,0:T(8,128)(2,1)S(1)}) custom-call(bf16[128,640]{1,0:T(8,128)(2,1)} %whole_ref.1), custom_call_target="tpu_custom_call" | custom-call | tf_op jit(solution)/shard_map/pallas_call | solution.py:243
  2.0 4.1 %collective-permute-start = (bf16[64,640]{1,0:T(8,128)(2,1)S(1)}, bf16[64,640]{1,0:T(8,128)(2,1)S(1)}, u32[]{:S(2)}, u32[]{:S(2)}) collective-permute-start(bf16[64,640]{1,0:T(8,128)(2,1)S(1)} %get-tuple-element.14.refs_0_), channel_id=1, source_target_pairs={{0,4},{1,5},{2,6},{3,7},{4,0},{5,1},{6,2},{7,3},{8,12},{9,13},{10,... | collective-permute-start | bytes 245768 | tf_op jit(solution)/shard_map/ppermute | solution.py:274
  6.1 4.4 %collective-permute-done.refs_3_ = bf16[64,640]{1,0:T(8,128)(2,1)S(1)} collective-permute-done((bf16[64,640]{1,0:T(8,128)(2,1)S(1)}, bf16[64,640]{1,0:T(8,128)(2,1)S(1)}, u32[]{:S(2)}, u32[]{:S(2)}) %collective-permute-start) | collective-permute-done | bytes 81952 | tf_op jit(solution)/shard_map/ppermute | solution.py:274
  10.5 1.0 %collective-permute-start.5 = (bf16[64,640]{1,0:T(8,128)(2,1)S(1)}, bf16[64,640]{1,0:T(8,128)(2,1)S(1)}, u32[]{:S(2)}, u32[]{:S(2)}) collective-permute-start(bf16[64,640]{1,0:T(8,128)(2,1)S(1)} %get-tuple-element.15.refs_1_), channel_id=1, source_target_pairs={{0,4},{1,5},{2,6},{3,7},{4,0},{5,1},{6,2},{7,3},{8,12},{9,13},{10,... | collective-permute-start | bytes 245768 | tf_op jit(solution)/shard_map/ppermute | solution.py:274
  11.5 6.1 %collective-permute-done.5.refs_4_ = bf16[64,640]{1,0:T(8,128)(2,1)S(1)} collective-permute-done((bf16[64,640]{1,0:T(8,128)(2,1)S(1)}, bf16[64,640]{1,0:T(8,128)(2,1)S(1)}, u32[]{:S(2)}, u32[]{:S(2)}) %collective-permute-start.5) | collective-permute-done | bytes 81952 | tf_op jit(solution)/shard_map/ppermute | solution.py:274
  17.5 0.0 collective-permute-start.4
  17.5 5.5 %collective-permute-done.4.refs_2_ = bf16[128,640]{1,0:T(8,128)(2,1)S(1)} collective-permute-done((bf16[128,640]{1,0:T(8,128)(2,1)}, bf16[128,640]{1,0:T(8,128)(2,1)S(1)}, u32[]{:S(2)}, u32[]{:S(2)}) %collective-permute-start.4) | collective-permute-done | bytes 163872 | tf_op jit(solution)/shard_map/ppermute | solution.py:274
  23.0 2.1 %collective-permute-start.2 = (bf16[64,640]{1,0:T(8,128)(2,1)S(1)}, bf16[64,640]{1,0:T(8,128)(2,1)S(1)}, u32[]{:S(2)}, u32[]{:S(2)}) collective-permute-start(bf16[64,640]{1,0:T(8,128)(2,1)S(1)} %get-tuple-element.15.refs_1_), channel_id=1, source_target_pairs={{0,6},{1,7},{2,4},{3,5},{4,2},{5,3},{6,0},{7,1},{8,14},{9,15},{10,... | collective-permute-start | bytes 245768 | tf_op jit(solution)/shard_map/ppermute | solution.py:274
  25.1 0.0 collective-permute-done.3.refs_6_.refs_3_
  25.1 0.0 collective-permute-start.1
  25.1 1.3 %shard_map.92 = (bf16[128,384]{1,0:T(8,128)(2,1)S(1)}, bf16[128,2560]{1,0:T(8,128)(2,1)S(1)}) custom-call(bf16[128,128]{1,0:T(8,128)(2,1)} %query_ref.1, bf16[128,128]{1,0:T(8,128)(2,1)} %key_ref.1, bf16[128,128]{1,0:T(8,128)(2,1)} %value_ref.1, bf16[128,5120]{1,0:T(8,128)(2,1)} %w_ref.1), custom_call_target="tpu_custom_call" | custom-call | tf_op jit(solution)/shard_map/pallas_call | solution.py:243
  26.4 0.4 shard_map.93.refs_4_
  26.8 0.0 copy-start.3
  26.8 2.5 %collective-permute-done.2.refs_1_ = bf16[64,640]{1,0:T(8,128)(2,1)S(1)} collective-permute-done((bf16[64,640]{1,0:T(8,128)(2,1)S(1)}, bf16[64,640]{1,0:T(8,128)(2,1)S(1)}, u32[]{:S(2)}, u32[]{:S(2)}) %collective-permute-start.2) | collective-permute-done | bytes 81952 | tf_op jit(solution)/shard_map/ppermute | solution.py:274
  29.3 0.8 %collective-permute-done.1.refs_0_ = bf16[64,640]{1,0:T(8,128)(2,1)S(1)} collective-permute-done((bf16[64,640]{1,0:T(8,128)(2,1)S(1)}, bf16[64,640]{1,0:T(8,128)(2,1)S(1)}, u32[]{:S(2)}, u32[]{:S(2)}) %collective-permute-start.1) | collective-permute-done | bytes 81952 | tf_op jit(solution)/shard_map/ppermute | solution.py:274
  30.2 0.2 shard_map.94.own_ref
  30.4 0.1 collective-permute-start.6
  30.5 2.5 %collective-permute-start.12 = (bf16[128,384]{1,0:T(8,128)(2,1)S(1)}, bf16[128,384]{1,0:T(8,128)(2,1)S(1)}, u32[]{:S(2)}, u32[]{:S(2)}) collective-permute-start(bf16[128,384]{1,0:T(8,128)(2,1)S(1)} %get-tuple-element.19.refs_0_), channel_id=1, source_target_pairs={{0,24},{8,16},{16,8},{24,0},{1,25},{9,17},{17,9},{25,1},{2,26},{10... | collective-permute-start | bytes 294920 | tf_op jit(solution)/shard_map/ppermute | solution.py:280
  33.0 0.0 collective-permute-done.6.mate_ref
  33.0 0.5 collective-permute-start.11
  33.5 3.1 %collective-permute-done.12.refs_3_ = bf16[128,384]{1,0:T(8,128)(2,1)S(1)} collective-permute-done((bf16[128,384]{1,0:T(8,128)(2,1)S(1)}, bf16[128,384]{1,0:T(8,128)(2,1)S(1)}, u32[]{:S(2)}, u32[]{:S(2)}) %collective-permute-start.12) | collective-permute-done | bytes 98336 | tf_op jit(solution)/shard_map/ppermute | solution.py:280
  36.7 1.5 %collective-permute-start.10 = (bf16[128,384]{1,0:T(8,128)(2,1)S(1)}, bf16[128,384]{1,0:T(8,128)(2,1)S(1)}, u32[]{:S(2)}, u32[]{:S(2)}) collective-permute-start(bf16[128,384]{1,0:T(8,128)(2,1)S(1)} %get-tuple-element.19.refs_0_), channel_id=1, source_target_pairs={{0,8},{8,0},{16,24},{24,16},{1,9},{9,1},{17,25},{25,17},{2,10},{10... | collective-permute-start | bytes 294920 | tf_op jit(solution)/shard_map/ppermute | solution.py:280
  38.2 0.5 collective-permute-done.11.refs_2_
  38.7 1.5 %collective-permute-start.7 = (bf16[128,256]{1,0:T(8,128)(2,1)S(1)}, bf16[128,256]{1,0:T(8,128)(2,1)S(1)}, u32[]{:S(2)}, u32[]{:S(2)}) collective-permute-start(bf16[128,256]{1,0:T(8,128)(2,1)S(1)} %get-tuple-element.18), channel_id=1, source_target_pairs={{0,8},{1,17},{2,10},{3,19},{4,12},{5,21},{6,14},{7,23},{8,0},{9,25... | collective-permute-start | bytes 196616 | tf_op jit(solution)/shard_map/ppermute | solution.py:284
  40.2 2.8 %collective-permute-done.7.beside = bf16[128,256]{1,0:T(8,128)(2,1)S(1)} collective-permute-done((bf16[128,256]{1,0:T(8,128)(2,1)S(1)}, bf16[128,256]{1,0:T(8,128)(2,1)S(1)}, u32[]{:S(2)}, u32[]{:S(2)}) %collective-permute-start.7) | collective-permute-done | bytes 65568 | tf_op jit(solution)/shard_map/ppermute | solution.py:284
  43.0 0.0 collective-permute-start.8
  43.0 0.0 collective-permute-done.10.refs_1_
  43.0 0.0 copy-start.1
  43.0 2.5 %collective-permute-start.9 = (bf16[128,128]{1,0:T(8,128)(2,1)S(1)}, bf16[128,128]{1,0:T(8,128)(2,1)S(1)}, u32[]{:S(2)}, u32[]{:S(2)}) collective-permute-start(bf16[128,128]{1,0:T(8,128)(2,1)S(1)} %get-tuple-element.17.grad_ref.own), channel_id=1, source_target_pairs={{0,24},{8,16},{16,8},{24,0},{1,25},{9,17},{17,9},{25,1},{2,26},{10... | collective-permute-start | bytes 98312 | tf_op jit(solution)/shard_map/ppermute | solution.py:280
  45.5 0.0 copy-done.3
  45.5 2.1 %shard_map.96 = (f32[128,512]{1,0:T(8,128)S(1)}, f32[512,128]{1,0:T(8,128)S(1)}, f32[512,128]{1,0:T(8,128)S(1)}) custom-call(s32[4,3]{1,0:T(4,128)S(1)} %copy-done.3, bf16[128,384]{1,0:T(8,128)(2,1)S(1)} %get-tuple-element.19.refs_0_, bf16[128,384]{1,0:T(8,128)(2,1)S(1)} %collective-permute-done.10.refs_1_, ...), custom_call_target="tpu_custom_call" | custom-call | tf_op jit(solution)/shard_map/pallas_call | solution.py:243
  47.6 0.3 shard_map.97.refs_4_
  47.9 0.0 collective-permute-done.9.across
  47.9 0.0 collective-permute-done.8.swapped
  47.9 0.5 shard_map.98.own_ref
  48.4 0.2 collective-permute-start.13
  48.6 0.0 copy-done.2
  48.6 0.0 copy-done
  48.6 0.7 shard_map.99.own_ref
  49.3 0.0 collective-permute-done.14.refs_0_
  49.3 0.0 collective-permute-done.15.refs_1_
  49.3 0.0 collective-permute-done.16.refs_2_
  49.3 0.4 collective-permute-done.13.mate_ref
  49.8 0.3 shard_map.102
  50.0 0.3 collective-permute-start.18
  50.4 0.3 shard_map.101
  50.7 1.8 %collective-permute-start.17 = (bf16[640,128]{1,0:T(8,128)(2,1)S(1)}, bf16[640,128]{1,0:T(8,128)(2,1)S(1)}, u32[]{:S(2)}, u32[]{:S(2)}) collective-permute-start(bf16[640,128]{1,0:T(8,128)(2,1)S(1)} %shard_map.101), channel_id=1, source_target_pairs={{0,2},{1,3},{2,0},{3,1},{4,6},{5,7},{6,4},{7,5},{8,10},{9,11},{10,... | collective-permute-start | bytes 491528 | tf_op jit(solution)/shard_map/ppermute | solution.py:274
  52.5 3.6 %collective-permute-done.18.refs_3_ = bf16[448,128]{1,0:T(8,128)(2,1)S(1)} collective-permute-done((bf16[448,128]{1,0:T(8,128)(2,1)S(1)}, bf16[448,128]{1,0:T(8,128)(2,1)S(1)}, u32[]{:S(2)}, u32[]{:S(2)}) %collective-permute-start.18) | collective-permute-done | bytes 114720 | tf_op jit(solution)/shard_map/ppermute | solution.py:274
  56.1 0.3 shard_map.103
  56.4 0.6 collective-permute-start.19
  57.0 0.2 shard_map.104
  57.2 2.4 %collective-permute-start.20 = (bf16[192,128]{1,0:T(8,128)(2,1)S(1)}, bf16[192,128]{1,0:T(8,128)(2,1)S(1)}, u32[]{:S(2)}, u32[]{:S(2)}) collective-permute-start(bf16[192,128]{1,0:T(8,128)(2,1)S(1)} %shard_map.104), channel_id=1, source_target_pairs={{0,4},{1,5},{2,6},{3,7},{4,0},{5,1},{6,2},{7,3},{8,12},{9,13},{10,... | collective-permute-start | bytes 147464 | tf_op jit(solution)/shard_map/ppermute | solution.py:274
  59.6 0.2 shard_map.105
  59.9 2.1 %collective-permute-start.21 = (bf16[192,128]{1,0:T(8,128)(2,1)S(1)}, bf16[192,128]{1,0:T(8,128)(2,1)S(1)}, u32[]{:S(2)}, u32[]{:S(2)}) collective-permute-start(bf16[192,128]{1,0:T(8,128)(2,1)S(1)} %shard_map.105), channel_id=1, source_target_pairs={{0,6},{1,7},{2,4},{3,5},{4,2},{5,3},{6,0},{7,1},{8,14},{9,15},{10,... | collective-permute-start | bytes 147464 | tf_op jit(solution)/shard_map/ppermute | solution.py:274
  61.9 0.3 shard_map.100.own_ref
  62.2 4.8 %collective-permute-done.20.low2 = bf16[192,128]{1,0:T(8,128)(2,1)S(1)} collective-permute-done((bf16[192,128]{1,0:T(8,128)(2,1)S(1)}, bf16[192,128]{1,0:T(8,128)(2,1)S(1)}, u32[]{:S(2)}, u32[]{:S(2)}) %collective-permute-start.20) | collective-permute-done | bytes 49184 | tf_op jit(solution)/shard_map/ppermute | solution.py:274
  67.0 0.0 collective-permute-done.21.low3
  67.0 0.0 collective-permute-done.17.near
  67.0 0.0 collective-permute-done.19.top2
  67.0 0.8 %shard_map.106 = f32[640,128]{1,0:T(8,128)} custom-call(f32[640,128]{1,0:T(8,128)S(1)} %shard_map.100.own_ref, bf16[640,128]{1,0:T(8,128)(2,1)S(1)} %collective-permute-done.17.near, bf16[448,128]{1,0:T(8,128)(2,1)S(1)} %collective-permute-done.19.top2, bf16[192,128]{1,0:T(8,128)(2,1)S(1)} %collective-permute-done.20.low2, ...), custom_call_target="tpu_custom_call" | custom-call | tf_op jit(solution)/shard_map/pallas_call | solution.py:243
  (4 shorter events, 0.0 us)
Async XLA Ops:
  0.0 25.1 %collective-permute-start.3 = (bf16[128,5120]{1,0:T(8,128)(2,1)}, bf16[128,5120]{1,0:T(8,128)(2,1)S(1)}, u32[]{:S(2)}, u32[]{:S(2)}) collective-permute-start(bf16[128,5120]{1,0:T(8,128)(2,1)} %w_ref.1), channel_id=1, source_target_pairs={{0,1},{1,0},{2,3},{3,2},{4,5},{5,4},{6,7},{7,6},{8,9},{9,8},{10,11... | collective-permute-start | bytes 3932168 | tf_op jit(solution)/shard_map/ppermute | solution.py:277
  0.5 48.8 %collective-permute-start.14 = (bf16[5120,128]{1,0:T(8,128)(2,1)}, bf16[5120,128]{1,0:T(8,128)(2,1)S(1)}, u32[]{:S(2)}, u32[]{:S(2)}) collective-permute-start(bf16[5120,128]{1,0:T(8,128)(2,1)} %refs_0_.1), channel_id=1, source_target_pairs={{0,1},{1,0},{2,3},{3,2},{4,5},{5,4},{6,7},{7,6},{8,9},{9,8},{10,11... | collective-permute-start | bytes 3932168 | tf_op jit(solution)/shard_map/ppermute | solution.py:277
  0.5 48.8 %collective-permute-start.15 = (bf16[5120,128]{1,0:T(8,128)(2,1)}, bf16[5120,128]{1,0:T(8,128)(2,1)S(1)}, u32[]{:S(2)}, u32[]{:S(2)}) collective-permute-start(bf16[5120,128]{1,0:T(8,128)(2,1)} %refs_1_.1), channel_id=1, source_target_pairs={{0,1},{1,0},{2,3},{3,2},{4,5},{5,4},{6,7},{7,6},{8,9},{9,8},{10,11... | collective-permute-start | bytes 3932168 | tf_op jit(solution)/shard_map/ppermute | solution.py:277
  1.0 48.3 %collective-permute-start.16 = (bf16[5120,128]{1,0:T(8,128)(2,1)}, bf16[5120,128]{1,0:T(8,128)(2,1)S(1)}, u32[]{:S(2)}, u32[]{:S(2)}) collective-permute-start(bf16[5120,128]{1,0:T(8,128)(2,1)} %refs_2_.1), channel_id=1, source_target_pairs={{0,1},{1,0},{2,3},{3,2},{4,5},{5,4},{6,7},{7,6},{8,9},{9,8},{10,11... | collective-permute-start | bytes 3932168 | tf_op jit(solution)/shard_map/ppermute | solution.py:277
  2.0 8.5 %collective-permute-start = (bf16[64,640]{1,0:T(8,128)(2,1)S(1)}, bf16[64,640]{1,0:T(8,128)(2,1)S(1)}, u32[]{:S(2)}, u32[]{:S(2)}) collective-permute-start(bf16[64,640]{1,0:T(8,128)(2,1)S(1)} %get-tuple-element.14.refs_0_), channel_id=1, source_target_pairs={{0,4},{1,5},{2,6},{3,7},{4,0},{5,1},{6,2},{7,3},{8,12},{9,13},{10,... | collective-permute-start | bytes 245768 | tf_op jit(solution)/shard_map/ppermute | solution.py:274
  10.5 7.0 %collective-permute-start.5 = (bf16[64,640]{1,0:T(8,128)(2,1)S(1)}, bf16[64,640]{1,0:T(8,128)(2,1)S(1)}, u32[]{:S(2)}, u32[]{:S(2)}) collective-permute-start(bf16[64,640]{1,0:T(8,128)(2,1)S(1)} %get-tuple-element.15.refs_1_), channel_id=1, source_target_pairs={{0,4},{1,5},{2,6},{3,7},{4,0},{5,1},{6,2},{7,3},{8,12},{9,13},{10,... | collective-permute-start | bytes 245768 | tf_op jit(solution)/shard_map/ppermute | solution.py:274
  17.5 5.5 %collective-permute-start.4 = (bf16[128,640]{1,0:T(8,128)(2,1)}, bf16[128,640]{1,0:T(8,128)(2,1)S(1)}, u32[]{:S(2)}, u32[]{:S(2)}) collective-permute-start(bf16[128,640]{1,0:T(8,128)(2,1)} %whole_ref.1), channel_id=1, source_target_pairs={{0,2},{1,3},{2,0},{3,1},{4,6},{5,7},{6,4},{7,5},{8,10},{9,11},{10,... | collective-permute-start | bytes 491528 | tf_op jit(solution)/shard_map/ppermute | solution.py:274
  23.0 6.3 %collective-permute-start.2 = (bf16[64,640]{1,0:T(8,128)(2,1)S(1)}, bf16[64,640]{1,0:T(8,128)(2,1)S(1)}, u32[]{:S(2)}, u32[]{:S(2)}) collective-permute-start(bf16[64,640]{1,0:T(8,128)(2,1)S(1)} %get-tuple-element.15.refs_1_), channel_id=1, source_target_pairs={{0,6},{1,7},{2,4},{3,5},{4,2},{5,3},{6,0},{7,1},{8,14},{9,15},{10,... | collective-permute-start | bytes 245768 | tf_op jit(solution)/shard_map/ppermute | solution.py:274
  25.1 5.1 %collective-permute-start.1 = (bf16[64,640]{1,0:T(8,128)(2,1)S(1)}, bf16[64,640]{1,0:T(8,128)(2,1)S(1)}, u32[]{:S(2)}, u32[]{:S(2)}) collective-permute-start(bf16[64,640]{1,0:T(8,128)(2,1)S(1)} %collective-permute-done.refs_3_), channel_id=1, source_target_pairs={{0,2},{1,3},{2,0},{3,1},{4,6},{5,7},{6,4},{7,5},{8,10},{9,11},{10,... | collective-permute-start | bytes 245768 | tf_op jit(solution)/shard_map/ppermute | solution.py:274
  26.8 18.7 %copy-start.3 = (s32[4,3]{1,0:T(4,128)S(1)}, s32[4,3]{1,0:T(4,128)}, u32[]{:S(2)}) copy-start(s32[4,3]{1,0:T(4,128)} %lists_ref.1) | copy-start | bytes 148
  30.2 18.5 %copy-start.2 = (bf16[5120,128]{1,0:T(8,128)(2,1)S(1)}, bf16[5120,128]{1,0:T(8,128)(2,1)}, u32[]{:S(2)}) copy-start(bf16[5120,128]{1,0:T(8,128)(2,1)} %refs_2_.1) | copy-start | bytes 3932164
  30.4 2.6 %collective-permute-start.6 = (f32[128,256]{1,0:T(8,128)S(1)}, f32[128,256]{1,0:T(8,128)S(1)}, u32[]{:S(2)}, u32[]{:S(2)}) collective-permute-start(f32[128,256]{1,0:T(8,128)S(1)} %shard_map.94.own_ref), channel_id=1, source_target_pairs={{0,1},{1,0},{2,3},{3,2},{4,5},{5,4},{6,7},{7,6},{8,9},{9,8},{10,11... | collective-permute-start | bytes 393224 | tf_op jit(solution)/shard_map/ppermute | solution.py:277
  30.5 6.2 %collective-permute-start.12 = (bf16[128,384]{1,0:T(8,128)(2,1)S(1)}, bf16[128,384]{1,0:T(8,128)(2,1)S(1)}, u32[]{:S(2)}, u32[]{:S(2)}) collective-permute-start(bf16[128,384]{1,0:T(8,128)(2,1)S(1)} %get-tuple-element.19.refs_0_), channel_id=1, source_target_pairs={{0,24},{8,16},{16,8},{24,0},{1,25},{9,17},{17,9},{25,1},{2,26},{10... | collective-permute-start | bytes 294920 | tf_op jit(solution)/shard_map/ppermute | solution.py:280
  33.0 5.7 %collective-permute-start.11 = (bf16[128,384]{1,0:T(8,128)(2,1)S(1)}, bf16[128,384]{1,0:T(8,128)(2,1)S(1)}, u32[]{:S(2)}, u32[]{:S(2)}) collective-permute-start(bf16[128,384]{1,0:T(8,128)(2,1)S(1)} %get-tuple-element.19.refs_0_), channel_id=1, source_target_pairs={{0,16},{8,24},{16,0},{24,8},{1,17},{9,25},{17,1},{25,9},{2,18},{10... | collective-permute-start | bytes 294920 | tf_op jit(solution)/shard_map/ppermute | solution.py:280
  36.7 6.3 %collective-permute-start.10 = (bf16[128,384]{1,0:T(8,128)(2,1)S(1)}, bf16[128,384]{1,0:T(8,128)(2,1)S(1)}, u32[]{:S(2)}, u32[]{:S(2)}) collective-permute-start(bf16[128,384]{1,0:T(8,128)(2,1)S(1)} %get-tuple-element.19.refs_0_), channel_id=1, source_target_pairs={{0,8},{8,0},{16,24},{24,16},{1,9},{9,1},{17,25},{25,17},{2,10},{10... | collective-permute-start | bytes 294920 | tf_op jit(solution)/shard_map/ppermute | solution.py:280
  38.7 4.3 %collective-permute-start.7 = (bf16[128,256]{1,0:T(8,128)(2,1)S(1)}, bf16[128,256]{1,0:T(8,128)(2,1)S(1)}, u32[]{:S(2)}, u32[]{:S(2)}) collective-permute-start(bf16[128,256]{1,0:T(8,128)(2,1)S(1)} %get-tuple-element.18), channel_id=1, source_target_pairs={{0,8},{1,17},{2,10},{3,19},{4,12},{5,21},{6,14},{7,23},{8,0},{9,25... | collective-permute-start | bytes 196616 | tf_op jit(solution)/shard_map/ppermute | solution.py:284
  43.0 5.0 %collective-permute-start.8 = (bf16[128,256]{1,0:T(8,128)(2,1)S(1)}, bf16[128,256]{1,0:T(8,128)(2,1)S(1)}, u32[]{:S(2)}, u32[]{:S(2)}) collective-permute-start(bf16[128,256]{1,0:T(8,128)(2,1)S(1)} %collective-permute-done.7.beside), channel_id=1, source_target_pairs={{0,1},{1,0},{2,3},{3,2},{4,5},{5,4},{6,7},{7,6},{8,9},{9,8},{10,11... | collective-permute-start | bytes 196616 | tf_op jit(solution)/shard_map/ppermute | solution.py:277
  43.0 5.7 %copy-start = (bf16[5120,128]{1,0:T(8,128)(2,1)S(1)}, bf16[5120,128]{1,0:T(8,128)(2,1)}, u32[]{:S(2)}) copy-start(bf16[5120,128]{1,0:T(8,128)(2,1)} %refs_0_.1) | copy-start | bytes 3932164
  43.0 5.7 %copy-start.1 = (bf16[5120,128]{1,0:T(8,128)(2,1)S(1)}, bf16[5120,128]{1,0:T(8,128)(2,1)}, u32[]{:S(2)}) copy-start(bf16[5120,128]{1,0:T(8,128)(2,1)} %refs_1_.1) | copy-start | bytes 3932164
  43.0 4.9 %collective-permute-start.9 = (bf16[128,128]{1,0:T(8,128)(2,1)S(1)}, bf16[128,128]{1,0:T(8,128)(2,1)S(1)}, u32[]{:S(2)}, u32[]{:S(2)}) collective-permute-start(bf16[128,128]{1,0:T(8,128)(2,1)S(1)} %get-tuple-element.17.grad_ref.own), channel_id=1, source_target_pairs={{0,24},{8,16},{16,8},{24,0},{1,25},{9,17},{17,9},{25,1},{2,26},{10... | collective-permute-start | bytes 98312 | tf_op jit(solution)/shard_map/ppermute | solution.py:280
  48.4 1.4 %collective-permute-start.13 = (bf16[128,384]{1,0:T(8,128)(2,1)S(1)}, bf16[128,384]{1,0:T(8,128)(2,1)S(1)}, u32[]{:S(2)}, u32[]{:S(2)}) collective-permute-start(bf16[128,384]{1,0:T(8,128)(2,1)S(1)} %shard_map.98.own_ref), channel_id=1, source_target_pairs={{0,1},{1,0},{2,3},{3,2},{4,5},{5,4},{6,7},{7,6},{8,9},{9,8},{10,11... | collective-permute-start | bytes 294920 | tf_op jit(solution)/shard_map/ppermute | solution.py:277
  50.0 6.1 %collective-permute-start.18 = (bf16[448,128]{1,0:T(8,128)(2,1)S(1)}, bf16[448,128]{1,0:T(8,128)(2,1)S(1)}, u32[]{:S(2)}, u32[]{:S(2)}) collective-permute-start(bf16[448,128]{1,0:T(8,128)(2,1)S(1)} %shard_map.102), channel_id=1, source_target_pairs={{0,2},{1,3},{2,0},{3,1},{4,6},{5,7},{6,4},{7,5},{8,10},{9,11},{10,... | collective-permute-start | bytes 344072 | tf_op jit(solution)/shard_map/ppermute | solution.py:274
  50.7 16.4 %collective-permute-start.17 = (bf16[640,128]{1,0:T(8,128)(2,1)S(1)}, bf16[640,128]{1,0:T(8,128)(2,1)S(1)}, u32[]{:S(2)}, u32[]{:S(2)}) collective-permute-start(bf16[640,128]{1,0:T(8,128)(2,1)S(1)} %shard_map.101), channel_id=1, source_target_pairs={{0,2},{1,3},{2,0},{3,1},{4,6},{5,7},{6,4},{7,5},{8,10},{9,11},{10,... | collective-permute-start | bytes 491528 | tf_op jit(solution)/shard_map/ppermute | solution.py:274
  56.4 10.6 %collective-permute-start.19 = (bf16[448,128]{1,0:T(8,128)(2,1)S(1)}, bf16[448,128]{1,0:T(8,128)(2,1)S(1)}, u32[]{:S(2)}, u32[]{:S(2)}) collective-permute-start(bf16[448,128]{1,0:T(8,128)(2,1)S(1)} %shard_map.103), channel_id=1, source_target_pairs={{0,4},{1,5},{2,6},{3,7},{4,0},{5,1},{6,2},{7,3},{8,12},{9,13},{10,... | collective-permute-start | bytes 344072 | tf_op jit(solution)/shard_map/ppermute | solution.py:274
  57.2 9.8 %collective-permute-start.20 = (bf16[192,128]{1,0:T(8,128)(2,1)S(1)}, bf16[192,128]{1,0:T(8,128)(2,1)S(1)}, u32[]{:S(2)}, u32[]{:S(2)}) collective-permute-start(bf16[192,128]{1,0:T(8,128)(2,1)S(1)} %shard_map.104), channel_id=1, source_target_pairs={{0,4},{1,5},{2,6},{3,7},{4,0},{5,1},{6,2},{7,3},{8,12},{9,13},{10,... | collective-permute-start | bytes 147464 | tf_op jit(solution)/shard_map/ppermute | solution.py:274
  59.9 7.2 %collective-permute-start.21 = (bf16[192,128]{1,0:T(8,128)(2,1)S(1)}, bf16[192,128]{1,0:T(8,128)(2,1)S(1)}, u32[]{:S(2)}, u32[]{:S(2)}) collective-permute-start(bf16[192,128]{1,0:T(8,128)(2,1)S(1)} %shard_map.105), channel_id=1, source_target_pairs={{0,6},{1,7},{2,4},{3,5},{4,2},{5,3},{6,0},{7,1},{8,14},{9,15},{10,... | collective-permute-start | bytes 147464 | tf_op jit(solution)/shard_map/ppermute | solution.py:274

commit v6 on v5

--- a/solution.py
+++ b/solution.py
@@ -9,6 +9,7 @@
 
 
 TILE = 128
+PIECES = 2
 EARLY = (0, 1, 2)
 CONTRACT_LAST = (((1,), (1,)), ((), ()))
 CONTRACT_FIRST = (((0,), (0,)), ((), ()))
@@ -93,8 +94,15 @@
     outs, sems = refs[:-1], refs[-1]
     copies, start = [], 0
     for place, out in enumerate(outs):
-        span = pl.ds(start, out.shape[0])
-        copies.append(pltpu.make_async_copy(whole_ref.at[span], out, sems.at[place]))
+        step = out.shape[0] // PIECES
+        for piece in range(PIECES):
+            copies.append(
+                pltpu.make_async_copy(
+                    whole_ref.at[pl.ds(start + piece * step, step)],
+                    out.at[pl.ds(piece * step, step)],
+                    sems.at[place * PIECES + piece],
+                )
+            )
         start += out.shape[0]
     for copy in copies:
         copy.start()
@@ -102,11 +110,12 @@
         copy.wait()
 
 
-def attn_grad_kernel(cols, steps, *refs):
+def attn_grad_kernel(cols, steps, results, *refs):
     index = lax.axis_index("tp")
     count = sum(1 if step == 1 else 2 for step in steps)
-    parts, own_w, mate_w, out_ref = list(refs[:count]), refs[count], refs[count + 1], refs[-1]
-    total = refs[-2][...] if len(refs) > count + 3 else None
+    refs, outs = refs[:-results], refs[-results:]
+    parts, own_w, mate_w = list(refs[:count]), refs[count], refs[count + 1]
+    total = refs[-1][...] if len(refs) > count + 2 else None
     for step in steps:
         start = pl.multiple_of((index ^ (2 * step)) * cols, 128)
         weight = jnp.concatenate(
@@ -116,7 +125,8 @@
         block = jnp.concatenate(pieces, axis=0)
         term = dot_f32(block, weight, CONTRACT_LAST)
         total = term if total is None else total + term
-    out_ref[...] = total
+    for out in outs:
+        out[...] = total.astype(out.dtype)
 
 
 def merge_kernel(own_ref, mate_ref, out_ref, own_out_ref):
@@ -285,7 +295,7 @@
 
     top, low = call(
         split_kernel, [grad_out], [((cut, cols), half), ((rows - cut, cols), half)],
-        raw=True, sems=2,
+        raw=True, sems=2 * PIECES,
     )
     top2 = to_chip(top, 2)
     near = to_chip(grad_out, 1)
@@ -306,18 +316,18 @@
         [((rows, slabs * rows), full), ((slabs * rows, rows), full), ((slabs * rows, size), full)],
     )
     (early,) = call(
-        functools.partial(attn_grad_kernel, cols, EARLY),
+        functools.partial(attn_grad_kernel, cols, EARLY, 1),
         [top, low, near] + ([top2, low2] if 2 in EARLY else []) + [near_out, mate_out],
         [((rows, 2 * size), full)],
     )
     late = tuple(step for step in range(4) if step not in EARLY)
-    (part,) = call(
-        functools.partial(attn_grad_kernel, cols, late),
+    part, narrow = call(
+        functools.partial(attn_grad_kernel, cols, late, 2),
         ([] if 2 in EARLY else [top2, low2]) + [top3, low3, near_out, mate_out, early],
-        [((rows, 2 * size), full)],
+        [((rows, 2 * size), full), ((rows, 2 * size), half)],
     )
     both, grad = call(
-        merge_kernel, [part, to_mate(part)],
+        merge_kernel, [part, to_mate(narrow)],
         [((rows, 2 * size), half), ((rows, size), half)],
     )
     beside = to_beside(both)

time: 68 us -> 67.9 us (level)
  no operation moved by 1% of the time
where the time goes in v6:
time: 67.9 us; the launch traced here: 67.7 us
  waiting for transfers between devices  34.6 us (51%)
  starting transfers between devices  24.3 us (36%)
  Pallas kernels  8.65 us (13%)
    ppermute x10, waiting for transfers between devices, to_chip(): return lax.ppermute(x, 'tp', [(t, t ^ 2 * step) for t in range(8)])  27.7 us
    ppermute x10, starting transfers between devices, to_chip(): return lax.ppermute(x, 'tp', [(t, t ^ 2 * step) for t in range(8)])  14.5 us
    pallas_call x16, Pallas kernels, call(): pl.pallas_call(kernel, in_specs=[SMEM if flag else there for flag in ints...  8.65 us
    ppermute x4, starting transfers between devices, to_slab(): return lax.ppermute(x, 'ctx', [(c, c ^ turn) for c in range(slabs)])  7.03 us
    ppermute x4, waiting for transfers between devices, to_slab(): return lax.ppermute(x, 'ctx', [(c, c ^ turn) for c in range(slabs)])  3.66 us
    ppermute x1, waiting for transfers between devices, to_beside(): return lax.ppermute(x, ('ctx', 'tp'), pairs)  2.78 us
    ppermute x1, starting transfers between devices, to_beside(): return lax.ppermute(x, ('ctx', 'tp'), pairs)  1.49 us
  transfers between devices with their start and end apart: 22, of which 11 were waited for; matrix products, arithmetic and copies ran while one was open for 0% of the time, Pallas kernels for 11%

profile of v6, /device:TPU:0, one launch (start us, length us, event | category | flops | bytes accessed | tf_op | source)
XLA Modules:
  0.0 67.7 jit_solution(1362420661145753124)
XLA Ops:
  0.0 0.5 collective-permute-start.3
  0.5 0.0 collective-permute-start.14
  0.5 0.5 collective-permute-start.15
  1.0 0.0 collective-permute-start.16
  1.0 0.9 %shard_map.91 = (bf16[64,640]{1,0:T(8,128)(2,1)S(1)}, bf16[64,640]{1,0:T(8,128)(2,1)S(1)}) custom-call(bf16[128,640]{1,0:T(8,128)(2,1)} %whole_ref.1), custom_call_target="tpu_custom_call" | custom-call | tf_op jit(solution)/shard_map/pallas_call | solution.py:253
  1.9 4.1 %collective-permute-start = (bf16[64,640]{1,0:T(8,128)(2,1)S(1)}, bf16[64,640]{1,0:T(8,128)(2,1)S(1)}, u32[]{:S(2)}, u32[]{:S(2)}) collective-permute-start(bf16[64,640]{1,0:T(8,128)(2,1)S(1)} %get-tuple-element.16.refs_0_), channel_id=1, source_target_pairs={{0,4},{1,5},{2,6},{3,7},{4,0},{5,1},{6,2},{7,3},{8,12},{9,13},{10,... | collective-permute-start | bytes 245768 | tf_op jit(solution)/shard_map/ppermute | solution.py:284
  6.0 4.4 %collective-permute-done.refs_3_ = bf16[64,640]{1,0:T(8,128)(2,1)S(1)} collective-permute-done((bf16[64,640]{1,0:T(8,128)(2,1)S(1)}, bf16[64,640]{1,0:T(8,128)(2,1)S(1)}, u32[]{:S(2)}, u32[]{:S(2)}) %collective-permute-start) | collective-permute-done | bytes 81952 | tf_op jit(solution)/shard_map/ppermute | solution.py:284
  10.4 1.0 %collective-permute-start.5 = (bf16[64,640]{1,0:T(8,128)(2,1)S(1)}, bf16[64,640]{1,0:T(8,128)(2,1)S(1)}, u32[]{:S(2)}, u32[]{:S(2)}) collective-permute-start(bf16[64,640]{1,0:T(8,128)(2,1)S(1)} %get-tuple-element.17.refs_1_), channel_id=1, source_target_pairs={{0,4},{1,5},{2,6},{3,7},{4,0},{5,1},{6,2},{7,3},{8,12},{9,13},{10,... | collective-permute-start | bytes 245768 | tf_op jit(solution)/shard_map/ppermute | solution.py:284
  11.4 6.1 %collective-permute-done.5.refs_4_ = bf16[64,640]{1,0:T(8,128)(2,1)S(1)} collective-permute-done((bf16[64,640]{1,0:T(8,128)(2,1)S(1)}, bf16[64,640]{1,0:T(8,128)(2,1)S(1)}, u32[]{:S(2)}, u32[]{:S(2)}) %collective-permute-start.5) | collective-permute-done | bytes 81952 | tf_op jit(solution)/shard_map/ppermute | solution.py:284
  17.4 0.0 collective-permute-start.4
  17.4 5.5 %collective-permute-done.4.refs_2_ = bf16[128,640]{1,0:T(8,128)(2,1)S(1)} collective-permute-done((bf16[128,640]{1,0:T(8,128)(2,1)}, bf16[128,640]{1,0:T(8,128)(2,1)S(1)}, u32[]{:S(2)}, u32[]{:S(2)}) %collective-permute-start.4) | collective-permute-done | bytes 163872 | tf_op jit(solution)/shard_map/ppermute | solution.py:284
  23.0 2.1 %collective-permute-start.2 = (bf16[64,640]{1,0:T(8,128)(2,1)S(1)}, bf16[64,640]{1,0:T(8,128)(2,1)S(1)}, u32[]{:S(2)}, u32[]{:S(2)}) collective-permute-start(bf16[64,640]{1,0:T(8,128)(2,1)S(1)} %get-tuple-element.17.refs_1_), channel_id=1, source_target_pairs={{0,6},{1,7},{2,4},{3,5},{4,2},{5,3},{6,0},{7,1},{8,14},{9,15},{10,... | collective-permute-start | bytes 245768 | tf_op jit(solution)/shard_map/ppermute | solution.py:284
  25.0 0.0 collective-permute-done.3.refs_6_.refs_3_
  25.0 0.0 collective-permute-start.1
  25.0 1.3 %shard_map.92 = (bf16[128,384]{1,0:T(8,128)(2,1)S(1)}, bf16[128,2560]{1,0:T(8,128)(2,1)S(1)}) custom-call(bf16[128,128]{1,0:T(8,128)(2,1)} %query_ref.1, bf16[128,128]{1,0:T(8,128)(2,1)} %key_ref.1, bf16[128,128]{1,0:T(8,128)(2,1)} %value_ref.1, bf16[128,5120]{1,0:T(8,128)(2,1)} %w_ref.1), custom_call_target="tpu_custom_call" | custom-call | tf_op jit(solution)/shard_map/pallas_call | solution.py:253
  26.3 0.4 shard_map.93.refs_4_
  26.8 0.0 copy-start.3
  26.8 2.5 %collective-permute-done.2.refs_1_ = bf16[64,640]{1,0:T(8,128)(2,1)S(1)} collective-permute-done((bf16[64,640]{1,0:T(8,128)(2,1)S(1)}, bf16[64,640]{1,0:T(8,128)(2,1)S(1)}, u32[]{:S(2)}, u32[]{:S(2)}) %collective-permute-start.2) | collective-permute-done | bytes 81952 | tf_op jit(solution)/shard_map/ppermute | solution.py:284
  29.3 0.8 %collective-permute-done.1.refs_0_ = bf16[64,640]{1,0:T(8,128)(2,1)S(1)} collective-permute-done((bf16[64,640]{1,0:T(8,128)(2,1)S(1)}, bf16[64,640]{1,0:T(8,128)(2,1)S(1)}, u32[]{:S(2)}, u32[]{:S(2)}) %collective-permute-start.1) | collective-permute-done | bytes 81952 | tf_op jit(solution)/shard_map/ppermute | solution.py:284
  30.1 0.2 shard_map.94
  30.3 0.1 collective-permute-start.6
  30.4 2.5 %collective-permute-start.12 = (bf16[128,384]{1,0:T(8,128)(2,1)S(1)}, bf16[128,384]{1,0:T(8,128)(2,1)S(1)}, u32[]{:S(2)}, u32[]{:S(2)}) collective-permute-start(bf16[128,384]{1,0:T(8,128)(2,1)S(1)} %get-tuple-element.23.refs_0_), channel_id=1, source_target_pairs={{0,24},{8,16},{16,8},{24,0},{1,25},{9,17},{17,9},{25,1},{2,26},{10... | collective-permute-start | bytes 294920 | tf_op jit(solution)/shard_map/ppermute | solution.py:290
  32.9 0.0 collective-permute-done.6.mate_ref
  32.9 0.5 collective-permute-start.11
  33.5 3.1 %collective-permute-done.12.refs_3_ = bf16[128,384]{1,0:T(8,128)(2,1)S(1)} collective-permute-done((bf16[128,384]{1,0:T(8,128)(2,1)S(1)}, bf16[128,384]{1,0:T(8,128)(2,1)S(1)}, u32[]{:S(2)}, u32[]{:S(2)}) %collective-permute-start.12) | collective-permute-done | bytes 98336 | tf_op jit(solution)/shard_map/ppermute | solution.py:290
  36.6 1.5 %collective-permute-start.10 = (bf16[128,384]{1,0:T(8,128)(2,1)S(1)}, bf16[128,384]{1,0:T(8,128)(2,1)S(1)}, u32[]{:S(2)}, u32[]{:S(2)}) collective-permute-start(bf16[128,384]{1,0:T(8,128)(2,1)S(1)} %get-tuple-element.23.refs_0_), channel_id=1, source_target_pairs={{0,8},{8,0},{16,24},{24,16},{1,9},{9,1},{17,25},{25,17},{2,10},{10... | collective-permute-start | bytes 294920 | tf_op jit(solution)/shard_map/ppermute | solution.py:290
  38.1 0.5 collective-permute-done.11.refs_2_
  38.6 1.5 %collective-permute-start.7 = (bf16[128,256]{1,0:T(8,128)(2,1)S(1)}, bf16[128,256]{1,0:T(8,128)(2,1)S(1)}, u32[]{:S(2)}, u32[]{:S(2)}) collective-permute-start(bf16[128,256]{1,0:T(8,128)(2,1)S(1)} %get-tuple-element.22), channel_id=1, source_target_pairs={{0,8},{1,17},{2,10},{3,19},{4,12},{5,21},{6,14},{7,23},{8,0},{9,25... | collective-permute-start | bytes 196616 | tf_op jit(solution)/shard_map/ppermute | solution.py:294
  40.1 2.8 %collective-permute-done.7.beside = bf16[128,256]{1,0:T(8,128)(2,1)S(1)} collective-permute-done((bf16[128,256]{1,0:T(8,128)(2,1)S(1)}, bf16[128,256]{1,0:T(8,128)(2,1)S(1)}, u32[]{:S(2)}, u32[]{:S(2)}) %collective-permute-start.7) | collective-permute-done | bytes 65568 | tf_op jit(solution)/shard_map/ppermute | solution.py:294
  42.9 0.0 collective-permute-start.8
  42.9 0.0 collective-permute-done.10.refs_1_
  42.9 0.0 copy-start.1
  42.9 2.5 %collective-permute-start.9 = (bf16[128,128]{1,0:T(8,128)(2,1)S(1)}, bf16[128,128]{1,0:T(8,128)(2,1)S(1)}, u32[]{:S(2)}, u32[]{:S(2)}) collective-permute-start(bf16[128,128]{1,0:T(8,128)(2,1)S(1)} %get-tuple-element.21.grad_ref.own), channel_id=1, source_target_pairs={{0,24},{8,16},{16,8},{24,0},{1,25},{9,17},{17,9},{25,1},{2,26},{10... | collective-permute-start | bytes 98312 | tf_op jit(solution)/shard_map/ppermute | solution.py:290
  45.4 0.0 copy-done.3
  45.4 2.1 %shard_map.96 = (f32[128,512]{1,0:T(8,128)S(1)}, f32[512,128]{1,0:T(8,128)S(1)}, f32[512,128]{1,0:T(8,128)S(1)}) custom-call(s32[4,3]{1,0:T(4,128)S(1)} %copy-done.3, bf16[128,384]{1,0:T(8,128)(2,1)S(1)} %get-tuple-element.23.refs_0_, bf16[128,384]{1,0:T(8,128)(2,1)S(1)} %collective-permute-done.10.refs_1_, ...), custom_call_target="tpu_custom_call" | custom-call | tf_op jit(solution)/shard_map/pallas_call | solution.py:253
  47.5 0.3 shard_map.97.refs_4_
  47.8 0.0 collective-permute-done.9.across
  47.9 0.0 collective-permute-done.8.swapped
  47.9 0.5 shard_map.98.own_ref
  48.3 0.2 collective-permute-start.13
  48.5 0.0 copy-done.2
  48.6 0.0 copy-done
  48.6 0.7 shard_map.99.own_ref
  49.2 0.0 collective-permute-done.14.refs_0_
  49.2 0.0 collective-permute-done.15.refs_1_
  49.2 0.0 collective-permute-done.16.refs_2_
  49.3 0.4 collective-permute-done.13.mate_ref
  49.7 0.3 shard_map.102
  50.0 0.3 collective-permute-start.18
  50.3 0.3 shard_map.101
  50.6 1.8 %collective-permute-start.17 = (bf16[640,128]{1,0:T(8,128)(2,1)S(1)}, bf16[640,128]{1,0:T(8,128)(2,1)S(1)}, u32[]{:S(2)}, u32[]{:S(2)}) collective-permute-start(bf16[640,128]{1,0:T(8,128)(2,1)S(1)} %shard_map.101), channel_id=1, source_target_pairs={{0,2},{1,3},{2,0},{3,1},{4,6},{5,7},{6,4},{7,5},{8,10},{9,11},{10,... | collective-permute-start | bytes 491528 | tf_op jit(solution)/shard_map/ppermute | solution.py:284
  52.4 3.6 %collective-permute-done.18.refs_3_ = bf16[448,128]{1,0:T(8,128)(2,1)S(1)} collective-permute-done((bf16[448,128]{1,0:T(8,128)(2,1)S(1)}, bf16[448,128]{1,0:T(8,128)(2,1)S(1)}, u32[]{:S(2)}, u32[]{:S(2)}) %collective-permute-start.18) | collective-permute-done | bytes 114720 | tf_op jit(solution)/shard_map/ppermute | solution.py:284
  56.0 0.3 shard_map.103
  56.3 0.6 collective-permute-start.19
  56.9 0.2 shard_map.104
  57.1 2.4 %collective-permute-start.20 = (bf16[192,128]{1,0:T(8,128)(2,1)S(1)}, bf16[192,128]{1,0:T(8,128)(2,1)S(1)}, u32[]{:S(2)}, u32[]{:S(2)}) collective-permute-start(bf16[192,128]{1,0:T(8,128)(2,1)S(1)} %shard_map.104), channel_id=1, source_target_pairs={{0,4},{1,5},{2,6},{3,7},{4,0},{5,1},{6,2},{7,3},{8,12},{9,13},{10,... | collective-permute-start | bytes 147464 | tf_op jit(solution)/shard_map/ppermute | solution.py:284
  59.6 0.2 shard_map.105
  59.8 2.1 %collective-permute-start.21 = (bf16[192,128]{1,0:T(8,128)(2,1)S(1)}, bf16[192,128]{1,0:T(8,128)(2,1)S(1)}, u32[]{:S(2)}, u32[]{:S(2)}) collective-permute-start(bf16[192,128]{1,0:T(8,128)(2,1)S(1)} %shard_map.105), channel_id=1, source_target_pairs={{0,6},{1,7},{2,4},{3,5},{4,2},{5,3},{6,0},{7,1},{8,14},{9,15},{10,... | collective-permute-start | bytes 147464 | tf_op jit(solution)/shard_map/ppermute | solution.py:284
  61.9 0.3 shard_map.100.own_ref
  62.2 4.8 %collective-permute-done.20.low2 = bf16[192,128]{1,0:T(8,128)(2,1)S(1)} collective-permute-done((bf16[192,128]{1,0:T(8,128)(2,1)S(1)}, bf16[192,128]{1,0:T(8,128)(2,1)S(1)}, u32[]{:S(2)}, u32[]{:S(2)}) %collective-permute-start.20) | collective-permute-done | bytes 49184 | tf_op jit(solution)/shard_map/ppermute | solution.py:284
  66.9 0.0 collective-permute-done.21.low3
  66.9 0.0 collective-permute-done.17.near
  66.9 0.0 collective-permute-done.19.top2
  66.9 0.8 %shard_map.106 = f32[640,128]{1,0:T(8,128)} custom-call(f32[640,128]{1,0:T(8,128)S(1)} %shard_map.100.own_ref, bf16[640,128]{1,0:T(8,128)(2,1)S(1)} %collective-permute-done.17.near, bf16[448,128]{1,0:T(8,128)(2,1)S(1)} %collective-permute-done.19.top2, bf16[192,128]{1,0:T(8,128)(2,1)S(1)} %collective-permute-done.20.low2, ...), custom_call_target="tpu_custom_call" | custom-call | tf_op jit(solution)/shard_map/pallas_call | solution.py:253
  (4 shorter events, 0.0 us)
Async XLA Ops:
  0.0 25.0 %collective-permute-start.3 = (bf16[128,5120]{1,0:T(8,128)(2,1)}, bf16[128,5120]{1,0:T(8,128)(2,1)S(1)}, u32[]{:S(2)}, u32[]{:S(2)}) collective-permute-start(bf16[128,5120]{1,0:T(8,128)(2,1)} %w_ref.1), channel_id=1, source_target_pairs={{0,1},{1,0},{2,3},{3,2},{4,5},{5,4},{6,7},{7,6},{8,9},{9,8},{10,11... | collective-permute-start | bytes 3932168 | tf_op jit(solution)/shard_map/ppermute | solution.py:287
  0.5 48.7 %collective-permute-start.14 = (bf16[5120,128]{1,0:T(8,128)(2,1)}, bf16[5120,128]{1,0:T(8,128)(2,1)S(1)}, u32[]{:S(2)}, u32[]{:S(2)}) collective-permute-start(bf16[5120,128]{1,0:T(8,128)(2,1)} %refs_0_.1), channel_id=1, source_target_pairs={{0,1},{1,0},{2,3},{3,2},{4,5},{5,4},{6,7},{7,6},{8,9},{9,8},{10,11... | collective-permute-start | bytes 3932168 | tf_op jit(solution)/shard_map/ppermute | solution.py:287
  0.5 48.7 %collective-permute-start.15 = (bf16[5120,128]{1,0:T(8,128)(2,1)}, bf16[5120,128]{1,0:T(8,128)(2,1)S(1)}, u32[]{:S(2)}, u32[]{:S(2)}) collective-permute-start(bf16[5120,128]{1,0:T(8,128)(2,1)} %refs_1_.1), channel_id=1, source_target_pairs={{0,1},{1,0},{2,3},{3,2},{4,5},{5,4},{6,7},{7,6},{8,9},{9,8},{10,11... | collective-permute-start | bytes 3932168 | tf_op jit(solution)/shard_map/ppermute | solution.py:287
  1.0 48.2 %collective-permute-start.16 = (bf16[5120,128]{1,0:T(8,128)(2,1)}, bf16[5120,128]{1,0:T(8,128)(2,1)S(1)}, u32[]{:S(2)}, u32[]{:S(2)}) collective-permute-start(bf16[5120,128]{1,0:T(8,128)(2,1)} %refs_2_.1), channel_id=1, source_target_pairs={{0,1},{1,0},{2,3},{3,2},{4,5},{5,4},{6,7},{7,6},{8,9},{9,8},{10,11... | collective-permute-start | bytes 3932168 | tf_op jit(solution)/shard_map/ppermute | solution.py:287
  1.9 8.5 %collective-permute-start = (bf16[64,640]{1,0:T(8,128)(2,1)S(1)}, bf16[64,640]{1,0:T(8,128)(2,1)S(1)}, u32[]{:S(2)}, u32[]{:S(2)}) collective-permute-start(bf16[64,640]{1,0:T(8,128)(2,1)S(1)} %get-tuple-element.16.refs_0_), channel_id=1, source_target_pairs={{0,4},{1,5},{2,6},{3,7},{4,0},{5,1},{6,2},{7,3},{8,12},{9,13},{10,... | collective-permute-start | bytes 245768 | tf_op jit(solution)/shard_map/ppermute | solution.py:284
  10.4 7.0 %collective-permute-start.5 = (bf16[64,640]{1,0:T(8,128)(2,1)S(1)}, bf16[64,640]{1,0:T(8,128)(2,1)S(1)}, u32[]{:S(2)}, u32[]{:S(2)}) collective-permute-start(bf16[64,640]{1,0:T(8,128)(2,1)S(1)} %get-tuple-element.17.refs_1_), channel_id=1, source_target_pairs={{0,4},{1,5},{2,6},{3,7},{4,0},{5,1},{6,2},{7,3},{8,12},{9,13},{10,... | collective-permute-start | bytes 245768 | tf_op jit(solution)/shard_map/ppermute | solution.py:284
  17.4 5.5 %collective-permute-start.4 = (bf16[128,640]{1,0:T(8,128)(2,1)}, bf16[128,640]{1,0:T(8,128)(2,1)S(1)}, u32[]{:S(2)}, u32[]{:S(2)}) collective-permute-start(bf16[128,640]{1,0:T(8,128)(2,1)} %whole_ref.1), channel_id=1, source_target_pairs={{0,2},{1,3},{2,0},{3,1},{4,6},{5,7},{6,4},{7,5},{8,10},{9,11},{10,... | collective-permute-start | bytes 491528 | tf_op jit(solution)/shard_map/ppermute | solution.py:284
  23.0 6.3 %collective-permute-start.2 = (bf16[64,640]{1,0:T(8,128)(2,1)S(1)}, bf16[64,640]{1,0:T(8,128)(2,1)S(1)}, u32[]{:S(2)}, u32[]{:S(2)}) collective-permute-start(bf16[64,640]{1,0:T(8,128)(2,1)S(1)} %get-tuple-element.17.refs_1_), channel_id=1, source_target_pairs={{0,6},{1,7},{2,4},{3,5},{4,2},{5,3},{6,0},{7,1},{8,14},{9,15},{10,... | collective-permute-start | bytes 245768 | tf_op jit(solution)/shard_map/ppermute | solution.py:284
  25.0 5.1 %collective-permute-start.1 = (bf16[64,640]{1,0:T(8,128)(2,1)S(1)}, bf16[64,640]{1,0:T(8,128)(2,1)S(1)}, u32[]{:S(2)}, u32[]{:S(2)}) collective-permute-start(bf16[64,640]{1,0:T(8,128)(2,1)S(1)} %collective-permute-done.refs_3_), channel_id=1, source_target_pairs={{0,2},{1,3},{2,0},{3,1},{4,6},{5,7},{6,4},{7,5},{8,10},{9,11},{10,... | collective-permute-start | bytes 245768 | tf_op jit(solution)/shard_map/ppermute | solution.py:284
  26.8 18.7 %copy-start.3 = (s32[4,3]{1,0:T(4,128)S(1)}, s32[4,3]{1,0:T(4,128)}, u32[]{:S(2)}) copy-start(s32[4,3]{1,0:T(4,128)} %lists_ref.1) | copy-start | bytes 148
  30.1 18.5 %copy-start.2 = (bf16[5120,128]{1,0:T(8,128)(2,1)S(1)}, bf16[5120,128]{1,0:T(8,128)(2,1)}, u32[]{:S(2)}) copy-start(bf16[5120,128]{1,0:T(8,128)(2,1)} %refs_2_.1) | copy-start | bytes 3932164
  30.3 2.6 %collective-permute-start.6 = (bf16[128,256]{1,0:T(8,128)(2,1)S(1)}, bf16[128,256]{1,0:T(8,128)(2,1)S(1)}, u32[]{:S(2)}, u32[]{:S(2)}) collective-permute-start(bf16[128,256]{1,0:T(8,128)(2,1)S(1)} %get-tuple-element.20), channel_id=1, source_target_pairs={{0,1},{1,0},{2,3},{3,2},{4,5},{5,4},{6,7},{7,6},{8,9},{9,8},{10,11... | collective-permute-start | bytes 196616 | tf_op jit(solution)/shard_map/ppermute | solution.py:287
  30.4 6.2 %collective-permute-start.12 = (bf16[128,384]{1,0:T(8,128)(2,1)S(1)}, bf16[128,384]{1,0:T(8,128)(2,1)S(1)}, u32[]{:S(2)}, u32[]{:S(2)}) collective-permute-start(bf16[128,384]{1,0:T(8,128)(2,1)S(1)} %get-tuple-element.23.refs_0_), channel_id=1, source_target_pairs={{0,24},{8,16},{16,8},{24,0},{1,25},{9,17},{17,9},{25,1},{2,26},{10... | collective-permute-start | bytes 294920 | tf_op jit(solution)/shard_map/ppermute | solution.py:290
  32.9 5.7 %collective-permute-start.11 = (bf16[128,384]{1,0:T(8,128)(2,1)S(1)}, bf16[128,384]{1,0:T(8,128)(2,1)S(1)}, u32[]{:S(2)}, u32[]{:S(2)}) collective-permute-start(bf16[128,384]{1,0:T(8,128)(2,1)S(1)} %get-tuple-element.23.refs_0_), channel_id=1, source_target_pairs={{0,16},{8,24},{16,0},{24,8},{1,17},{9,25},{17,1},{25,9},{2,18},{10... | collective-permute-start | bytes 294920 | tf_op jit(solution)/shard_map/ppermute | solution.py:290
  36.6 6.3 %collective-permute-start.10 = (bf16[128,384]{1,0:T(8,128)(2,1)S(1)}, bf16[128,384]{1,0:T(8,128)(2,1)S(1)}, u32[]{:S(2)}, u32[]{:S(2)}) collective-permute-start(bf16[128,384]{1,0:T(8,128)(2,1)S(1)} %get-tuple-element.23.refs_0_), channel_id=1, source_target_pairs={{0,8},{8,0},{16,24},{24,16},{1,9},{9,1},{17,25},{25,17},{2,10},{10... | collective-permute-start | bytes 294920 | tf_op jit(solution)/shard_map/ppermute | solution.py:290
  38.6 4.3 %collective-permute-start.7 = (bf16[128,256]{1,0:T(8,128)(2,1)S(1)}, bf16[128,256]{1,0:T(8,128)(2,1)S(1)}, u32[]{:S(2)}, u32[]{:S(2)}) collective-permute-start(bf16[128,256]{1,0:T(8,128)(2,1)S(1)} %get-tuple-element.22), channel_id=1, source_target_pairs={{0,8},{1,17},{2,10},{3,19},{4,12},{5,21},{6,14},{7,23},{8,0},{9,25... | collective-permute-start | bytes 196616 | tf_op jit(solution)/shard_map/ppermute | solution.py:294
  42.9 5.0 %collective-permute-start.8 = (bf16[128,256]{1,0:T(8,128)(2,1)S(1)}, bf16[128,256]{1,0:T(8,128)(2,1)S(1)}, u32[]{:S(2)}, u32[]{:S(2)}) collective-permute-start(bf16[128,256]{1,0:T(8,128)(2,1)S(1)} %collective-permute-done.7.beside), channel_id=1, source_target_pairs={{0,1},{1,0},{2,3},{3,2},{4,5},{5,4},{6,7},{7,6},{8,9},{9,8},{10,11... | collective-permute-start | bytes 196616 | tf_op jit(solution)/shard_map/ppermute | solution.py:287
  42.9 5.7 %copy-start = (bf16[5120,128]{1,0:T(8,128)(2,1)S(1)}, bf16[5120,128]{1,0:T(8,128)(2,1)}, u32[]{:S(2)}) copy-start(bf16[5120,128]{1,0:T(8,128)(2,1)} %refs_0_.1) | copy-start | bytes 3932164
  42.9 5.7 %copy-start.1 = (bf16[5120,128]{1,0:T(8,128)(2,1)S(1)}, bf16[5120,128]{1,0:T(8,128)(2,1)}, u32[]{:S(2)}) copy-start(bf16[5120,128]{1,0:T(8,128)(2,1)} %refs_1_.1) | copy-start | bytes 3932164
  42.9 4.9 %collective-permute-start.9 = (bf16[128,128]{1,0:T(8,128)(2,1)S(1)}, bf16[128,128]{1,0:T(8,128)(2,1)S(1)}, u32[]{:S(2)}, u32[]{:S(2)}) collective-permute-start(bf16[128,128]{1,0:T(8,128)(2,1)S(1)} %get-tuple-element.21.grad_ref.own), channel_id=1, source_target_pairs={{0,24},{8,16},{16,8},{24,0},{1,25},{9,17},{17,9},{25,1},{2,26},{10... | collective-permute-start | bytes 98312 | tf_op jit(solution)/shard_map/ppermute | solution.py:290
  48.3 1.4 %collective-permute-start.13 = (bf16[128,384]{1,0:T(8,128)(2,1)S(1)}, bf16[128,384]{1,0:T(8,128)(2,1)S(1)}, u32[]{:S(2)}, u32[]{:S(2)}) collective-permute-start(bf16[128,384]{1,0:T(8,128)(2,1)S(1)} %shard_map.98.own_ref), channel_id=1, source_target_pairs={{0,1},{1,0},{2,3},{3,2},{4,5},{5,4},{6,7},{7,6},{8,9},{9,8},{10,11... | collective-permute-start | bytes 294920 | tf_op jit(solution)/shard_map/ppermute | solution.py:287
  50.0 6.1 %collective-permute-start.18 = (bf16[448,128]{1,0:T(8,128)(2,1)S(1)}, bf16[448,128]{1,0:T(8,128)(2,1)S(1)}, u32[]{:S(2)}, u32[]{:S(2)}) collective-permute-start(bf16[448,128]{1,0:T(8,128)(2,1)S(1)} %shard_map.102), channel_id=1, source_target_pairs={{0,2},{1,3},{2,0},{3,1},{4,6},{5,7},{6,4},{7,5},{8,10},{9,11},{10,... | collective-permute-start | bytes 344072 | tf_op jit(solution)/shard_map/ppermute | solution.py:284
  50.6 16.4 %collective-permute-start.17 = (bf16[640,128]{1,0:T(8,128)(2,1)S(1)}, bf16[640,128]{1,0:T(8,128)(2,1)S(1)}, u32[]{:S(2)}, u32[]{:S(2)}) collective-permute-start(bf16[640,128]{1,0:T(8,128)(2,1)S(1)} %shard_map.101), channel_id=1, source_target_pairs={{0,2},{1,3},{2,0},{3,1},{4,6},{5,7},{6,4},{7,5},{8,10},{9,11},{10,... | collective-permute-start | bytes 491528 | tf_op jit(solution)/shard_map/ppermute | solution.py:284
  56.3 10.6 %collective-permute-start.19 = (bf16[448,128]{1,0:T(8,128)(2,1)S(1)}, bf16[448,128]{1,0:T(8,128)(2,1)S(1)}, u32[]{:S(2)}, u32[]{:S(2)}) collective-permute-start(bf16[448,128]{1,0:T(8,128)(2,1)S(1)} %shard_map.103), channel_id=1, source_target_pairs={{0,4},{1,5},{2,6},{3,7},{4,0},{5,1},{6,2},{7,3},{8,12},{9,13},{10,... | collective-permute-start | bytes 344072 | tf_op jit(solution)/shard_map/ppermute | solution.py:284
  57.1 9.8 %collective-permute-start.20 = (bf16[192,128]{1,0:T(8,128)(2,1)S(1)}, bf16[192,128]{1,0:T(8,128)(2,1)S(1)}, u32[]{:S(2)}, u32[]{:S(2)}) collective-permute-start(bf16[192,128]{1,0:T(8,128)(2,1)S(1)} %shard_map.104), channel_id=1, source_target_pairs={{0,4},{1,5},{2,6},{3,7},{4,0},{5,1},{6,2},{7,3},{8,12},{9,13},{10,... | collective-permute-start | bytes 147464 | tf_op jit(solution)/shard_map/ppermute | solution.py:284
  59.8 7.2 %collective-permute-start.21 = (bf16[192,128]{1,0:T(8,128)(2,1)S(1)}, bf16[192,128]{1,0:T(8,128)(2,1)S(1)}, u32[]{:S(2)}, u32[]{:S(2)}) collective-permute-start(bf16[192,128]{1,0:T(8,128)(2,1)S(1)} %shard_map.105), channel_id=1, source_target_pairs={{0,6},{1,7},{2,4},{3,5},{4,2},{5,3},{6,0},{7,1},{8,14},{9,15},{10,... | collective-permute-start | bytes 147464 | tf_op jit(solution)/shard_map/ppermute | solution.py:284

commit v7 on v5

--- a/solution.py
+++ b/solution.py
@@ -9,6 +9,7 @@
 
 
 TILE = 128
+PIECES = 2
 EARLY = (0, 1, 2)
 CONTRACT_LAST = (((1,), (1,)), ((), ()))
 CONTRACT_FIRST = (((0,), (0,)), ((), ()))
@@ -93,8 +94,15 @@
     outs, sems = refs[:-1], refs[-1]
     copies, start = [], 0
     for place, out in enumerate(outs):
-        span = pl.ds(start, out.shape[0])
-        copies.append(pltpu.make_async_copy(whole_ref.at[span], out, sems.at[place]))
+        step = out.shape[0] // PIECES
+        for piece in range(PIECES):
+            copies.append(
+                pltpu.make_async_copy(
+                    whole_ref.at[pl.ds(start + piece * step, step)],
+                    out.at[pl.ds(piece * step, step)],
+                    sems.at[place * PIECES + piece],
+                )
+            )
         start += out.shape[0]
     for copy in copies:
         copy.start()
@@ -285,7 +293,7 @@
 
     top, low = call(
         split_kernel, [grad_out], [((cut, cols), half), ((rows - cut, cols), half)],
-        raw=True, sems=2,
+        raw=True, sems=2 * PIECES,
     )
     top2 = to_chip(top, 2)
     near = to_chip(grad_out, 1)

time: 68 us -> 67.9 us (level)
  no operation moved by 1% of the time
where the time goes in v7:
time: 67.9 us; the launch traced here: 67.7 us
  waiting for transfers between devices  34.6 us (51%)
  starting transfers between devices  24.3 us (36%)
  Pallas kernels  8.65 us (13%)
    ppermute x10, waiting for transfers between devices, to_chip(): return lax.ppermute(x, 'tp', [(t, t ^ 2 * step) for t in range(8)])  27.7 us
    ppermute x10, starting transfers between devices, to_chip(): return lax.ppermute(x, 'tp', [(t, t ^ 2 * step) for t in range(8)])  14.5 us
    pallas_call x16, Pallas kernels, call(): pl.pallas_call(kernel, in_specs=[SMEM if flag else there for flag in ints...  8.65 us
    ppermute x4, starting transfers between devices, to_slab(): return lax.ppermute(x, 'ctx', [(c, c ^ turn) for c in range(slabs)])  7.03 us
    ppermute x4, waiting for transfers between devices, to_slab(): return lax.ppermute(x, 'ctx', [(c, c ^ turn) for c in range(slabs)])  3.66 us
    ppermute x1, waiting for transfers between devices, to_beside(): return lax.ppermute(x, ('ctx', 'tp'), pairs)  2.78 us
    ppermute x1, starting transfers between devices, to_beside(): return lax.ppermute(x, ('ctx', 'tp'), pairs)  1.49 us
  transfers between devices with their start and end apart: 22, of which 11 were waited for; matrix products, arithmetic and copies ran while one was open for 0% of the time, Pallas kernels for 11%

profile of v7, /device:TPU:0, one launch (start us, length us, event | category | flops | bytes accessed | tf_op | source)
XLA Modules:
  0.0 67.7 jit_solution(5441497522575424806)
XLA Ops:
  0.0 0.5 collective-permute-start.3
  0.5 0.0 collective-permute-start.14
  0.5 0.5 collective-permute-start.15
  1.0 0.0 collective-permute-start.16
  1.0 0.9 %shard_map.91 = (bf16[64,640]{1,0:T(8,128)(2,1)S(1)}, bf16[64,640]{1,0:T(8,128)(2,1)S(1)}) custom-call(bf16[128,640]{1,0:T(8,128)(2,1)} %whole_ref.1), custom_call_target="tpu_custom_call" | custom-call | tf_op jit(solution)/shard_map/pallas_call | solution.py:251
  1.9 4.1 %collective-permute-start = (bf16[64,640]{1,0:T(8,128)(2,1)S(1)}, bf16[64,640]{1,0:T(8,128)(2,1)S(1)}, u32[]{:S(2)}, u32[]{:S(2)}) collective-permute-start(bf16[64,640]{1,0:T(8,128)(2,1)S(1)} %get-tuple-element.14.refs_0_), channel_id=1, source_target_pairs={{0,4},{1,5},{2,6},{3,7},{4,0},{5,1},{6,2},{7,3},{8,12},{9,13},{10,... | collective-permute-start | bytes 245768 | tf_op jit(solution)/shard_map/ppermute | solution.py:282
  6.0 4.4 %collective-permute-done.refs_3_ = bf16[64,640]{1,0:T(8,128)(2,1)S(1)} collective-permute-done((bf16[64,640]{1,0:T(8,128)(2,1)S(1)}, bf16[64,640]{1,0:T(8,128)(2,1)S(1)}, u32[]{:S(2)}, u32[]{:S(2)}) %collective-permute-start) | collective-permute-done | bytes 81952 | tf_op jit(solution)/shard_map/ppermute | solution.py:282
  10.4 1.0 %collective-permute-start.5 = (bf16[64,640]{1,0:T(8,128)(2,1)S(1)}, bf16[64,640]{1,0:T(8,128)(2,1)S(1)}, u32[]{:S(2)}, u32[]{:S(2)}) collective-permute-start(bf16[64,640]{1,0:T(8,128)(2,1)S(1)} %get-tuple-element.15.refs_1_), channel_id=1, source_target_pairs={{0,4},{1,5},{2,6},{3,7},{4,0},{5,1},{6,2},{7,3},{8,12},{9,13},{10,... | collective-permute-start | bytes 245768 | tf_op jit(solution)/shard_map/ppermute | solution.py:282
  11.4 6.1 %collective-permute-done.5.refs_4_ = bf16[64,640]{1,0:T(8,128)(2,1)S(1)} collective-permute-done((bf16[64,640]{1,0:T(8,128)(2,1)S(1)}, bf16[64,640]{1,0:T(8,128)(2,1)S(1)}, u32[]{:S(2)}, u32[]{:S(2)}) %collective-permute-start.5) | collective-permute-done | bytes 81952 | tf_op jit(solution)/shard_map/ppermute | solution.py:282
  17.4 0.0 collective-permute-start.4
  17.4 5.5 %collective-permute-done.4.refs_2_ = bf16[128,640]{1,0:T(8,128)(2,1)S(1)} collective-permute-done((bf16[128,640]{1,0:T(8,128)(2,1)}, bf16[128,640]{1,0:T(8,128)(2,1)S(1)}, u32[]{:S(2)}, u32[]{:S(2)}) %collective-permute-start.4) | collective-permute-done | bytes 163872 | tf_op jit(solution)/shard_map/ppermute | solution.py:282
  23.0 2.1 %collective-permute-start.2 = (bf16[64,640]{1,0:T(8,128)(2,1)S(1)}, bf16[64,640]{1,0:T(8,128)(2,1)S(1)}, u32[]{:S(2)}, u32[]{:S(2)}) collective-permute-start(bf16[64,640]{1,0:T(8,128)(2,1)S(1)} %get-tuple-element.15.refs_1_), channel_id=1, source_target_pairs={{0,6},{1,7},{2,4},{3,5},{4,2},{5,3},{6,0},{7,1},{8,14},{9,15},{10,... | collective-permute-start | bytes 245768 | tf_op jit(solution)/shard_map/ppermute | solution.py:282
  25.0 0.0 collective-permute-done.3.refs_6_.refs_3_
  25.0 0.0 collective-permute-start.1
  25.0 1.3 %shard_map.92 = (bf16[128,384]{1,0:T(8,128)(2,1)S(1)}, bf16[128,2560]{1,0:T(8,128)(2,1)S(1)}) custom-call(bf16[128,128]{1,0:T(8,128)(2,1)} %query_ref.1, bf16[128,128]{1,0:T(8,128)(2,1)} %key_ref.1, bf16[128,128]{1,0:T(8,128)(2,1)} %value_ref.1, bf16[128,5120]{1,0:T(8,128)(2,1)} %w_ref.1), custom_call_target="tpu_custom_call" | custom-call | tf_op jit(solution)/shard_map/pallas_call | solution.py:251
  26.3 0.4 shard_map.93.refs_4_
  26.8 0.0 copy-start.3
  26.8 2.5 %collective-permute-done.2.refs_1_ = bf16[64,640]{1,0:T(8,128)(2,1)S(1)} collective-permute-done((bf16[64,640]{1,0:T(8,128)(2,1)S(1)}, bf16[64,640]{1,0:T(8,128)(2,1)S(1)}, u32[]{:S(2)}, u32[]{:S(2)}) %collective-permute-start.2) | collective-permute-done | bytes 81952 | tf_op jit(solution)/shard_map/ppermute | solution.py:282
  29.3 0.8 %collective-permute-done.1.refs_0_ = bf16[64,640]{1,0:T(8,128)(2,1)S(1)} collective-permute-done((bf16[64,640]{1,0:T(8,128)(2,1)S(1)}, bf16[64,640]{1,0:T(8,128)(2,1)S(1)}, u32[]{:S(2)}, u32[]{:S(2)}) %collective-permute-start.1) | collective-permute-done | bytes 81952 | tf_op jit(solution)/shard_map/ppermute | solution.py:282
  30.1 0.2 shard_map.94.own_ref
  30.3 0.1 collective-permute-start.6
  30.4 2.5 %collective-permute-start.12 = (bf16[128,384]{1,0:T(8,128)(2,1)S(1)}, bf16[128,384]{1,0:T(8,128)(2,1)S(1)}, u32[]{:S(2)}, u32[]{:S(2)}) collective-permute-start(bf16[128,384]{1,0:T(8,128)(2,1)S(1)} %get-tuple-element.19.refs_0_), channel_id=1, source_target_pairs={{0,24},{8,16},{16,8},{24,0},{1,25},{9,17},{17,9},{25,1},{2,26},{10... | collective-permute-start | bytes 294920 | tf_op jit(solution)/shard_map/ppermute | solution.py:288
  32.9 0.0 collective-permute-done.6.mate_ref
  32.9 0.5 collective-permute-start.11
  33.5 3.1 %collective-permute-done.12.refs_3_ = bf16[128,384]{1,0:T(8,128)(2,1)S(1)} collective-permute-done((bf16[128,384]{1,0:T(8,128)(2,1)S(1)}, bf16[128,384]{1,0:T(8,128)(2,1)S(1)}, u32[]{:S(2)}, u32[]{:S(2)}) %collective-permute-start.12) | collective-permute-done | bytes 98336 | tf_op jit(solution)/shard_map/ppermute | solution.py:288
  36.6 1.5 %collective-permute-start.10 = (bf16[128,384]{1,0:T(8,128)(2,1)S(1)}, bf16[128,384]{1,0:T(8,128)(2,1)S(1)}, u32[]{:S(2)}, u32[]{:S(2)}) collective-permute-start(bf16[128,384]{1,0:T(8,128)(2,1)S(1)} %get-tuple-element.19.refs_0_), channel_id=1, source_target_pairs={{0,8},{8,0},{16,24},{24,16},{1,9},{9,1},{17,25},{25,17},{2,10},{10... | collective-permute-start | bytes 294920 | tf_op jit(solution)/shard_map/ppermute | solution.py:288
  38.1 0.5 collective-permute-done.11.refs_2_
  38.6 1.5 %collective-permute-start.7 = (bf16[128,256]{1,0:T(8,128)(2,1)S(1)}, bf16[128,256]{1,0:T(8,128)(2,1)S(1)}, u32[]{:S(2)}, u32[]{:S(2)}) collective-permute-start(bf16[128,256]{1,0:T(8,128)(2,1)S(1)} %get-tuple-element.18), channel_id=1, source_target_pairs={{0,8},{1,17},{2,10},{3,19},{4,12},{5,21},{6,14},{7,23},{8,0},{9,25... | collective-permute-start | bytes 196616 | tf_op jit(solution)/shard_map/ppermute | solution.py:292
  40.1 2.8 %collective-permute-done.7.beside = bf16[128,256]{1,0:T(8,128)(2,1)S(1)} collective-permute-done((bf16[128,256]{1,0:T(8,128)(2,1)S(1)}, bf16[128,256]{1,0:T(8,128)(2,1)S(1)}, u32[]{:S(2)}, u32[]{:S(2)}) %collective-permute-start.7) | collective-permute-done | bytes 65568 | tf_op jit(solution)/shard_map/ppermute | solution.py:292
  42.9 0.0 collective-permute-start.8
  42.9 0.0 collective-permute-done.10.refs_1_
  42.9 0.0 copy-start.1
  42.9 2.5 %collective-permute-start.9 = (bf16[128,128]{1,0:T(8,128)(2,1)S(1)}, bf16[128,128]{1,0:T(8,128)(2,1)S(1)}, u32[]{:S(2)}, u32[]{:S(2)}) collective-permute-start(bf16[128,128]{1,0:T(8,128)(2,1)S(1)} %get-tuple-element.17.grad_ref.own), channel_id=1, source_target_pairs={{0,24},{8,16},{16,8},{24,0},{1,25},{9,17},{17,9},{25,1},{2,26},{10... | collective-permute-start | bytes 98312 | tf_op jit(solution)/shard_map/ppermute | solution.py:288
  45.4 0.0 copy-done.3
  45.4 2.1 %shard_map.96 = (f32[128,512]{1,0:T(8,128)S(1)}, f32[512,128]{1,0:T(8,128)S(1)}, f32[512,128]{1,0:T(8,128)S(1)}) custom-call(s32[4,3]{1,0:T(4,128)S(1)} %copy-done.3, bf16[128,384]{1,0:T(8,128)(2,1)S(1)} %get-tuple-element.19.refs_0_, bf16[128,384]{1,0:T(8,128)(2,1)S(1)} %collective-permute-done.10.refs_1_, ...), custom_call_target="tpu_custom_call" | custom-call | tf_op jit(solution)/shard_map/pallas_call | solution.py:251
  47.5 0.3 shard_map.97.refs_4_
  47.8 0.0 collective-permute-done.9.across
  47.9 0.0 collective-permute-done.8.swapped
  47.9 0.5 shard_map.98.own_ref
  48.3 0.2 collective-permute-start.13
  48.5 0.0 copy-done.2
  48.6 0.0 copy-done
  48.6 0.7 shard_map.99.own_ref
  49.2 0.0 collective-permute-done.14.refs_0_
  49.2 0.0 collective-permute-done.15.refs_1_
  49.2 0.0 collective-permute-done.16.refs_2_
  49.3 0.4 collective-permute-done.13.mate_ref
  49.7 0.3 shard_map.102
  50.0 0.3 collective-permute-start.18
  50.3 0.3 shard_map.101
  50.6 1.8 %collective-permute-start.17 = (bf16[640,128]{1,0:T(8,128)(2,1)S(1)}, bf16[640,128]{1,0:T(8,128)(2,1)S(1)}, u32[]{:S(2)}, u32[]{:S(2)}) collective-permute-start(bf16[640,128]{1,0:T(8,128)(2,1)S(1)} %shard_map.101), channel_id=1, source_target_pairs={{0,2},{1,3},{2,0},{3,1},{4,6},{5,7},{6,4},{7,5},{8,10},{9,11},{10,... | collective-permute-start | bytes 491528 | tf_op jit(solution)/shard_map/ppermute | solution.py:282
  52.4 3.6 %collective-permute-done.18.refs_3_ = bf16[448,128]{1,0:T(8,128)(2,1)S(1)} collective-permute-done((bf16[448,128]{1,0:T(8,128)(2,1)S(1)}, bf16[448,128]{1,0:T(8,128)(2,1)S(1)}, u32[]{:S(2)}, u32[]{:S(2)}) %collective-permute-start.18) | collective-permute-done | bytes 114720 | tf_op jit(solution)/shard_map/ppermute | solution.py:282
  56.0 0.3 shard_map.103
  56.3 0.6 collective-permute-start.19
  56.9 0.2 shard_map.104
  57.1 2.4 %collective-permute-start.20 = (bf16[192,128]{1,0:T(8,128)(2,1)S(1)}, bf16[192,128]{1,0:T(8,128)(2,1)S(1)}, u32[]{:S(2)}, u32[]{:S(2)}) collective-permute-start(bf16[192,128]{1,0:T(8,128)(2,1)S(1)} %shard_map.104), channel_id=1, source_target_pairs={{0,4},{1,5},{2,6},{3,7},{4,0},{5,1},{6,2},{7,3},{8,12},{9,13},{10,... | collective-permute-start | bytes 147464 | tf_op jit(solution)/shard_map/ppermute | solution.py:282
  59.6 0.2 shard_map.105
  59.8 2.1 %collective-permute-start.21 = (bf16[192,128]{1,0:T(8,128)(2,1)S(1)}, bf16[192,128]{1,0:T(8,128)(2,1)S(1)}, u32[]{:S(2)}, u32[]{:S(2)}) collective-permute-start(bf16[192,128]{1,0:T(8,128)(2,1)S(1)} %shard_map.105), channel_id=1, source_target_pairs={{0,6},{1,7},{2,4},{3,5},{4,2},{5,3},{6,0},{7,1},{8,14},{9,15},{10,... | collective-permute-start | bytes 147464 | tf_op jit(solution)/shard_map/ppermute | solution.py:282
  61.9 0.3 shard_map.100.own_ref
  62.2 4.8 %collective-permute-done.20.low2 = bf16[192,128]{1,0:T(8,128)(2,1)S(1)} collective-permute-done((bf16[192,128]{1,0:T(8,128)(2,1)S(1)}, bf16[192,128]{1,0:T(8,128)(2,1)S(1)}, u32[]{:S(2)}, u32[]{:S(2)}) %collective-permute-start.20) | collective-permute-done | bytes 49184 | tf_op jit(solution)/shard_map/ppermute | solution.py:282
  66.9 0.0 collective-permute-done.21.low3
  66.9 0.0 collective-permute-done.17.near
  66.9 0.0 collective-permute-done.19.top2
  66.9 0.8 %shard_map.106 = f32[640,128]{1,0:T(8,128)} custom-call(f32[640,128]{1,0:T(8,128)S(1)} %shard_map.100.own_ref, bf16[640,128]{1,0:T(8,128)(2,1)S(1)} %collective-permute-done.17.near, bf16[448,128]{1,0:T(8,128)(2,1)S(1)} %collective-permute-done.19.top2, bf16[192,128]{1,0:T(8,128)(2,1)S(1)} %collective-permute-done.20.low2, ...), custom_call_target="tpu_custom_call" | custom-call | tf_op jit(solution)/shard_map/pallas_call | solution.py:251
  (4 shorter events, 0.0 us)
Async XLA Ops:
  0.0 25.0 %collective-permute-start.3 = (bf16[128,5120]{1,0:T(8,128)(2,1)}, bf16[128,5120]{1,0:T(8,128)(2,1)S(1)}, u32[]{:S(2)}, u32[]{:S(2)}) collective-permute-start(bf16[128,5120]{1,0:T(8,128)(2,1)} %w_ref.1), channel_id=1, source_target_pairs={{0,1},{1,0},{2,3},{3,2},{4,5},{5,4},{6,7},{7,6},{8,9},{9,8},{10,11... | collective-permute-start | bytes 3932168 | tf_op jit(solution)/shard_map/ppermute | solution.py:285
  0.5 48.7 %collective-permute-start.14 = (bf16[5120,128]{1,0:T(8,128)(2,1)}, bf16[5120,128]{1,0:T(8,128)(2,1)S(1)}, u32[]{:S(2)}, u32[]{:S(2)}) collective-permute-start(bf16[5120,128]{1,0:T(8,128)(2,1)} %refs_0_.1), channel_id=1, source_target_pairs={{0,1},{1,0},{2,3},{3,2},{4,5},{5,4},{6,7},{7,6},{8,9},{9,8},{10,11... | collective-permute-start | bytes 3932168 | tf_op jit(solution)/shard_map/ppermute | solution.py:285
  0.5 48.7 %collective-permute-start.15 = (bf16[5120,128]{1,0:T(8,128)(2,1)}, bf16[5120,128]{1,0:T(8,128)(2,1)S(1)}, u32[]{:S(2)}, u32[]{:S(2)}) collective-permute-start(bf16[5120,128]{1,0:T(8,128)(2,1)} %refs_1_.1), channel_id=1, source_target_pairs={{0,1},{1,0},{2,3},{3,2},{4,5},{5,4},{6,7},{7,6},{8,9},{9,8},{10,11... | collective-permute-start | bytes 3932168 | tf_op jit(solution)/shard_map/ppermute | solution.py:285
  1.0 48.2 %collective-permute-start.16 = (bf16[5120,128]{1,0:T(8,128)(2,1)}, bf16[5120,128]{1,0:T(8,128)(2,1)S(1)}, u32[]{:S(2)}, u32[]{:S(2)}) collective-permute-start(bf16[5120,128]{1,0:T(8,128)(2,1)} %refs_2_.1), channel_id=1, source_target_pairs={{0,1},{1,0},{2,3},{3,2},{4,5},{5,4},{6,7},{7,6},{8,9},{9,8},{10,11... | collective-permute-start | bytes 3932168 | tf_op jit(solution)/shard_map/ppermute | solution.py:285
  1.9 8.5 %collective-permute-start = (bf16[64,640]{1,0:T(8,128)(2,1)S(1)}, bf16[64,640]{1,0:T(8,128)(2,1)S(1)}, u32[]{:S(2)}, u32[]{:S(2)}) collective-permute-start(bf16[64,640]{1,0:T(8,128)(2,1)S(1)} %get-tuple-element.14.refs_0_), channel_id=1, source_target_pairs={{0,4},{1,5},{2,6},{3,7},{4,0},{5,1},{6,2},{7,3},{8,12},{9,13},{10,... | collective-permute-start | bytes 245768 | tf_op jit(solution)/shard_map/ppermute | solution.py:282
  10.4 7.0 %collective-permute-start.5 = (bf16[64,640]{1,0:T(8,128)(2,1)S(1)}, bf16[64,640]{1,0:T(8,128)(2,1)S(1)}, u32[]{:S(2)}, u32[]{:S(2)}) collective-permute-start(bf16[64,640]{1,0:T(8,128)(2,1)S(1)} %get-tuple-element.15.refs_1_), channel_id=1, source_target_pairs={{0,4},{1,5},{2,6},{3,7},{4,0},{5,1},{6,2},{7,3},{8,12},{9,13},{10,... | collective-permute-start | bytes 245768 | tf_op jit(solution)/shard_map/ppermute | solution.py:282
  17.4 5.5 %collective-permute-start.4 = (bf16[128,640]{1,0:T(8,128)(2,1)}, bf16[128,640]{1,0:T(8,128)(2,1)S(1)}, u32[]{:S(2)}, u32[]{:S(2)}) collective-permute-start(bf16[128,640]{1,0:T(8,128)(2,1)} %whole_ref.1), channel_id=1, source_target_pairs={{0,2},{1,3},{2,0},{3,1},{4,6},{5,7},{6,4},{7,5},{8,10},{9,11},{10,... | collective-permute-start | bytes 491528 | tf_op jit(solution)/shard_map/ppermute | solution.py:282
  23.0 6.3 %collective-permute-start.2 = (bf16[64,640]{1,0:T(8,128)(2,1)S(1)}, bf16[64,640]{1,0:T(8,128)(2,1)S(1)}, u32[]{:S(2)}, u32[]{:S(2)}) collective-permute-start(bf16[64,640]{1,0:T(8,128)(2,1)S(1)} %get-tuple-element.15.refs_1_), channel_id=1, source_target_pairs={{0,6},{1,7},{2,4},{3,5},{4,2},{5,3},{6,0},{7,1},{8,14},{9,15},{10,... | collective-permute-start | bytes 245768 | tf_op jit(solution)/shard_map/ppermute | solution.py:282
  25.0 5.1 %collective-permute-start.1 = (bf16[64,640]{1,0:T(8,128)(2,1)S(1)}, bf16[64,640]{1,0:T(8,128)(2,1)S(1)}, u32[]{:S(2)}, u32[]{:S(2)}) collective-permute-start(bf16[64,640]{1,0:T(8,128)(2,1)S(1)} %collective-permute-done.refs_3_), channel_id=1, source_target_pairs={{0,2},{1,3},{2,0},{3,1},{4,6},{5,7},{6,4},{7,5},{8,10},{9,11},{10,... | collective-permute-start | bytes 245768 | tf_op jit(solution)/shard_map/ppermute | solution.py:282
  26.8 18.7 %copy-start.3 = (s32[4,3]{1,0:T(4,128)S(1)}, s32[4,3]{1,0:T(4,128)}, u32[]{:S(2)}) copy-start(s32[4,3]{1,0:T(4,128)} %lists_ref.1) | copy-start | bytes 148
  30.1 18.5 %copy-start.2 = (bf16[5120,128]{1,0:T(8,128)(2,1)S(1)}, bf16[5120,128]{1,0:T(8,128)(2,1)}, u32[]{:S(2)}) copy-start(bf16[5120,128]{1,0:T(8,128)(2,1)} %refs_2_.1) | copy-start | bytes 3932164
  30.3 2.6 %collective-permute-start.6 = (f32[128,256]{1,0:T(8,128)S(1)}, f32[128,256]{1,0:T(8,128)S(1)}, u32[]{:S(2)}, u32[]{:S(2)}) collective-permute-start(f32[128,256]{1,0:T(8,128)S(1)} %shard_map.94.own_ref), channel_id=1, source_target_pairs={{0,1},{1,0},{2,3},{3,2},{4,5},{5,4},{6,7},{7,6},{8,9},{9,8},{10,11... | collective-permute-start | bytes 393224 | tf_op jit(solution)/shard_map/ppermute | solution.py:285
  30.4 6.2 %collective-permute-start.12 = (bf16[128,384]{1,0:T(8,128)(2,1)S(1)}, bf16[128,384]{1,0:T(8,128)(2,1)S(1)}, u32[]{:S(2)}, u32[]{:S(2)}) collective-permute-start(bf16[128,384]{1,0:T(8,128)(2,1)S(1)} %get-tuple-element.19.refs_0_), channel_id=1, source_target_pairs={{0,24},{8,16},{16,8},{24,0},{1,25},{9,17},{17,9},{25,1},{2,26},{10... | collective-permute-start | bytes 294920 | tf_op jit(solution)/shard_map/ppermute | solution.py:288
  32.9 5.7 %collective-permute-start.11 = (bf16[128,384]{1,0:T(8,128)(2,1)S(1)}, bf16[128,384]{1,0:T(8,128)(2,1)S(1)}, u32[]{:S(2)}, u32[]{:S(2)}) collective-permute-start(bf16[128,384]{1,0:T(8,128)(2,1)S(1)} %get-tuple-element.19.refs_0_), channel_id=1, source_target_pairs={{0,16},{8,24},{16,0},{24,8},{1,17},{9,25},{17,1},{25,9},{2,18},{10... | collective-permute-start | bytes 294920 | tf_op jit(solution)/shard_map/ppermute | solution.py:288
  36.6 6.3 %collective-permute-start.10 = (bf16[128,384]{1,0:T(8,128)(2,1)S(1)}, bf16[128,384]{1,0:T(8,128)(2,1)S(1)}, u32[]{:S(2)}, u32[]{:S(2)}) collective-permute-start(bf16[128,384]{1,0:T(8,128)(2,1)S(1)} %get-tuple-element.19.refs_0_), channel_id=1, source_target_pairs={{0,8},{8,0},{16,24},{24,16},{1,9},{9,1},{17,25},{25,17},{2,10},{10... | collective-permute-start | bytes 294920 | tf_op jit(solution)/shard_map/ppermute | solution.py:288
  38.6 4.3 %collective-permute-start.7 = (bf16[128,256]{1,0:T(8,128)(2,1)S(1)}, bf16[128,256]{1,0:T(8,128)(2,1)S(1)}, u32[]{:S(2)}, u32[]{:S(2)}) collective-permute-start(bf16[128,256]{1,0:T(8,128)(2,1)S(1)} %get-tuple-element.18), channel_id=1, source_target_pairs={{0,8},{1,17},{2,10},{3,19},{4,12},{5,21},{6,14},{7,23},{8,0},{9,25... | collective-permute-start | bytes 196616 | tf_op jit(solution)/shard_map/ppermute | solution.py:292
  42.9 5.0 %collective-permute-start.8 = (bf16[128,256]{1,0:T(8,128)(2,1)S(1)}, bf16[128,256]{1,0:T(8,128)(2,1)S(1)}, u32[]{:S(2)}, u32[]{:S(2)}) collective-permute-start(bf16[128,256]{1,0:T(8,128)(2,1)S(1)} %collective-permute-done.7.beside), channel_id=1, source_target_pairs={{0,1},{1,0},{2,3},{3,2},{4,5},{5,4},{6,7},{7,6},{8,9},{9,8},{10,11... | collective-permute-start | bytes 196616 | tf_op jit(solution)/shard_map/ppermute | solution.py:285
  42.9 5.7 %copy-start = (bf16[5120,128]{1,0:T(8,128)(2,1)S(1)}, bf16[5120,128]{1,0:T(8,128)(2,1)}, u32[]{:S(2)}) copy-start(bf16[5120,128]{1,0:T(8,128)(2,1)} %refs_0_.1) | copy-start | bytes 3932164
  42.9 5.7 %copy-start.1 = (bf16[5120,128]{1,0:T(8,128)(2,1)S(1)}, bf16[5120,128]{1,0:T(8,128)(2,1)}, u32[]{:S(2)}) copy-start(bf16[5120,128]{1,0:T(8,128)(2,1)} %refs_1_.1) | copy-start | bytes 3932164
  42.9 4.9 %collective-permute-start.9 = (bf16[128,128]{1,0:T(8,128)(2,1)S(1)}, bf16[128,128]{1,0:T(8,128)(2,1)S(1)}, u32[]{:S(2)}, u32[]{:S(2)}) collective-permute-start(bf16[128,128]{1,0:T(8,128)(2,1)S(1)} %get-tuple-element.17.grad_ref.own), channel_id=1, source_target_pairs={{0,24},{8,16},{16,8},{24,0},{1,25},{9,17},{17,9},{25,1},{2,26},{10... | collective-permute-start | bytes 98312 | tf_op jit(solution)/shard_map/ppermute | solution.py:288
  48.3 1.4 %collective-permute-start.13 = (bf16[128,384]{1,0:T(8,128)(2,1)S(1)}, bf16[128,384]{1,0:T(8,128)(2,1)S(1)}, u32[]{:S(2)}, u32[]{:S(2)}) collective-permute-start(bf16[128,384]{1,0:T(8,128)(2,1)S(1)} %shard_map.98.own_ref), channel_id=1, source_target_pairs={{0,1},{1,0},{2,3},{3,2},{4,5},{5,4},{6,7},{7,6},{8,9},{9,8},{10,11... | collective-permute-start | bytes 294920 | tf_op jit(solution)/shard_map/ppermute | solution.py:285
  50.0 6.1 %collective-permute-start.18 = (bf16[448,128]{1,0:T(8,128)(2,1)S(1)}, bf16[448,128]{1,0:T(8,128)(2,1)S(1)}, u32[]{:S(2)}, u32[]{:S(2)}) collective-permute-start(bf16[448,128]{1,0:T(8,128)(2,1)S(1)} %shard_map.102), channel_id=1, source_target_pairs={{0,2},{1,3},{2,0},{3,1},{4,6},{5,7},{6,4},{7,5},{8,10},{9,11},{10,... | collective-permute-start | bytes 344072 | tf_op jit(solution)/shard_map/ppermute | solution.py:282
  50.6 16.4 %collective-permute-start.17 = (bf16[640,128]{1,0:T(8,128)(2,1)S(1)}, bf16[640,128]{1,0:T(8,128)(2,1)S(1)}, u32[]{:S(2)}, u32[]{:S(2)}) collective-permute-start(bf16[640,128]{1,0:T(8,128)(2,1)S(1)} %shard_map.101), channel_id=1, source_target_pairs={{0,2},{1,3},{2,0},{3,1},{4,6},{5,7},{6,4},{7,5},{8,10},{9,11},{10,... | collective-permute-start | bytes 491528 | tf_op jit(solution)/shard_map/ppermute | solution.py:282
  56.3 10.6 %collective-permute-start.19 = (bf16[448,128]{1,0:T(8,128)(2,1)S(1)}, bf16[448,128]{1,0:T(8,128)(2,1)S(1)}, u32[]{:S(2)}, u32[]{:S(2)}) collective-permute-start(bf16[448,128]{1,0:T(8,128)(2,1)S(1)} %shard_map.103), channel_id=1, source_target_pairs={{0,4},{1,5},{2,6},{3,7},{4,0},{5,1},{6,2},{7,3},{8,12},{9,13},{10,... | collective-permute-start | bytes 344072 | tf_op jit(solution)/shard_map/ppermute | solution.py:282
  57.1 9.8 %collective-permute-start.20 = (bf16[192,128]{1,0:T(8,128)(2,1)S(1)}, bf16[192,128]{1,0:T(8,128)(2,1)S(1)}, u32[]{:S(2)}, u32[]{:S(2)}) collective-permute-start(bf16[192,128]{1,0:T(8,128)(2,1)S(1)} %shard_map.104), channel_id=1, source_target_pairs={{0,4},{1,5},{2,6},{3,7},{4,0},{5,1},{6,2},{7,3},{8,12},{9,13},{10,... | collective-permute-start | bytes 147464 | tf_op jit(solution)/shard_map/ppermute | solution.py:282
  59.8 7.2 %collective-permute-start.21 = (bf16[192,128]{1,0:T(8,128)(2,1)S(1)}, bf16[192,128]{1,0:T(8,128)(2,1)S(1)}, u32[]{:S(2)}, u32[]{:S(2)}) collective-permute-start(bf16[192,128]{1,0:T(8,128)(2,1)S(1)} %shard_map.105), channel_id=1, source_target_pairs={{0,6},{1,7},{2,4},{3,5},{4,2},{5,3},{6,0},{7,1},{8,14},{9,15},{10,... | collective-permute-start | bytes 147464 | tf_op jit(solution)/shard_map/ppermute | solution.py:282

commit v8 on v5

--- a/solution.py
+++ b/solution.py
@@ -225,14 +225,6 @@
     out_ref[...] = total.astype(out_ref.dtype)
 
 
-def sum_kernel(own_ref, near, top2, low2, low3, out_ref):
-    full = jnp.float32
-    cut = top2.shape[0]
-    out_ref[:cut, :] = own_ref[:cut, :] + near[:cut, :].astype(full) + top2[...].astype(full)
-    low = low2[...].astype(full) + low3[...].astype(full)
-    out_ref[cut:, :] = own_ref[cut:, :] + near[cut:, :].astype(full) + low
-
-
 def call(kernel, args, outs, fast_out=True, raw=False, sems=0):
     ints = [x.dtype == jnp.int32 for x in args]
     space = pltpu.HBM if raw else pltpu.VMEM
@@ -353,12 +345,10 @@
     low2 = to_chip(project(2, feature_cut, rest, half), 2)
     near = to_chip(project(1, 0, cols, half), 1)
     top2 = to_chip(project(2, 0, feature_cut, half, fed), 2)
-    (out,) = call(
-        sum_kernel,
-        [project(0, 0, cols, full), near, top2, low2, low3],
-        [((cols, rows), full)],
-        fast_out=False,
-    )
+    own = project(0, 0, cols, full)
+    through = jnp.concatenate([top2, low2], axis=0).astype(full)
+    low3 = jnp.pad(low3, ((feature_cut, 0), (0, 0))).astype(full)
+    out = own + near.astype(full) + through + low3
     return out
 
 

time: 68 us -> 68 us (level)
  Pallas kernels: 8.72 us -> 7.94 us
  other arithmetic: 0 us -> 0.78 us
    add x0 -> x1, other arithmetic: none -> 0.78 us  [few_slabs(): out = own + near.astype(full) + through + low3]
    pallas_call x16 -> x15, Pallas kernels: 8.72 us -> 7.94 us  [call(): pl.pallas_call(kernel, in_specs=[SMEM if flag else there for flag in ints...]
where the time goes in v8:
time: 68 us; the launch traced here: 67.8 us
  waiting for transfers between devices  34.5 us (51%)
  starting transfers between devices  24.3 us (36%)
  Pallas kernels  7.94 us (12%)
  other arithmetic  0.78 us (1%)
    ppermute x10, waiting for transfers between devices, to_chip(): return lax.ppermute(x, 'tp', [(t, t ^ 2 * step) for t in range(8)])  27.7 us
    ppermute x10, starting transfers between devices, to_chip(): return lax.ppermute(x, 'tp', [(t, t ^ 2 * step) for t in range(8)])  14.5 us
    pallas_call x15, Pallas kernels, call(): pl.pallas_call(kernel, in_specs=[SMEM if flag else there for flag in ints...  7.94 us
    ppermute x4, starting transfers between devices, to_slab(): return lax.ppermute(x, 'ctx', [(c, c ^ turn) for c in range(slabs)])  7.05 us
    ppermute x4, waiting for transfers between devices, to_slab(): return lax.ppermute(x, 'ctx', [(c, c ^ turn) for c in range(slabs)])  3.65 us
    ppermute x1, waiting for transfers between devices, to_beside(): return lax.ppermute(x, ('ctx', 'tp'), pairs)  2.77 us
    ppermute x1, starting transfers between devices, to_beside(): return lax.ppermute(x, ('ctx', 'tp'), pairs)  1.5 us
  transfers between devices with their start and end apart: 22, of which 11 were waited for; matrix products, arithmetic and copies ran while one was open for 0% of the time, Pallas kernels for 11%

profile of v8, /device:TPU:0, one launch (start us, length us, event | category | flops | bytes accessed | tf_op | source)
XLA Modules:
  0.0 67.8 jit_solution(8412253381835438050)
XLA Ops:
  0.0 0.5 collective-permute-start.3
  0.5 0.0 collective-permute-start.14
  0.5 0.5 collective-permute-start.15
  1.0 0.0 collective-permute-start.16
  1.0 0.9 %shard_map.91 = (bf16[64,640]{1,0:T(8,128)(2,1)S(1)}, bf16[64,640]{1,0:T(8,128)(2,1)S(1)}) custom-call(bf16[128,640]{1,0:T(8,128)(2,1)} %whole_ref.1), custom_call_target="tpu_custom_call" | custom-call | tf_op jit(solution)/shard_map/pallas_call | solution.py:235
  2.0 4.1 %collective-permute-start = (bf16[64,640]{1,0:T(8,128)(2,1)S(1)}, bf16[64,640]{1,0:T(8,128)(2,1)S(1)}, u32[]{:S(2)}, u32[]{:S(2)}) collective-permute-start(bf16[64,640]{1,0:T(8,128)(2,1)S(1)} %get-tuple-element.14.refs_0_), channel_id=1, source_target_pairs={{0,4},{1,5},{2,6},{3,7},{4,0},{5,1},{6,2},{7,3},{8,12},{9,13},{10,... | collective-permute-start | bytes 245768 | tf_op jit(solution)/shard_map/ppermute | solution.py:266
  6.1 4.4 %collective-permute-done.refs_3_ = bf16[64,640]{1,0:T(8,128)(2,1)S(1)} collective-permute-done((bf16[64,640]{1,0:T(8,128)(2,1)S(1)}, bf16[64,640]{1,0:T(8,128)(2,1)S(1)}, u32[]{:S(2)}, u32[]{:S(2)}) %collective-permute-start) | collective-permute-done | bytes 81952 | tf_op jit(solution)/shard_map/ppermute | solution.py:266
  10.5 1.0 %collective-permute-start.5 = (bf16[64,640]{1,0:T(8,128)(2,1)S(1)}, bf16[64,640]{1,0:T(8,128)(2,1)S(1)}, u32[]{:S(2)}, u32[]{:S(2)}) collective-permute-start(bf16[64,640]{1,0:T(8,128)(2,1)S(1)} %get-tuple-element.15.refs_1_), channel_id=1, source_target_pairs={{0,4},{1,5},{2,6},{3,7},{4,0},{5,1},{6,2},{7,3},{8,12},{9,13},{10,... | collective-permute-start | bytes 245768 | tf_op jit(solution)/shard_map/ppermute | solution.py:266
  11.5 6.1 %collective-permute-done.5.refs_4_ = bf16[64,640]{1,0:T(8,128)(2,1)S(1)} collective-permute-done((bf16[64,640]{1,0:T(8,128)(2,1)S(1)}, bf16[64,640]{1,0:T(8,128)(2,1)S(1)}, u32[]{:S(2)}, u32[]{:S(2)}) %collective-permute-start.5) | collective-permute-done | bytes 81952 | tf_op jit(solution)/shard_map/ppermute | solution.py:266
  17.5 0.0 collective-permute-start.4
  17.5 5.5 %collective-permute-done.4.refs_2_ = bf16[128,640]{1,0:T(8,128)(2,1)S(1)} collective-permute-done((bf16[128,640]{1,0:T(8,128)(2,1)}, bf16[128,640]{1,0:T(8,128)(2,1)S(1)}, u32[]{:S(2)}, u32[]{:S(2)}) %collective-permute-start.4) | collective-permute-done | bytes 163872 | tf_op jit(solution)/shard_map/ppermute | solution.py:266
  23.0 2.1 %collective-permute-start.2 = (bf16[64,640]{1,0:T(8,128)(2,1)S(1)}, bf16[64,640]{1,0:T(8,128)(2,1)S(1)}, u32[]{:S(2)}, u32[]{:S(2)}) collective-permute-start(bf16[64,640]{1,0:T(8,128)(2,1)S(1)} %get-tuple-element.15.refs_1_), channel_id=1, source_target_pairs={{0,6},{1,7},{2,4},{3,5},{4,2},{5,3},{6,0},{7,1},{8,14},{9,15},{10,... | collective-permute-start | bytes 245768 | tf_op jit(solution)/shard_map/ppermute | solution.py:266
  25.1 0.0 collective-permute-done.3.refs_6_.refs_3_
  25.1 0.0 collective-permute-start.1
  25.1 1.3 %shard_map.92 = (bf16[128,384]{1,0:T(8,128)(2,1)S(1)}, bf16[128,2560]{1,0:T(8,128)(2,1)S(1)}) custom-call(bf16[128,128]{1,0:T(8,128)(2,1)} %query_ref.1, bf16[128,128]{1,0:T(8,128)(2,1)} %key_ref.1, bf16[128,128]{1,0:T(8,128)(2,1)} %value_ref.1, bf16[128,5120]{1,0:T(8,128)(2,1)} %w_ref.1), custom_call_target="tpu_custom_call" | custom-call | tf_op jit(solution)/shard_map/pallas_call | solution.py:235
  26.4 0.4 shard_map.93.refs_4_
  26.8 0.0 copy-start.3
  26.8 2.5 %collective-permute-done.2.refs_1_ = bf16[64,640]{1,0:T(8,128)(2,1)S(1)} collective-permute-done((bf16[64,640]{1,0:T(8,128)(2,1)S(1)}, bf16[64,640]{1,0:T(8,128)(2,1)S(1)}, u32[]{:S(2)}, u32[]{:S(2)}) %collective-permute-start.2) | collective-permute-done | bytes 81952 | tf_op jit(solution)/shard_map/ppermute | solution.py:266
  29.3 0.8 %collective-permute-done.1.refs_0_ = bf16[64,640]{1,0:T(8,128)(2,1)S(1)} collective-permute-done((bf16[64,640]{1,0:T(8,128)(2,1)S(1)}, bf16[64,640]{1,0:T(8,128)(2,1)S(1)}, u32[]{:S(2)}, u32[]{:S(2)}) %collective-permute-start.1) | collective-permute-done | bytes 81952 | tf_op jit(solution)/shard_map/ppermute | solution.py:266
  30.2 0.2 shard_map.94.own_ref
  30.4 0.1 collective-permute-start.6
  30.5 2.5 %collective-permute-start.12 = (bf16[128,384]{1,0:T(8,128)(2,1)S(1)}, bf16[128,384]{1,0:T(8,128)(2,1)S(1)}, u32[]{:S(2)}, u32[]{:S(2)}) collective-permute-start(bf16[128,384]{1,0:T(8,128)(2,1)S(1)} %get-tuple-element.19.refs_0_), channel_id=1, source_target_pairs={{0,24},{8,16},{16,8},{24,0},{1,25},{9,17},{17,9},{25,1},{2,26},{10... | collective-permute-start | bytes 294920 | tf_op jit(solution)/shard_map/ppermute | solution.py:272
  33.0 0.0 collective-permute-done.6.mate_ref
  33.0 0.5 collective-permute-start.11
  33.5 3.1 %collective-permute-done.12.refs_3_ = bf16[128,384]{1,0:T(8,128)(2,1)S(1)} collective-permute-done((bf16[128,384]{1,0:T(8,128)(2,1)S(1)}, bf16[128,384]{1,0:T(8,128)(2,1)S(1)}, u32[]{:S(2)}, u32[]{:S(2)}) %collective-permute-start.12) | collective-permute-done | bytes 98336 | tf_op jit(solution)/shard_map/ppermute | solution.py:272
  36.7 1.5 %collective-permute-start.10 = (bf16[128,384]{1,0:T(8,128)(2,1)S(1)}, bf16[128,384]{1,0:T(8,128)(2,1)S(1)}, u32[]{:S(2)}, u32[]{:S(2)}) collective-permute-start(bf16[128,384]{1,0:T(8,128)(2,1)S(1)} %get-tuple-element.19.refs_0_), channel_id=1, source_target_pairs={{0,8},{8,0},{16,24},{24,16},{1,9},{9,1},{17,25},{25,17},{2,10},{10... | collective-permute-start | bytes 294920 | tf_op jit(solution)/shard_map/ppermute | solution.py:272
  38.2 0.5 collective-permute-done.11.refs_2_
  38.7 1.5 %collective-permute-start.7 = (bf16[128,256]{1,0:T(8,128)(2,1)S(1)}, bf16[128,256]{1,0:T(8,128)(2,1)S(1)}, u32[]{:S(2)}, u32[]{:S(2)}) collective-permute-start(bf16[128,256]{1,0:T(8,128)(2,1)S(1)} %get-tuple-element.18), channel_id=1, source_target_pairs={{0,8},{1,17},{2,10},{3,19},{4,12},{5,21},{6,14},{7,23},{8,0},{9,25... | collective-permute-start | bytes 196616 | tf_op jit(solution)/shard_map/ppermute | solution.py:276
  40.2 2.8 %collective-permute-done.7.beside = bf16[128,256]{1,0:T(8,128)(2,1)S(1)} collective-permute-done((bf16[128,256]{1,0:T(8,128)(2,1)S(1)}, bf16[128,256]{1,0:T(8,128)(2,1)S(1)}, u32[]{:S(2)}, u32[]{:S(2)}) %collective-permute-start.7) | collective-permute-done | bytes 65568 | tf_op jit(solution)/shard_map/ppermute | solution.py:276
  43.0 0.0 collective-permute-start.8
  43.0 0.0 collective-permute-done.10.refs_1_
  43.0 0.0 copy-start.1
  43.0 2.5 %collective-permute-start.9 = (bf16[128,128]{1,0:T(8,128)(2,1)S(1)}, bf16[128,128]{1,0:T(8,128)(2,1)S(1)}, u32[]{:S(2)}, u32[]{:S(2)}) collective-permute-start(bf16[128,128]{1,0:T(8,128)(2,1)S(1)} %get-tuple-element.17.grad_ref.own), channel_id=1, source_target_pairs={{0,24},{8,16},{16,8},{24,0},{1,25},{9,17},{17,9},{25,1},{2,26},{10... | collective-permute-start | bytes 98312 | tf_op jit(solution)/shard_map/ppermute | solution.py:272
  45.5 0.0 copy-done.3
  45.5 2.1 %shard_map.96 = (f32[128,512]{1,0:T(8,128)S(1)}, f32[512,128]{1,0:T(8,128)S(1)}, f32[512,128]{1,0:T(8,128)S(1)}) custom-call(s32[4,3]{1,0:T(4,128)S(1)} %copy-done.3, bf16[128,384]{1,0:T(8,128)(2,1)S(1)} %get-tuple-element.19.refs_0_, bf16[128,384]{1,0:T(8,128)(2,1)S(1)} %collective-permute-done.10.refs_1_, ...), custom_call_target="tpu_custom_call" | custom-call | tf_op jit(solution)/shard_map/pallas_call | solution.py:235
  47.6 0.3 shard_map.97.refs_4_
  47.9 0.0 collective-permute-done.9.across
  47.9 0.0 collective-permute-done.8.swapped
  47.9 0.5 shard_map.98.own_ref
  48.4 0.2 collective-permute-start.13
  48.6 0.0 copy-done.2
  48.6 0.0 copy-done
  48.6 0.7 shard_map.99.own_ref
  49.3 0.0 collective-permute-done.14.refs_0_
  49.3 0.0 collective-permute-done.15.refs_1_
  49.3 0.0 collective-permute-done.16.refs_2_
  49.3 0.4 collective-permute-done.13.mate_ref
  49.8 0.3 shard_map.102
  50.0 0.3 collective-permute-start.18
  50.4 0.3 shard_map.101
  50.7 1.8 %collective-permute-start.17 = (bf16[640,128]{1,0:T(8,128)(2,1)S(1)}, bf16[640,128]{1,0:T(8,128)(2,1)S(1)}, u32[]{:S(2)}, u32[]{:S(2)}) collective-permute-start(bf16[640,128]{1,0:T(8,128)(2,1)S(1)} %shard_map.101), channel_id=1, source_target_pairs={{0,2},{1,3},{2,0},{3,1},{4,6},{5,7},{6,4},{7,5},{8,10},{9,11},{10,... | collective-permute-start | bytes 491528 | tf_op jit(solution)/shard_map/ppermute | solution.py:266
  52.5 3.6 %collective-permute-done.18.refs_3_ = bf16[448,128]{1,0:T(8,128)(2,1)S(1)} collective-permute-done((bf16[448,128]{1,0:T(8,128)(2,1)S(1)}, bf16[448,128]{1,0:T(8,128)(2,1)S(1)}, u32[]{:S(2)}, u32[]{:S(2)}) %collective-permute-start.18) | collective-permute-done | bytes 114720 | tf_op jit(solution)/shard_map/ppermute | solution.py:266
  56.1 0.3 shard_map.103
  56.4 0.6 collective-permute-start.19
  57.0 0.2 shard_map.104
  57.2 2.4 %collective-permute-start.20 = (bf16[192,128]{1,0:T(8,128)(2,1)S(1)}, bf16[192,128]{1,0:T(8,128)(2,1)S(1)}, u32[]{:S(2)}, u32[]{:S(2)}) collective-permute-start(bf16[192,128]{1,0:T(8,128)(2,1)S(1)} %shard_map.104), channel_id=1, source_target_pairs={{0,4},{1,5},{2,6},{3,7},{4,0},{5,1},{6,2},{7,3},{8,12},{9,13},{10,... | collective-permute-start | bytes 147464 | tf_op jit(solution)/shard_map/ppermute | solution.py:266
  59.6 0.2 shard_map.105
  59.9 2.1 %collective-permute-start.21 = (bf16[192,128]{1,0:T(8,128)(2,1)S(1)}, bf16[192,128]{1,0:T(8,128)(2,1)S(1)}, u32[]{:S(2)}, u32[]{:S(2)}) collective-permute-start(bf16[192,128]{1,0:T(8,128)(2,1)S(1)} %shard_map.105), channel_id=1, source_target_pairs={{0,6},{1,7},{2,4},{3,5},{4,2},{5,3},{6,0},{7,1},{8,14},{9,15},{10,... | collective-permute-start | bytes 147464 | tf_op jit(solution)/shard_map/ppermute | solution.py:266
  61.9 0.3 shard_map.100
  62.2 4.8 %collective-permute-done.20 = bf16[192,128]{1,0:T(8,128)(2,1)S(1)} collective-permute-done((bf16[192,128]{1,0:T(8,128)(2,1)S(1)}, bf16[192,128]{1,0:T(8,128)(2,1)S(1)}, u32[]{:S(2)}, u32[]{:S(2)}) %collective-permute-start.20) | collective-permute-done | bytes 49184 | tf_op jit(solution)/shard_map/ppermute | solution.py:266
  67.0 0.0 collective-permute-done.21
  67.0 0.0 collective-permute-done.17
  67.0 0.0 collective-permute-done.19
  67.0 0.8 %convert_add_fusion = f32[640,128]{1,0:T(8,128)} fusion(f32[640,128]{1,0:T(8,128)S(1)} %shard_map.100, bf16[640,128]{1,0:T(8,128)(2,1)S(1)} %collective-permute-done.17, bf16[192,128]{1,0:T(8,128)(2,1)S(1)} %collective-permute-done.20, bf16[448,128]{1,0:T(8,128)(2,1)S(1)} %collective-permute-done.19, bf16[192,128]{1,0:T(8,128)(2,1)S(1)} %collective-permute-done.21), kind=kLoop, calls=%fused_computation | loop fusion | flops 737280 | bytes 1032192 | tf_op jit(solution)/shard_map/add | solution.py:351
  (4 shorter events, 0.0 us)
Async XLA Ops:
  0.0 25.1 %collective-permute-start.3 = (bf16[128,5120]{1,0:T(8,128)(2,1)}, bf16[128,5120]{1,0:T(8,128)(2,1)S(1)}, u32[]{:S(2)}, u32[]{:S(2)}) collective-permute-start(bf16[128,5120]{1,0:T(8,128)(2,1)} %w_ref.1), channel_id=1, source_target_pairs={{0,1},{1,0},{2,3},{3,2},{4,5},{5,4},{6,7},{7,6},{8,9},{9,8},{10,11... | collective-permute-start | bytes 3932168 | tf_op jit(solution)/shard_map/ppermute | solution.py:269
  0.5 48.8 %collective-permute-start.14 = (bf16[5120,128]{1,0:T(8,128)(2,1)}, bf16[5120,128]{1,0:T(8,128)(2,1)S(1)}, u32[]{:S(2)}, u32[]{:S(2)}) collective-permute-start(bf16[5120,128]{1,0:T(8,128)(2,1)} %refs_0_.1), channel_id=1, source_target_pairs={{0,1},{1,0},{2,3},{3,2},{4,5},{5,4},{6,7},{7,6},{8,9},{9,8},{10,11... | collective-permute-start | bytes 3932168 | tf_op jit(solution)/shard_map/ppermute | solution.py:269
  0.5 48.8 %collective-permute-start.15 = (bf16[5120,128]{1,0:T(8,128)(2,1)}, bf16[5120,128]{1,0:T(8,128)(2,1)S(1)}, u32[]{:S(2)}, u32[]{:S(2)}) collective-permute-start(bf16[5120,128]{1,0:T(8,128)(2,1)} %refs_1_.1), channel_id=1, source_target_pairs={{0,1},{1,0},{2,3},{3,2},{4,5},{5,4},{6,7},{7,6},{8,9},{9,8},{10,11... | collective-permute-start | bytes 3932168 | tf_op jit(solution)/shard_map/ppermute | solution.py:269
  1.0 48.3 %collective-permute-start.16 = (bf16[5120,128]{1,0:T(8,128)(2,1)}, bf16[5120,128]{1,0:T(8,128)(2,1)S(1)}, u32[]{:S(2)}, u32[]{:S(2)}) collective-permute-start(bf16[5120,128]{1,0:T(8,128)(2,1)} %refs_2_.1), channel_id=1, source_target_pairs={{0,1},{1,0},{2,3},{3,2},{4,5},{5,4},{6,7},{7,6},{8,9},{9,8},{10,11... | collective-permute-start | bytes 3932168 | tf_op jit(solution)/shard_map/ppermute | solution.py:269
  2.0 8.5 %collective-permute-start = (bf16[64,640]{1,0:T(8,128)(2,1)S(1)}, bf16[64,640]{1,0:T(8,128)(2,1)S(1)}, u32[]{:S(2)}, u32[]{:S(2)}) collective-permute-start(bf16[64,640]{1,0:T(8,128)(2,1)S(1)} %get-tuple-element.14.refs_0_), channel_id=1, source_target_pairs={{0,4},{1,5},{2,6},{3,7},{4,0},{5,1},{6,2},{7,3},{8,12},{9,13},{10,... | collective-permute-start | bytes 245768 | tf_op jit(solution)/shard_map/ppermute | solution.py:266
  10.5 7.0 %collective-permute-start.5 = (bf16[64,640]{1,0:T(8,128)(2,1)S(1)}, bf16[64,640]{1,0:T(8,128)(2,1)S(1)}, u32[]{:S(2)}, u32[]{:S(2)}) collective-permute-start(bf16[64,640]{1,0:T(8,128)(2,1)S(1)} %get-tuple-element.15.refs_1_), channel_id=1, source_target_pairs={{0,4},{1,5},{2,6},{3,7},{4,0},{5,1},{6,2},{7,3},{8,12},{9,13},{10,... | collective-permute-start | bytes 245768 | tf_op jit(solution)/shard_map/ppermute | solution.py:266
  17.5 5.5 %collective-permute-start.4 = (bf16[128,640]{1,0:T(8,128)(2,1)}, bf16[128,640]{1,0:T(8,128)(2,1)S(1)}, u32[]{:S(2)}, u32[]{:S(2)}) collective-permute-start(bf16[128,640]{1,0:T(8,128)(2,1)} %whole_ref.1), channel_id=1, source_target_pairs={{0,2},{1,3},{2,0},{3,1},{4,6},{5,7},{6,4},{7,5},{8,10},{9,11},{10,... | collective-permute-start | bytes 491528 | tf_op jit(solution)/shard_map/ppermute | solution.py:266
  23.0 6.3 %collective-permute-start.2 = (bf16[64,640]{1,0:T(8,128)(2,1)S(1)}, bf16[64,640]{1,0:T(8,128)(2,1)S(1)}, u32[]{:S(2)}, u32[]{:S(2)}) collective-permute-start(bf16[64,640]{1,0:T(8,128)(2,1)S(1)} %get-tuple-element.15.refs_1_), channel_id=1, source_target_pairs={{0,6},{1,7},{2,4},{3,5},{4,2},{5,3},{6,0},{7,1},{8,14},{9,15},{10,... | collective-permute-start | bytes 245768 | tf_op jit(solution)/shard_map/ppermute | solution.py:266
  25.1 5.1 %collective-permute-start.1 = (bf16[64,640]{1,0:T(8,128)(2,1)S(1)}, bf16[64,640]{1,0:T(8,128)(2,1)S(1)}, u32[]{:S(2)}, u32[]{:S(2)}) collective-permute-start(bf16[64,640]{1,0:T(8,128)(2,1)S(1)} %collective-permute-done.refs_3_), channel_id=1, source_target_pairs={{0,2},{1,3},{2,0},{3,1},{4,6},{5,7},{6,4},{7,5},{8,10},{9,11},{10,... | collective-permute-start | bytes 245768 | tf_op jit(solution)/shard_map/ppermute | solution.py:266
  26.8 18.7 %copy-start.3 = (s32[4,3]{1,0:T(4,128)S(1)}, s32[4,3]{1,0:T(4,128)}, u32[]{:S(2)}) copy-start(s32[4,3]{1,0:T(4,128)} %lists_ref.1) | copy-start | bytes 148
  30.2 18.5 %copy-start.2 = (bf16[5120,128]{1,0:T(8,128)(2,1)S(1)}, bf16[5120,128]{1,0:T(8,128)(2,1)}, u32[]{:S(2)}) copy-start(bf16[5120,128]{1,0:T(8,128)(2,1)} %refs_2_.1) | copy-start | bytes 3932164
  30.4 2.6 %collective-permute-start.6 = (f32[128,256]{1,0:T(8,128)S(1)}, f32[128,256]{1,0:T(8,128)S(1)}, u32[]{:S(2)}, u32[]{:S(2)}) collective-permute-start(f32[128,256]{1,0:T(8,128)S(1)} %shard_map.94.own_ref), channel_id=1, source_target_pairs={{0,1},{1,0},{2,3},{3,2},{4,5},{5,4},{6,7},{7,6},{8,9},{9,8},{10,11... | collective-permute-start | bytes 393224 | tf_op jit(solution)/shard_map/ppermute | solution.py:269
  30.5 6.2 %collective-permute-start.12 = (bf16[128,384]{1,0:T(8,128)(2,1)S(1)}, bf16[128,384]{1,0:T(8,128)(2,1)S(1)}, u32[]{:S(2)}, u32[]{:S(2)}) collective-permute-start(bf16[128,384]{1,0:T(8,128)(2,1)S(1)} %get-tuple-element.19.refs_0_), channel_id=1, source_target_pairs={{0,24},{8,16},{16,8},{24,0},{1,25},{9,17},{17,9},{25,1},{2,26},{10... | collective-permute-start | bytes 294920 | tf_op jit(solution)/shard_map/ppermute | solution.py:272
  33.0 5.7 %collective-permute-start.11 = (bf16[128,384]{1,0:T(8,128)(2,1)S(1)}, bf16[128,384]{1,0:T(8,128)(2,1)S(1)}, u32[]{:S(2)}, u32[]{:S(2)}) collective-permute-start(bf16[128,384]{1,0:T(8,128)(2,1)S(1)} %get-tuple-element.19.refs_0_), channel_id=1, source_target_pairs={{0,16},{8,24},{16,0},{24,8},{1,17},{9,25},{17,1},{25,9},{2,18},{10... | collective-permute-start | bytes 294920 | tf_op jit(solution)/shard_map/ppermute | solution.py:272
  36.7 6.3 %collective-permute-start.10 = (bf16[128,384]{1,0:T(8,128)(2,1)S(1)}, bf16[128,384]{1,0:T(8,128)(2,1)S(1)}, u32[]{:S(2)}, u32[]{:S(2)}) collective-permute-start(bf16[128,384]{1,0:T(8,128)(2,1)S(1)} %get-tuple-element.19.refs_0_), channel_id=1, source_target_pairs={{0,8},{8,0},{16,24},{24,16},{1,9},{9,1},{17,25},{25,17},{2,10},{10... | collective-permute-start | bytes 294920 | tf_op jit(solution)/shard_map/ppermute | solution.py:272
  38.7 4.3 %collective-permute-start.7 = (bf16[128,256]{1,0:T(8,128)(2,1)S(1)}, bf16[128,256]{1,0:T(8,128)(2,1)S(1)}, u32[]{:S(2)}, u32[]{:S(2)}) collective-permute-start(bf16[128,256]{1,0:T(8,128)(2,1)S(1)} %get-tuple-element.18), channel_id=1, source_target_pairs={{0,8},{1,17},{2,10},{3,19},{4,12},{5,21},{6,14},{7,23},{8,0},{9,25... | collective-permute-start | bytes 196616 | tf_op jit(solution)/shard_map/ppermute | solution.py:276
  43.0 5.0 %collective-permute-start.8 = (bf16[128,256]{1,0:T(8,128)(2,1)S(1)}, bf16[128,256]{1,0:T(8,128)(2,1)S(1)}, u32[]{:S(2)}, u32[]{:S(2)}) collective-permute-start(bf16[128,256]{1,0:T(8,128)(2,1)S(1)} %collective-permute-done.7.beside), channel_id=1, source_target_pairs={{0,1},{1,0},{2,3},{3,2},{4,5},{5,4},{6,7},{7,6},{8,9},{9,8},{10,11... | collective-permute-start | bytes 196616 | tf_op jit(solution)/shard_map/ppermute | solution.py:269
  43.0 5.7 %copy-start = (bf16[5120,128]{1,0:T(8,128)(2,1)S(1)}, bf16[5120,128]{1,0:T(8,128)(2,1)}, u32[]{:S(2)}) copy-start(bf16[5120,128]{1,0:T(8,128)(2,1)} %refs_0_.1) | copy-start | bytes 3932164
  43.0 5.7 %copy-start.1 = (bf16[5120,128]{1,0:T(8,128)(2,1)S(1)}, bf16[5120,128]{1,0:T(8,128)(2,1)}, u32[]{:S(2)}) copy-start(bf16[5120,128]{1,0:T(8,128)(2,1)} %refs_1_.1) | copy-start | bytes 3932164
  43.0 4.9 %collective-permute-start.9 = (bf16[128,128]{1,0:T(8,128)(2,1)S(1)}, bf16[128,128]{1,0:T(8,128)(2,1)S(1)}, u32[]{:S(2)}, u32[]{:S(2)}) collective-permute-start(bf16[128,128]{1,0:T(8,128)(2,1)S(1)} %get-tuple-element.17.grad_ref.own), channel_id=1, source_target_pairs={{0,24},{8,16},{16,8},{24,0},{1,25},{9,17},{17,9},{25,1},{2,26},{10... | collective-permute-start | bytes 98312 | tf_op jit(solution)/shard_map/ppermute | solution.py:272
  48.4 1.4 %collective-permute-start.13 = (bf16[128,384]{1,0:T(8,128)(2,1)S(1)}, bf16[128,384]{1,0:T(8,128)(2,1)S(1)}, u32[]{:S(2)}, u32[]{:S(2)}) collective-permute-start(bf16[128,384]{1,0:T(8,128)(2,1)S(1)} %shard_map.98.own_ref), channel_id=1, source_target_pairs={{0,1},{1,0},{2,3},{3,2},{4,5},{5,4},{6,7},{7,6},{8,9},{9,8},{10,11... | collective-permute-start | bytes 294920 | tf_op jit(solution)/shard_map/ppermute | solution.py:269
  50.0 6.1 %collective-permute-start.18 = (bf16[448,128]{1,0:T(8,128)(2,1)S(1)}, bf16[448,128]{1,0:T(8,128)(2,1)S(1)}, u32[]{:S(2)}, u32[]{:S(2)}) collective-permute-start(bf16[448,128]{1,0:T(8,128)(2,1)S(1)} %shard_map.102), channel_id=1, source_target_pairs={{0,2},{1,3},{2,0},{3,1},{4,6},{5,7},{6,4},{7,5},{8,10},{9,11},{10,... | collective-permute-start | bytes 344072 | tf_op jit(solution)/shard_map/ppermute | solution.py:266
  50.7 16.4 %collective-permute-start.17 = (bf16[640,128]{1,0:T(8,128)(2,1)S(1)}, bf16[640,128]{1,0:T(8,128)(2,1)S(1)}, u32[]{:S(2)}, u32[]{:S(2)}) collective-permute-start(bf16[640,128]{1,0:T(8,128)(2,1)S(1)} %shard_map.101), channel_id=1, source_target_pairs={{0,2},{1,3},{2,0},{3,1},{4,6},{5,7},{6,4},{7,5},{8,10},{9,11},{10,... | collective-permute-start | bytes 491528 | tf_op jit(solution)/shard_map/ppermute | solution.py:266
  56.4 10.6 %collective-permute-start.19 = (bf16[448,128]{1,0:T(8,128)(2,1)S(1)}, bf16[448,128]{1,0:T(8,128)(2,1)S(1)}, u32[]{:S(2)}, u32[]{:S(2)}) collective-permute-start(bf16[448,128]{1,0:T(8,128)(2,1)S(1)} %shard_map.103), channel_id=1, source_target_pairs={{0,4},{1,5},{2,6},{3,7},{4,0},{5,1},{6,2},{7,3},{8,12},{9,13},{10,... | collective-permute-start | bytes 344072 | tf_op jit(solution)/shard_map/ppermute | solution.py:266
  57.2 9.8 %collective-permute-start.20 = (bf16[192,128]{1,0:T(8,128)(2,1)S(1)}, bf16[192,128]{1,0:T(8,128)(2,1)S(1)}, u32[]{:S(2)}, u32[]{:S(2)}) collective-permute-start(bf16[192,128]{1,0:T(8,128)(2,1)S(1)} %shard_map.104), channel_id=1, source_target_pairs={{0,4},{1,5},{2,6},{3,7},{4,0},{5,1},{6,2},{7,3},{8,12},{9,13},{10,... | collective-permute-start | bytes 147464 | tf_op jit(solution)/shard_map/ppermute | solution.py:266
  59.9 7.2 %collective-permute-start.21 = (bf16[192,128]{1,0:T(8,128)(2,1)S(1)}, bf16[192,128]{1,0:T(8,128)(2,1)S(1)}, u32[]{:S(2)}, u32[]{:S(2)}) collective-permute-start(bf16[192,128]{1,0:T(8,128)(2,1)S(1)} %shard_map.105), channel_id=1, source_target_pairs={{0,6},{1,7},{2,4},{3,5},{4,2},{5,3},{6,0},{7,1},{8,14},{9,15},{10,... | collective-permute-start | bytes 147464 | tf_op jit(solution)/shard_map/ppermute | solution.py:266
